TPU v7x, 32 devices: a whole 2x2x4 slice. The times are simulated.
32 devices in a mesh: batch: 8 (over z, core), seq: 4 (over y, x).
Axes of the slice: x: 2, y: 2, z: 4, core: 2. Of those that a mesh axis runs over, the one named last changes fastest.
Arguments:
- tokens: bfloat16 [16, 1024, 1024], P('batch', 'seq'), may hold values from -6 to 6
- memory: bfloat16 [16, 256, 1024], P('batch', 'seq'), may hold values from -6 to 6
- output_grad: bfloat16 [16, 1024, 1024], P('batch', 'seq'), may hold values from -6 to 6
- segments: int32 [16, 1024], P('batch', 'seq'), may hold values from 0 to 3, never falling along the last dimension, each value on 1 to 512 neighbouring positions
- memory_segments: int32 [16, 256], P('batch', 'seq'), may hold values from 0 to 3, never falling along the last dimension, each value on 1 to 128 neighbouring positions
- buckets: int32 [1024], replicated, may hold values from 0 to 31
- w_query: float32 [2, 1024, 1024], P(None, ('batch', 'seq')), may hold values from -0.03125 to 0.03125
- keyvalue_weight: float32 [2, 2, 1024, 512], P(None, None, ('batch', 'seq')), may hold values from -0.1875 to 0.1875
- w_output: float32 [2, 1024, 1024], P(None, ('batch', 'seq')), may hold values from -0.75 to 0.75
- w_expand: float32 [2, 1024, 2816], P(None, ('batch', 'seq')), may hold values from -0.1875 to 0.1875
- w_reduce: float32 [2816, 1024], P(('batch', 'seq')), may hold values from -0.109375 to 0.109375
- gains: float32 [3, 1024], P(None, ('batch', 'seq')), may hold values from 0.5 to 1.5
- position_bias: float32 [512], P(('batch', 'seq')), may hold values from -3 to 3
- momentum_query: float32 [2, 1024, 1024], P(None, ('batch', 'seq')), may hold values from -1536 to 1536
- keyvalue_momentum: float32 [2, 2, 1024, 512], P(None, None, ('batch', 'seq')), may hold values from -384 to 384
- momentum_output: float32 [2, 1024, 1024], P(None, ('batch', 'seq')), may hold values from -160 to 160
- momentum_expand: float32 [2, 1024, 2816], P(None, ('batch', 'seq')), may hold values from -320 to 320
- momentum_reduce: float32 [2816, 1024], P(('batch', 'seq')), may hold values from -448 to 448
- momentum_gains: float32 [3, 1024], P(None, ('batch', 'seq')), may hold values from -448 to 448
- momentum_position: float32 [512], P(('batch', 'seq')), may hold values from -224 to 224
- average_query: float32 [2, 1024, 1024], P(None, ('batch', 'seq')), may hold values from -0.03125 to 0.03125
- keyvalue_average: float32 [2, 2, 1024, 512], P(None, None, ('batch', 'seq')), may hold values from -0.1875 to 0.1875
- average_output: float32 [2, 1024, 1024], P(None, ('batch', 'seq')), may hold values from -0.75 to 0.75
- average_expand: float32 [2, 1024, 2816], P(None, ('batch', 'seq')), may hold values from -0.1875 to 0.1875
- average_reduce: float32 [2816, 1024], P(('batch', 'seq')), may hold values from -0.109375 to 0.109375
- average_gains: float32 [3, 1024], P(None, ('batch', 'seq')), may hold values from 0.5 to 1.5
- average_position: float32 [512], P(('batch', 'seq')), may hold values from -3 to 3
Outputs:
- output: bfloat16 [16, 1024, 1024], P('batch', 'seq')
- input_grad: float32 [16, 1024, 1024], P('batch', 'seq')
- memory_grad: float32 [16, 256, 1024], P('batch', 'seq')
- grad_query: float32 [2, 1024, 1024], P(None, ('batch', 'seq'))
- grad_keyval: float32 [2, 2, 1024, 512], P(None, None, ('batch', 'seq'))
- grad_output: float32 [2, 1024, 1024], P(None, ('batch', 'seq'))
- grad_expand: float32 [2, 1024, 2816], P(None, ('batch', 'seq'))
- grad_reduce: float32 [2816, 1024], P(('batch', 'seq'))
- grad_gains: float32 [3, 1024], P(None, ('batch', 'seq'))
- grad_position: float32 [512], P(('batch', 'seq'))
- renewed_query: float32 [2, 1024, 1024], P(None, ('batch', 'seq'))
- renewed_keyval: float32 [2, 2, 1024, 512], P(None, None, ('batch', 'seq'))
- renewed_output: float32 [2, 1024, 1024], P(None, ('batch', 'seq'))
- renewed_expand: float32 [2, 1024, 2816], P(None, ('batch', 'seq'))
- renewed_reduce: float32 [2816, 1024], P(('batch', 'seq'))
- renewed_gains: float32 [3, 1024], P(None, ('batch', 'seq'))
- renewed_position: float32 [512], P(('batch', 'seq'))
- state_query: float32 [2, 2, 1024, 1024], P(None, None, ('batch', 'seq'))
- state_keyval: float32 [2, 2, 2, 1024, 512], P(None, None, None, ('batch', 'seq'))
- state_output: float32 [2, 2, 1024, 1024], P(None, None, ('batch', 'seq'))
- state_expand: float32 [2, 2, 1024, 2816], P(None, None, ('batch', 'seq'))
- state_reduce: float32 [2, 2816, 1024], P(None, ('batch', 'seq'))
- state_gains: float32 [2, 3, 1024], P(None, None, ('batch', 'seq'))
- state_position: float32 [2, 512], P(None, ('batch', 'seq'))
Inputs may be any that keep to these rules, and one draw needn't show every extreme that they name: `segments`: along each row the ids never fall, and each of the 4 ids occurs in every row. `memory_segments`: along each memory row the ids never fall, and each of the 4 ids occurs in every memory row.
All inputs are finite; a program needn't handle non-finite values.
Results may differ from a plain program's by a relative error of at most 0.02.
The roundings to bfloat16 on the way count: a program that leaves them out, or rounds other values in their place, can miss the bound.
Values may be sent and summed in bfloat16 or wider, within the bound.
No kernel may reach another device: no remote copies, remote signals or barrier semaphores. Data moves between devices by JAX's collectives and lax.ppermute only.
A program may use at most 256 MiB of HBM per device.

v0:
```python
import jax
import jax.numpy as jnp
from jax import lax
from jax.sharding import PartitionSpec as P

QUERY_HEADS = 16
HEAD_SIZE = 64
NB = 32


HIGHEST = lax.Precision.HIGHEST
EPSILON = 1e-06
NEGATIVE = -1e30
MOMENTUM = 0.9
AVERAGE = 0.99
STEP_RATES = (0.0015, 0.03, 0.3, 0.04, 0.015, 0.1, 1.0)


def normalize(values, gain):
    return values * lax.rsqrt(jnp.mean(values * values, axis=-1, keepdims=True) + EPSILON) * gain


def project(left, right):
    return jnp.einsum("rse,ed->rsd", left, right, preferred_element_type=jnp.float32)


def project_back(left, right):
    return jnp.einsum("rse,de->rsd", left, right, preferred_element_type=jnp.float32)


def weight_grad(left, right):
    return jnp.einsum("rsd,rse->de", left, right, preferred_element_type=jnp.float32)


def distance_select(bucket_list, offset, count):
    length = bucket_list.shape[0]
    shift = jnp.arange(2 * length, dtype=jnp.int32)
    lag = jnp.where(shift < length, shift, shift - 2 * length)
    distance = offset - lag
    valid = (distance >= 0) & (distance < length)
    picked = jnp.take(bucket_list, jnp.clip(distance, 0, length - 1), axis=0)
    hits = (picked[:, None] == jnp.arange(count, dtype=jnp.int32)[None, :]) & valid[:, None]
    return hits.astype(jnp.float32)


def expand_lags(per_lag, rows, cols):
    heads, width = per_lag.shape
    tiled = jnp.tile(per_lag, (1, rows))[:, : rows * (width - 1)]
    return tiled.reshape(heads, rows, width - 1)[:, :, :cols]


def diagonal_sums(values, width):
    heads, rows, cols = values.shape
    padded = jnp.pad(values, ((0, 0), (0, 0), (0, width - 1 - cols))).reshape(
        heads, rows * (width - 1)
    )
    padded = jnp.pad(padded, ((0, 0), (0, rows)))
    return jnp.sum(padded.reshape(heads, rows, width), axis=1)


def bias_table_grad(score_grad, selection):
    groups, per_group, rows, cols = score_grad.shape
    values = score_grad.astype(jnp.float32).reshape(groups * per_group, rows, cols)
    lag_sums = diagonal_sums(values, selection.shape[0])
    return jnp.dot(selection.T, lag_sums.T, precision=HIGHEST)


def block_scores(query_block, grouped_key_heads, segment_block, key_segments, offset, bias_spec):
    scores = jnp.einsum(
        "qgcd,kgd->gcqk", query_block, grouped_key_heads, preferred_element_type=jnp.float32
    )
    query_pos = offset + jnp.arange(query_block.shape[0], dtype=jnp.int32)
    key_pos = jnp.arange(grouped_key_heads.shape[0], dtype=jnp.int32)
    allowed = segment_block[:, None] == key_segments[None, :]
    selection = None
    if bias_spec is not None:
        table_local, bucket_list = bias_spec
        selection = distance_select(bucket_list, offset, table_local.shape[0])
        per_lag = jnp.dot(selection, table_local, precision=HIGHEST).T
        bias = expand_lags(per_lag, scores.shape[2], scores.shape[3]).reshape(scores.shape)
        allowed = allowed & (key_pos[None, :] <= query_pos[:, None])
        scores = scores + bias
    return (jnp.where(allowed, scores, NEGATIVE), selection)


def attend_forward(
    query_rows, key_matrix_rows, value_matrix_rows, query_segments, key_segments, bias_spec
):
    row_length = query_rows.shape[0]
    groups = key_matrix_rows.shape[1] // HEAD_SIZE
    block_rows = min(512, row_length)
    block_count = row_length // block_rows
    grouped_key_heads = key_matrix_rows.reshape(key_matrix_rows.shape[0], groups, HEAD_SIZE)
    grouped_value_heads = value_matrix_rows.reshape(value_matrix_rows.shape[0], groups, HEAD_SIZE)
    query_blocks = query_rows.reshape(block_count, block_rows, groups, -1, HEAD_SIZE)
    segment_blocks = query_segments.reshape(block_count, block_rows)
    offsets = jnp.arange(block_count, dtype=jnp.int32) * block_rows

    def one_block(inputs):
        query_block, segment_block, offset = inputs
        scores, _ = block_scores(
            query_block, grouped_key_heads, segment_block, key_segments, offset, bias_spec
        )
        largest = jnp.max(scores, axis=-1, keepdims=True)
        exponent = jnp.exp(scores - largest)
        totals = jnp.sum(exponent, axis=-1, keepdims=True)
        weights = (exponent / totals).astype(jnp.bfloat16)
        context = jnp.einsum(
            "gcqk,kgd->qgcd", weights, grouped_value_heads, preferred_element_type=jnp.float32
        )
        return (
            context.reshape(block_rows, -1).astype(jnp.bfloat16),
            (largest + jnp.log(totals))[..., 0],
        )

    context, logsum = lax.map(one_block, (query_blocks, segment_blocks, offsets))
    return (context.reshape(row_length, -1), logsum)


def attend_backward(
    query_rows,
    key_matrix_rows,
    value_matrix_rows,
    context_grad,
    logsum,
    query_segments,
    key_segments,
    bias_spec,
):
    row_length = query_rows.shape[0]
    groups = key_matrix_rows.shape[1] // HEAD_SIZE
    block_rows = min(512, row_length)
    block_count = row_length // block_rows
    grouped_key_heads = key_matrix_rows.reshape(key_matrix_rows.shape[0], groups, HEAD_SIZE)
    grouped_value_heads = value_matrix_rows.reshape(value_matrix_rows.shape[0], groups, HEAD_SIZE)
    query_blocks = query_rows.reshape(block_count, block_rows, groups, -1, HEAD_SIZE)
    grad_blocks = context_grad.reshape(block_count, block_rows, groups, -1, HEAD_SIZE)
    segment_blocks = query_segments.reshape(block_count, block_rows)
    offsets = jnp.arange(block_count, dtype=jnp.int32) * block_rows
    bias_shape = (1,) if bias_spec is None else bias_spec[0].shape

    def one_block(running, inputs):
        key_grad, value_grad, bias_grad = running
        query_block, grad_block, logsum_block, segment_block, offset = inputs
        scores, selection = block_scores(
            query_block, grouped_key_heads, segment_block, key_segments, offset, bias_spec
        )
        weights = jnp.exp(scores - logsum_block[..., None])
        probability_grad = jnp.einsum(
            "qgcd,kgd->gcqk", grad_block, grouped_value_heads, preferred_element_type=jnp.float32
        )
        centered = probability_grad - jnp.sum(weights * probability_grad, axis=-1, keepdims=True)
        score_grad = (weights * centered).astype(jnp.bfloat16)
        query_grad = jnp.einsum(
            "gcqk,kgd->qgcd", score_grad, grouped_key_heads, preferred_element_type=jnp.float32
        )
        key_grad = key_grad + jnp.einsum(
            "gcqk,qgcd->kgd", score_grad, query_block, preferred_element_type=jnp.float32
        )
        value_grad = value_grad + jnp.einsum(
            "gcqk,qgcd->kgd",
            weights.astype(jnp.bfloat16),
            grad_block,
            preferred_element_type=jnp.float32,
        )
        if bias_spec is not None:
            bias_grad = bias_grad + bias_table_grad(score_grad, selection)
        return (
            (key_grad, value_grad, bias_grad),
            query_grad.reshape(block_rows, -1).astype(jnp.bfloat16),
        )

    initial = (
        jnp.zeros(grouped_key_heads.shape, jnp.float32),
        jnp.zeros(grouped_value_heads.shape, jnp.float32),
        jnp.zeros(bias_shape, jnp.float32),
    )
    (key_grad, value_grad, bias_grad), query_grad = lax.scan(
        one_block, initial, (query_blocks, grad_blocks, logsum, segment_blocks, offsets)
    )
    return (
        query_grad.reshape(row_length, -1),
        key_grad.reshape(key_matrix_rows.shape[0], -1).astype(jnp.bfloat16),
        value_grad.reshape(value_matrix_rows.shape[0], -1).astype(jnp.bfloat16),
        bias_grad,
    )


def attend_rows(
    query_rows, key_matrix_rows, value_matrix_rows, query_segments, key_segments, bias_spec
):
    return lax.map(
        lambda inputs: attend_forward(*inputs, bias_spec),
        (query_rows, key_matrix_rows, value_matrix_rows, query_segments, key_segments),
    )


def attend_rows_back(
    query_rows,
    key_matrix_rows,
    value_matrix_rows,
    context_grad,
    logsum,
    query_segments,
    key_segments,
    bias_spec,
):
    query_grad, key_grad, value_grad, bias_grad = lax.map(
        lambda inputs: attend_backward(*inputs, bias_spec),
        (
            query_rows,
            key_matrix_rows,
            value_matrix_rows,
            context_grad,
            logsum,
            query_segments,
            key_segments,
        ),
    )
    return (query_grad, key_grad, value_grad, jnp.sum(bias_grad, axis=0))


def shards(
    tokens,
    memory,
    output_grad,
    segments,
    memory_segments,
    buckets,
    w_query,
    keyvalue_weight,
    w_output,
    w_expand,
    w_reduce,
    gains,
    position_bias,
    momentum_query,
    keyvalue_momentum,
    momentum_output,
    momentum_expand,
    momentum_reduce,
    momentum_gains,
    momentum_position,
    average_query,
    keyvalue_average,
    average_output,
    average_expand,
    average_reduce,
    average_gains,
    average_position,
):
    query_w, keyval_w, output_w, expand_w, reduce_w, gain_rows, table_flat = (
        lax.all_gather(w_query.astype(jnp.bfloat16), ("batch", "seq"), axis=1, tiled=True),
        lax.all_gather(keyvalue_weight.astype(jnp.bfloat16), ("batch", "seq"), axis=2, tiled=True),
        lax.all_gather(w_output.astype(jnp.bfloat16), ("batch", "seq"), axis=1, tiled=True),
        lax.all_gather(w_expand.astype(jnp.bfloat16), ("batch", "seq"), axis=1, tiled=True),
        lax.all_gather(w_reduce.astype(jnp.bfloat16), ("batch", "seq"), axis=0, tiled=True),
        lax.all_gather(gains.astype(jnp.bfloat16), ("batch", "seq"), axis=1, tiled=True),
        lax.all_gather(position_bias.astype(jnp.bfloat16), ("batch", "seq"), axis=0, tiled=True),
    )
    seq_count = lax.axis_size("seq")
    seq_index = lax.axis_index("seq")
    heads_local = QUERY_HEADS // seq_count
    table_full = table_flat.astype(jnp.float32).reshape(NB, QUERY_HEADS)
    table_local = lax.dynamic_slice_in_dim(table_full, seq_index * heads_local, heads_local, 1)
    bias_spec = (table_local, buckets)
    gain_values = gain_rows.astype(jnp.float32)
    all_segments, all_memory_segments = (
        lax.all_gather(segments, "seq", axis=1, tiled=True),
        lax.all_gather(memory_segments, "seq", axis=1, tiled=True),
    )
    token_values = tokens.astype(jnp.float32)
    normed = normalize(token_values, gain_values[0]).astype(jnp.bfloat16)
    query_rows = project(normed, query_w[0]).astype(jnp.bfloat16)
    key_matrix_rows = project(normed, keyval_w[0, 0]).astype(jnp.bfloat16)
    value_matrix_rows = project(normed, keyval_w[0, 1]).astype(jnp.bfloat16)
    memory_keys = project(memory, keyval_w[1, 0]).astype(jnp.bfloat16)
    memory_values = project(memory, keyval_w[1, 1]).astype(jnp.bfloat16)
    head_queries, head_keys, head_values, head_mkeys, head_mvalues = (
        lax.all_to_all(query_rows, "seq", split_axis=2, concat_axis=1, tiled=True),
        lax.all_to_all(key_matrix_rows, "seq", split_axis=2, concat_axis=1, tiled=True),
        lax.all_to_all(value_matrix_rows, "seq", split_axis=2, concat_axis=1, tiled=True),
        lax.all_to_all(memory_keys, "seq", split_axis=2, concat_axis=1, tiled=True),
        lax.all_to_all(memory_values, "seq", split_axis=2, concat_axis=1, tiled=True),
    )
    head_context, self_logsum = attend_rows(
        head_queries, head_keys, head_values, all_segments, all_segments, bias_spec
    )
    context = lax.all_to_all(head_context, "seq", split_axis=1, concat_axis=2, tiled=True)
    hidden_one = token_values + project(context, output_w[0])
    normed_one = normalize(hidden_one, gain_values[1]).astype(jnp.bfloat16)
    cross_queries = project(normed_one, query_w[1]).astype(jnp.bfloat16)
    head_cross = lax.all_to_all(cross_queries, "seq", split_axis=2, concat_axis=1, tiled=True)
    head_cross_context, cross_logsum = attend_rows(
        head_cross, head_mkeys, head_mvalues, all_segments, all_memory_segments, None
    )
    cross_context = lax.all_to_all(
        head_cross_context, "seq", split_axis=1, concat_axis=2, tiled=True
    )
    hidden_two = hidden_one + project(cross_context, output_w[1])
    normed_two = normalize(hidden_two, gain_values[2]).astype(jnp.bfloat16)
    gate_values = project(normed_two, expand_w[0])
    up_values = project(normed_two, expand_w[1])
    activated = (jax.nn.gelu(gate_values, approximate=True) * up_values).astype(jnp.bfloat16)
    result = hidden_two + project(activated, reduce_w)
    back_values = output_grad.astype(jnp.float32)
    grad_reduce_full = weight_grad(activated, output_grad)
    activated_grad = project_back(output_grad, reduce_w)
    _, gelu_pull = jax.vjp(
        lambda gate_part, upward: jax.nn.gelu(gate_part, approximate=True) * upward,
        gate_values,
        up_values,
    )
    gate_grad, up_grad = gelu_pull(activated_grad)
    gate_grad = gate_grad.astype(jnp.bfloat16)
    up_grad = up_grad.astype(jnp.bfloat16)
    grad_expand_full = jnp.stack(
        [weight_grad(normed_two, gate_grad), weight_grad(normed_two, up_grad)]
    )
    normed_two_grad = project_back(gate_grad, expand_w[0]) + project_back(up_grad, expand_w[1])
    _, norm_two_pull = jax.vjp(normalize, hidden_two, gain_values[2])
    hidden_two_part, gain_two_grad = norm_two_pull(normed_two_grad)
    hidden_two_grad = back_values + hidden_two_part
    cross_out_grad = hidden_two_grad.astype(jnp.bfloat16)
    grad_output_cross = weight_grad(cross_context, cross_out_grad)
    cross_context_grad = project_back(cross_out_grad, output_w[1]).astype(jnp.bfloat16)
    head_cross_grad = lax.all_to_all(
        cross_context_grad, "seq", split_axis=2, concat_axis=1, tiled=True
    )
    cross_query_heads, mkey_heads, mvalue_heads, _ = attend_rows_back(
        head_cross,
        head_mkeys,
        head_mvalues,
        head_cross_grad,
        cross_logsum,
        all_segments,
        all_memory_segments,
        None,
    )
    cross_query_grad, mkey_grad, mvalue_grad = (
        lax.all_to_all(cross_query_heads, "seq", split_axis=1, concat_axis=2, tiled=True),
        lax.all_to_all(mkey_heads, "seq", split_axis=1, concat_axis=2, tiled=True),
        lax.all_to_all(mvalue_heads, "seq", split_axis=1, concat_axis=2, tiled=True),
    )
    memory_grad = project_back(mkey_grad, keyval_w[1, 0]) + project_back(
        mvalue_grad, keyval_w[1, 1]
    )
    grad_mkey = weight_grad(memory, mkey_grad)
    grad_mvalue = weight_grad(memory, mvalue_grad)
    normed_one_grad = project_back(cross_query_grad, query_w[1])
    _, norm_one_pull = jax.vjp(normalize, hidden_one, gain_values[1])
    hidden_one_part, gain_one_grad = norm_one_pull(normed_one_grad)
    hidden_one_grad = hidden_two_grad + hidden_one_part
    self_out_grad = hidden_one_grad.astype(jnp.bfloat16)
    grad_output_self = weight_grad(context, self_out_grad)
    context_grad = project_back(self_out_grad, output_w[0]).astype(jnp.bfloat16)
    head_context_grad = lax.all_to_all(context_grad, "seq", split_axis=2, concat_axis=1, tiled=True)
    query_heads_grad, key_heads_grad, value_heads_grad, table_grad_local = attend_rows_back(
        head_queries,
        head_keys,
        head_values,
        head_context_grad,
        self_logsum,
        all_segments,
        all_segments,
        bias_spec,
    )
    query_grad, key_grad, value_grad = (
        lax.all_to_all(query_heads_grad, "seq", split_axis=1, concat_axis=2, tiled=True),
        lax.all_to_all(key_heads_grad, "seq", split_axis=1, concat_axis=2, tiled=True),
        lax.all_to_all(value_heads_grad, "seq", split_axis=1, concat_axis=2, tiled=True),
    )
    normed_grad = (
        project_back(query_grad, query_w[0])
        + project_back(key_grad, keyval_w[0, 0])
        + project_back(value_grad, keyval_w[0, 1])
    )
    _, norm_zero_pull = jax.vjp(normalize, token_values, gain_values[0])
    token_part, gain_zero_grad = norm_zero_pull(normed_grad)
    input_grad = hidden_one_grad + token_part
    grad_query_full = jnp.stack(
        [weight_grad(normed, query_grad), weight_grad(normed_one, cross_query_grad)]
    )
    grad_keyval_full = jnp.stack(
        [
            jnp.stack([weight_grad(normed, key_grad), weight_grad(normed, value_grad)]),
            jnp.stack([grad_mkey, grad_mvalue]),
        ]
    )
    grad_output_full = jnp.stack([grad_output_self, grad_output_cross])
    gains_grad = jnp.stack([gain_zero_grad, gain_one_grad, gain_two_grad])
    table_grad = lax.dynamic_update_slice(
        jnp.zeros((NB, QUERY_HEADS), jnp.float32), table_grad_local, (0, seq_index * heads_local)
    ).reshape(-1)
    (
        shard_query,
        shard_keyval,
        shard_output,
        shard_expand,
        shard_reduce,
        shard_gains,
        shard_table,
    ) = (
        lax.psum_scatter(grad_query_full, ("batch", "seq"), scatter_dimension=1, tiled=True),
        lax.psum_scatter(grad_keyval_full, ("batch", "seq"), scatter_dimension=2, tiled=True),
        lax.psum_scatter(grad_output_full, ("batch", "seq"), scatter_dimension=1, tiled=True),
        lax.psum_scatter(grad_expand_full, ("batch", "seq"), scatter_dimension=1, tiled=True),
        lax.psum_scatter(grad_reduce_full, ("batch", "seq"), scatter_dimension=0, tiled=True),
        lax.psum_scatter(gains_grad, ("batch", "seq"), scatter_dimension=1, tiled=True),
        lax.psum_scatter(table_grad, ("batch", "seq"), scatter_dimension=0, tiled=True),
    )
    token_total = tokens.shape[0] * tokens.shape[1] * lax.axis_size("batch") * seq_count
    token_scale = token_total ** (-0.5)
    gradients = (
        shard_query,
        shard_keyval,
        shard_output,
        shard_expand,
        shard_reduce,
        shard_gains,
        shard_table,
    )
    masters = (w_query, keyvalue_weight, w_output, w_expand, w_reduce, gains, position_bias)
    momenta = (
        momentum_query,
        keyvalue_momentum,
        momentum_output,
        momentum_expand,
        momentum_reduce,
        momentum_gains,
        momentum_position,
    )
    averages = (
        average_query,
        keyvalue_average,
        average_output,
        average_expand,
        average_reduce,
        average_gains,
        average_position,
    )
    renewals = []
    states = []
    for gradient, master, momentum, average, step_rate in zip(
        gradients, masters, momenta, averages, STEP_RATES
    ):
        renewed = MOMENTUM * momentum + gradient
        weight = master - step_rate * token_scale * (gradient + MOMENTUM * renewed)
        renewals.append(renewed)
        states.append(jnp.stack([weight, AVERAGE * average + (1.0 - AVERAGE) * weight]))
    return (
        result.astype(jnp.bfloat16),
        input_grad,
        memory_grad,
        shard_query,
        shard_keyval,
        shard_output,
        shard_expand,
        shard_reduce,
        shard_gains,
        shard_table,
        renewals[0],
        renewals[1],
        renewals[2],
        renewals[3],
        renewals[4],
        renewals[5],
        renewals[6],
        states[0],
        states[1],
        states[2],
        states[3],
        states[4],
        states[5],
        states[6],
    )


def solution(mesh):
    placed = (
        P("batch", "seq", None),
        P("batch", "seq", None),
        P("batch", "seq", None),
        P("batch", "seq"),
        P("batch", "seq"),
        P(),
        P(None, ("batch", "seq"), None),
        P(None, None, ("batch", "seq"), None),
        P(None, ("batch", "seq"), None),
        P(None, ("batch", "seq"), None),
        P(("batch", "seq"), None),
        P(None, ("batch", "seq")),
        P(("batch", "seq")),
        P(None, ("batch", "seq"), None),
        P(None, None, ("batch", "seq"), None),
        P(None, ("batch", "seq"), None),
        P(None, ("batch", "seq"), None),
        P(("batch", "seq"), None),
        P(None, ("batch", "seq")),
        P(("batch", "seq")),
        P(None, ("batch", "seq"), None),
        P(None, None, ("batch", "seq"), None),
        P(None, ("batch", "seq"), None),
        P(None, ("batch", "seq"), None),
        P(("batch", "seq"), None),
        P(None, ("batch", "seq")),
        P(("batch", "seq")),
    )
    return jax.shard_map(
        shards,
        mesh=mesh,
        in_specs=placed,
        out_specs=(
            P("batch", "seq", None),
            P("batch", "seq", None),
            P("batch", "seq", None),
            P(None, ("batch", "seq"), None),
            P(None, None, ("batch", "seq"), None),
            P(None, ("batch", "seq"), None),
            P(None, ("batch", "seq"), None),
            P(("batch", "seq"), None),
            P(None, ("batch", "seq")),
            P(("batch", "seq")),
            P(None, ("batch", "seq"), None),
            P(None, None, ("batch", "seq"), None),
            P(None, ("batch", "seq"), None),
            P(None, ("batch", "seq"), None),
            P(("batch", "seq"), None),
            P(None, ("batch", "seq")),
            P(("batch", "seq")),
            P(None, None, ("batch", "seq"), None),
            P(None, None, None, ("batch", "seq"), None),
            P(None, None, ("batch", "seq"), None),
            P(None, None, ("batch", "seq"), None),
            P(None, ("batch", "seq"), None),
            P(None, None, ("batch", "seq")),
            P(None, ("batch", "seq")),
        ),
        check_vma=False,
    )
```

profile of v0, /device:TPU:0, one launch (start us, length us, event | category | flops | bytes accessed | tf_op | source)
XLA Modules:
  0.0 3376.0 jit_solution(18300084040219356490)
XLA Ops:
  13.0 69.9 %all-gather = bf16[32,32,3]{1,2,0:T(4,128)(2,1)S(1)} all-gather(bf16[1,32,3]{1,2,0:T(4,128)(2,1)S(1)} %convert_bitcast_fusion), channel_id=1, replica_groups=mesh['batch'=8,'seq'=4] {'batch','seq'}, dimensions={0}, use_global_device_ids=true | all-gather | bytes 6336 | tf_op jit(solution)/shard_map/all_gather | solution.py:258
  102.3 39.1 %all-gather.8.cloned.1.call-done = bf16[2,1024,1024]{2,1,0:T(8,128)(2,1)} async-done(((bf16[2,32,1024]{2,1,0:T(8,128)(2,1)}), bf16[2,1024,1024]{2,1,0:T(8,128)(2,1)}) %all-gather.8.cloned.1.call-update) | async-done | bytes 4194320 | tf_op jit(solution)/shard_map/all_gather | solution.py:253
  153.6 47.3 %all-reduce.2 = bf16[512]{0:T(512)(128)(2,1)S(1)} all-reduce(bf16[512]{0:T(512)(128)(2,1)S(1)} %dynamic-update-slice), channel_id=1, replica_groups=mesh['batch'=8,'seq'=4] {'batch','seq'}, use_global_device_ids=true, to_apply=%add.2 | all-reduce | flops 512 | bytes 2048
  217.8 498.2 %while.145 = (s32[]{:T(128)}, bf16[2,1024,256]{2,1,0:T(8,128)(2,1)}, f32[2,2,2,2,512]{4,3,2,1,0:T(2,128)}, bf16[2,1024,256]{1,2,0:T(8,128)(2,1)}, s32[2,1024]{1,...) while((s32[]{:T(128)}, bf16[2,1024,256]{2,1,0:T(8,128)(2,1)}, ...), condition=%wide.region_6.8_spmd, body=%wide.region_1.7_spmd.sunk | while | flops 558684672 | bytes 226966576 | solution.py:192
  241.3 230.3 %while.152 = (s32[]{:T(128)}, bf16[2,512,256]{2,1,0:T(8,128)(2,1)S(1)}, f32[2,2,2,512]{3,2,1,0:T(2,128)S(1)}, s32[2,512]{1,0:T(2,128)S(1)}, s32[1024]{0:T(1024)S...) while((s32[]{:T(128)}, ...), condition=%wide.region_5.6_spmd, body=%wide.region_2.5_spmd.sunk | while | flops 558684672 | bytes 213019312 | solution.py:116
  274.8 47.9 %reshape.660 = f32[4192256]{0:T(1024)} reshape(f32[4,1048064]{1,0:T(4,128)} %slice.179) | data formatting | bytes 33538048 | tf_op jit(solution)/shard_map/while/body/eval_jaxpr/while
  390.4 46.9 %reshape.660 = f32[4192256]{0:T(1024)} reshape(f32[4,1048064]{1,0:T(4,128)} %slice.179) | data formatting | bytes 33538048 | tf_op jit(solution)/shard_map/while/body/eval_jaxpr/while
  477.2 229.3 %while.152 = (s32[]{:T(128)}, bf16[2,512,256]{2,1,0:T(8,128)(2,1)S(1)}, f32[2,2,2,512]{3,2,1,0:T(2,128)S(1)}, s32[2,512]{1,0:T(2,128)S(1)}, s32[1024]{0:T(1024)S...) while((s32[]{:T(128)}, ...), condition=%wide.region_5.6_spmd, body=%wide.region_2.5_spmd.sunk | while | flops 558684672 | bytes 213019312 | solution.py:116
  510.7 46.9 %reshape.660 = f32[4192256]{0:T(1024)} reshape(f32[4,1048064]{1,0:T(4,128)} %slice.179) | data formatting | bytes 33538048 | tf_op jit(solution)/shard_map/while/body/eval_jaxpr/while
  625.3 46.9 %reshape.660 = f32[4192256]{0:T(1024)} reshape(f32[4,1048064]{1,0:T(4,128)} %slice.179) | data formatting | bytes 33538048 | tf_op jit(solution)/shard_map/while/body/eval_jaxpr/while
  916.6 70.1 %while.149 = (s32[]{:T(128)}, bf16[2,1024,256]{2,1,0:T(8,128)(2,1)}, bf16[2,256,128]{1,2,0:T(8,128)(2,1)}, bf16[2,256,128]{1,2,0:T(8,128)(2,1)}, bf16[2,1024,256...) while((s32[]{:T(128)}, bf16[2,1024,256]{2,1,0:T(8,128)(2,1)}, ...), condition=%wide.region_20.22_spmd, body=%wide.region_16.21_spmd.sunk | while | flops 340195328 | bytes 27428308 | solution.py:208
  1032.1 835.2 %while.151 = (s32[]{:T(128)}, bf16[2,1024,256]{2,1,0:T(8,128)(2,1)}, bf16[2,1024,128]{1,2,0:T(8,128)(2,1)}, bf16[2,1024,128]{1,2,0:T(8,128)(2,1)}, f32[2,32,4]{1...) while((s32[]{:T(128)}, bf16[2,1024,256]{2,1,0:T(8,128)(2,1)}, ...), condition=%wide.region_27.29_spmd, body=%wide.region_22.28_spmd.sunk | while | flops 1378532096 | bytes 420206848 | solution.py:208
  1039.9 402.3 %while.155 = (s32[]{:T(128)}, f32[1024,2,64]{0,2,1:T(8,128)S(1)}, f32[1024,2,64]{0,2,1:T(8,128)S(1)}, f32[32,4]{0,1:T(4,128)S(1)}, bf16[2,512,256]{2,1,0:T(8,128...) while((s32[]{:T(128)}, f32[1024,2,64]{0,2,1:T(8,128)S(1)}, ...), condition=%wide.region_26.27_spmd.clone, body=%wide.region_23.26_spmd.clone.sunk | while | flops 1378269952 | bytes 409130816 | solution.py:178
  1078.4 47.3 %reshape.654 = f32[4192256]{0:T(1024)} reshape(f32[4,1048064]{1,0:T(4,128)} %slice.176) | data formatting | bytes 33538048 | tf_op jit(solution)/shard_map/while/body/eval_jaxpr/while
  1279.0 47.1 %reshape.654 = f32[4192256]{0:T(1024)} reshape(f32[4,1048064]{1,0:T(4,128)} %slice.176) | data formatting | bytes 33538048 | tf_op jit(solution)/shard_map/while/body/eval_jaxpr/while
  1453.5 402.4 %while.155 = (s32[]{:T(128)}, f32[1024,2,64]{0,2,1:T(8,128)S(1)}, f32[1024,2,64]{0,2,1:T(8,128)S(1)}, f32[32,4]{0,1:T(4,128)S(1)}, bf16[2,512,256]{2,1,0:T(8,128...) while((s32[]{:T(128)}, f32[1024,2,64]{0,2,1:T(8,128)S(1)}, ...), condition=%wide.region_26.27_spmd.clone, body=%wide.region_23.26_spmd.clone.sunk | while | flops 1378269952 | bytes 409130816 | solution.py:178
  1492.3 47.0 %reshape.654 = f32[4192256]{0:T(1024)} reshape(f32[4,1048064]{1,0:T(4,128)} %slice.176) | data formatting | bytes 33538048 | tf_op jit(solution)/shard_map/while/body/eval_jaxpr/while
  1692.7 47.3 %reshape.654 = f32[4192256]{0:T(1024)} reshape(f32[4,1048064]{1,0:T(4,128)} %slice.176) | data formatting | bytes 33538048 | tf_op jit(solution)/shard_map/while/body/eval_jaxpr/while
  2013.3 38.9 %all-reduce.3 = f32[512]{0:T(512)S(1)} all-reduce(f32[512]{0:T(512)S(1)} %reshape.501), channel_id=8, replica_groups=mesh['batch'=8,'seq'=4] {'batch','seq'}, use_global_device_ids=true, to_apply=%region_39.41.clone | all-reduce | flops 512 | bytes 4096
  2063.2 180.9 %reduce-scatter.13.cloned.1.call-done = f32[2,32,1024]{2,1,0:T(8,128)} async-done(((f32[2,1024,1024]{2,1,0:T(8,128)}), f32[2,32,1024]{2,1,0:T(8,128)}) %reduce-scatter.13.cloned.1.call-update) | async-done | bytes 262160 | tf_op jit(solution)/shard_map/reduce_scatter | solution.py:406
  2247.5 184.1 %reduce-scatter.11.cloned.1.call-done = f32[2,2,32,512]{3,2,1,0:T(8,128)} async-done(((f32[2,2,1024,512]{3,2,1,0:T(8,128)}), f32[2,2,32,512]{3,2,1,0:T(8,128)}) %reduce-scatter.11.cloned.1.call-update) | async-done | bytes 262160 | tf_op jit(solution)/shard_map/reduce_scatter | solution.py:405
  2434.7 184.4 %reduce-scatter.9.cloned.1.call-done = f32[2,32,1024]{2,1,0:T(8,128)} async-done(((f32[2,1024,1024]{2,1,0:T(8,128)}), f32[2,32,1024]{2,1,0:T(8,128)}) %reduce-scatter.9.cloned.1.call-update) | async-done | bytes 262160 | tf_op jit(solution)/shard_map/reduce_scatter | solution.py:404
  2622.3 249.4 %reduce-scatter.17.cloned.1.call-done = f32[88,1024]{1,0:T(8,128)} async-done(((f32[2816,1024]{1,0:T(8,128)}), f32[88,1024]{1,0:T(8,128)}) %reduce-scatter.17.cloned.1.call-update) | async-done | bytes 360464 | tf_op jit(solution)/shard_map/reduce_scatter | solution.py:408
  2875.1 489.7 %reduce-scatter.15.cloned.1.call-done = f32[2,32,2816]{2,1,0:T(8,128)} async-done(((f32[2,1024,2816]{2,1,0:T(8,128)}), f32[2,32,2816]{2,1,0:T(8,128)}) %reduce-scatter.15.cloned.1.call-update) | async-done | bytes 720912 | tf_op jit(solution)/shard_map/reduce_scatter | solution.py:407
  (857 shorter events, 1553.7 us)
Async XLA Ops:
  7.2 78.0 %all-gather.10.cloned.1.call-start = ((), (), s32[]{:S(2)}) async-start(), calls=%async_computation.23 | async-start | bytes 4325376 | tf_op jit(solution)/shard_map/all_gather | solution.py:254
  8.9 132.4 %all-gather.8.cloned.1.call-start = ((), (), s32[]{:S(2)}) async-start(), calls=%async_computation.22 | async-start | bytes 4325376 | tf_op jit(solution)/shard_map/all_gather | solution.py:253
  10.6 729.7 %all-gather.12.cloned.1.call-start = ((), (), s32[]{:S(2)}) async-start(), calls=%async_computation.24 | async-start | bytes 4325376 | tf_op jit(solution)/shard_map/all_gather | solution.py:255
  88.7 10.0 all-to-all-start.1
  98.8 50.2 %all-to-all-start.2 = ((bf16[2,256,512]{1,0,2:T(2,128)(2,1)}), bf16[2,256,512]{1,0,2:T(2,128)(2,1)S(1)}, u32[]{:S(2)}, u32[]{:S(2)}) async-start(bf16[2,256,512]{1,0,2:T(2,128)(2,1)} %copy.296), calls=%async_computation.2 | async-start | bytes 1048576 | tf_op jit(solution)/shard_map/all_to_all | solution.py:282
  149.0 64.8 %all-to-all-start = ((bf16[2,256,1024]{1,0,2:T(2,128)(2,1)}), bf16[2,256,1024]{1,0,2:T(2,128)(2,1)S(1)}, u32[]{:S(2)}, u32[]{:S(2)}) async-start(bf16[2,256,1024]{1,0,2:T(2,128)(2,1)} %copy.292), calls=%async_computation | async-start | bytes 2097152 | tf_op jit(solution)/shard_map/all_to_all | solution.py:280
  152.5 700.2 %all-gather.14.cloned.1.call-start = ((), (), s32[]{:S(2)}) async-start(), calls=%async_computation.25 | async-start | bytes 11894784 | tf_op jit(solution)/shard_map/all_gather | solution.py:256
  719.3 14.7 all-to-all-start.3
  734.0 9.6 all-to-all-start.5
  743.7 9.3 all-to-all-start.6
  753.0 32.2 all-to-all-start.4
  757.0 108.5 %all-gather.16.cloned.1.call-start = ((), (), s32[]{:S(2)}) async-start(), calls=%async_computation.26 | async-start | bytes 5947392 | tf_op jit(solution)/shard_map/all_gather | solution.py:257
  899.6 13.5 all-to-all-start.8
  1015.7 12.9 all-to-all-start.10
  1869.4 12.7 all-to-all-start.13
  1882.1 15.0 all-to-all-start.12
  1897.1 18.6 all-to-all-start.11
  1901.4 160.4 %reduce-scatter.19.cloned.1.call-start = ((), (), s32[]{:S(2)}) async-start(), calls=%async_computation.32 | async-start | bytes 540672
  1928.1 316.0 %reduce-scatter.13.cloned.1.call-start = ((), (), s32[]{:S(2)}) async-start(), calls=%async_computation.29 | async-start | bytes 8650752 | tf_op jit(solution)/shard_map/reduce_scatter | solution.py:406
  1938.3 9.1 all-to-all-start.14
  1950.7 480.9 %reduce-scatter.11.cloned.1.call-start = ((), (), s32[]{:S(2)}) async-start(), calls=%async_computation.28 | async-start | bytes 8650752 | tf_op jit(solution)/shard_map/reduce_scatter | solution.py:405
  1964.5 654.6 %reduce-scatter.9.cloned.1.call-start = ((), (), s32[]{:S(2)}) async-start(), calls=%async_computation.27 | async-start | bytes 8650752 | tf_op jit(solution)/shard_map/reduce_scatter | solution.py:404
  1974.4 897.3 %reduce-scatter.17.cloned.1.call-start = ((), (), s32[]{:S(2)}) async-start(), calls=%async_computation.31 | async-start | bytes 11894784 | tf_op jit(solution)/shard_map/reduce_scatter | solution.py:408
  1983.4 1381.3 %reduce-scatter.15.cloned.1.call-start = ((), (), s32[]{:S(2)}) async-start(), calls=%async_computation.30 | async-start | bytes 23789568 | tf_op jit(solution)/shard_map/reduce_scatter | solution.py:407
  (118 other events, 8288.0 us)
Sparse Core Ops, SparseCore 0:
  11.5 64.9 all-gather.9
  80.1 61.2 all-gather.7
  144.9 66.4 all-gather.11
  214.7 89.5 all-gather.13
  761.0 66.6 all-gather.15
  1928.2 133.5 reduce-scatter.18
  2064.7 179.3 reduce-scatter.12
  2247.1 184.4 reduce-scatter.10
  2434.6 184.4 reduce-scatter.8
  2621.9 249.6 reduce-scatter.16
  2874.7 490.0 reduce-scatter.14
where the time goes:
time: 3390 us; the launch traced here: 3380 us
  waiting for transfers between devices  1380 us (41%)
  local copies, waits for them, and re-layouts  1180 us (35%)
  matrix products  278 us (8%)
  other arithmetic  219 us (6%)
  blocking collectives  206 us (6%)
  starting transfers between devices  54.3 us (2%)
  loops' own time  41.1 us (1%)
    while x92, local copies, waits for them, and re-layouts  571 us
    reduce_scatter x1, waiting for transfers between devices, shards(): lax.psum_scatter(grad_expand_full, ('batch', 'seq'), scatter_dimension=1,...  490 us
    reduce_scatter x1, waiting for transfers between devices, shards(): lax.psum_scatter(grad_reduce_full, ('batch', 'seq'), scatter_dimension=0,...  249 us
    reshape x8, local copies, waits for them, and re-layouts, expand_lags(): return tiled.reshape(heads, rows, width - 1)[:, :, :cols]  198 us
    reduce_scatter x1, waiting for transfers between devices, shards(): lax.psum_scatter(grad_query_full, ('batch', 'seq'), scatter_dimension=1,...  184 us
    reduce_scatter x1, waiting for transfers between devices, shards(): lax.psum_scatter(grad_keyval_full, ('batch', 'seq'), scatter_dimension=2,...  184 us
    reduce_scatter x1, waiting for transfers between devices, shards(): lax.psum_scatter(grad_output_full, ('batch', 'seq'), scatter_dimension=1,...  181 us
    unnamed x2, blocking collectives  86.2 us
  transfers between devices with their start and end apart: 25, of which 16 were waited for; matrix products, arithmetic and copies ran while one was open for 20% of the time, Pallas kernels for 0%

commit v1 on v0

v1 whole, which is shorter than its diff:
```python
import functools

import jax
import jax.numpy as jnp
from jax import lax
from jax.experimental import pallas as pl
from jax.experimental.pallas import tpu as pltpu
from jax.sharding import PartitionSpec as P

HEAD_SIZE = 64
QUERY_HEADS = 16
NB = 32
EPSILON = 1e-06
NEGATIVE = -1e30
MOMENTUM = 0.9
AVERAGE = 0.99
STEP_RATES = (0.0015, 0.03, 0.3, 0.04, 0.015, 0.1, 1.0)
BF16 = jnp.bfloat16
F32 = jnp.float32
BQ = 128


def nt(a, b):
    return lax.dot_general(a, b, (((1,), (1,)), ((), ())), preferred_element_type=F32)


def nn(a, b):
    return lax.dot_general(a, b, (((1,), (0,)), ((), ())), preferred_element_type=F32)


def tn(a, b):
    return lax.dot_general(a, b, (((0,), (0,)), ((), ())), preferred_element_type=F32)


def stacked(block, group, per):
    first = group * per
    return jnp.concatenate(
        [block[:, (first + c) * HEAD_SIZE : (first + c + 1) * HEAD_SIZE] for c in range(per)], axis=0
    )


def lanes(block, index):
    return block[:, index * HEAD_SIZE : (index + 1) * HEAD_SIZE]


def skew(held, back):
    count, width = held.shape
    rows = lax.broadcasted_iota(jnp.int32, (count, width), 0)
    amount = 1
    while amount < count:
        turned = pltpu.roll(held, width - amount if back else amount, 1)
        held = jnp.where((rows & amount) != 0, turned, held)
        amount *= 2
    return held


def make_strips(base_ref, strip_ref):
    heads, rows, width = strip_ref.shape
    for h in range(heads):
        strip_ref[h] = skew(jnp.broadcast_to(base_ref[h : h + 1, :], (rows, width)), False)


def windows(length):
    reach = length // 2
    for step in range(length // BQ):
        here = slice(step * BQ, (step + 1) * BQ)
        start = max(step * BQ - reach, 0)
        lead = reach - (step * BQ - start)
        yield here, slice(start, (step + 1) * BQ), slice(lead, lead + (step + 1) * BQ - start)


def self_fwd_kernel(q_ref, k_ref, v_ref, seg_row_ref, seg_col_ref, base_ref, o_ref, lse_ref, strip_ref):
    heads = strip_ref.shape[0]
    groups = k_ref.shape[2] // HEAD_SIZE
    per = heads // groups

    @pl.when(pl.program_id(0) == 0)
    def _():
        make_strips(base_ref, strip_ref)

    for here, seen, strip in windows(k_ref.shape[1]):
        same = seg_col_ref[0, here, :] == seg_row_ref[0, :, seen]
        block, keys, values = q_ref[0, here, :], k_ref[0, seen, :], v_ref[0, seen, :]
        outs, sums = [], []
        for g in range(groups):
            scores = nt(stacked(block, g, per), lanes(keys, g))
            probs = []
            for c in range(per):
                bias = strip_ref[g * per + c, :, strip]
                s = jnp.where(same, scores[c * BQ : (c + 1) * BQ] + bias, NEGATIVE)
                top = jnp.max(s, axis=-1, keepdims=True)
                e = jnp.exp(s - top)
                total = jnp.sum(e, axis=-1, keepdims=True)
                probs.append((e * (1.0 / total)).astype(BF16))
                sums.append(top + jnp.log(total))
            ctx = nn(jnp.concatenate(probs, axis=0), lanes(values, g)).astype(BF16)
            outs += [ctx[c * BQ : (c + 1) * BQ] for c in range(per)]
        o_ref[0, here, :] = jnp.concatenate(outs, axis=1)
        lse_ref[0, here, :] = jnp.concatenate(sums, axis=1)


def self_bwd_kernel(
    q_ref, k_ref, v_ref, c_ref, lse_ref, seg_row_ref, seg_col_ref, base_ref,
    dq_ref, dk_ref, dv_ref, lag_ref, strip_ref, grad_ref, dk_acc, dv_acc,
):
    heads = strip_ref.shape[0]
    groups = k_ref.shape[2] // HEAD_SIZE
    per = heads // groups

    @pl.when(pl.program_id(0) == 0)
    def _():
        make_strips(base_ref, strip_ref)
        grad_ref[...] = jnp.zeros_like(grad_ref)

    dk_acc[...] = jnp.zeros_like(dk_acc)
    dv_acc[...] = jnp.zeros_like(dv_acc)
    for here, seen, strip in windows(k_ref.shape[1]):
        same = seg_col_ref[0, here, :] == seg_row_ref[0, :, seen]
        block, keys, values = q_ref[0, here, :], k_ref[0, seen, :], v_ref[0, seen, :]
        cots, lse = c_ref[0, here, :], lse_ref[0, here, :]
        outs = []
        for g in range(groups):
            q2, c2 = stacked(block, g, per), stacked(cots, g, per)
            scores = nt(q2, lanes(keys, g))
            dprobs = nt(c2, lanes(values, g))
            probs, dscores = [], []
            for c in range(per):
                h = g * per + c
                bias = strip_ref[h, :, strip]
                s = jnp.where(same, scores[c * BQ : (c + 1) * BQ] + bias, NEGATIVE)
                p = jnp.exp(s - lse[:, h : h + 1])
                dp = dprobs[c * BQ : (c + 1) * BQ]
                ds = (p * (dp - jnp.sum(p * dp, axis=-1, keepdims=True))).astype(BF16)
                grad_ref[h, :, strip] += ds.astype(F32)
                probs.append(p.astype(BF16))
                dscores.append(ds)
            p2, ds2 = jnp.concatenate(probs, axis=0), jnp.concatenate(dscores, axis=0)
            dq2 = nn(ds2, lanes(keys, g)).astype(BF16)
            outs += [dq2[c * BQ : (c + 1) * BQ] for c in range(per)]
            mine = slice(g * HEAD_SIZE, (g + 1) * HEAD_SIZE)
            dk_acc[mine, seen] += tn(q2, ds2)
            dv_acc[mine, seen] += tn(c2, p2)
        dq_ref[0, here, :] = jnp.concatenate(outs, axis=1)
    dk_ref[0] = dk_acc[...].T.astype(BF16)
    dv_ref[0] = dv_acc[...].T.astype(BF16)

    @pl.when(pl.program_id(0) == pl.num_programs(0) - 1)
    def _():
        for h in range(heads):
            lag_ref[h : h + 1, :] = jnp.sum(skew(grad_ref[h], True), axis=0, keepdims=True)


def self_specs(length, q_width, k_width, heads, strip_width):
    queries = pl.BlockSpec((1, length, q_width), lambda r: (r, 0, 0))
    keys = pl.BlockSpec((1, length, k_width), lambda r: (r, 0, 0))
    sums = pl.BlockSpec((1, length, heads), lambda r: (r, 0, 0))
    seg_row = pl.BlockSpec((1, 1, length), lambda r: (r, 0, 0))
    seg_col = pl.BlockSpec((1, length, 1), lambda r: (r, 0, 0))
    base = pl.BlockSpec((heads, strip_width), lambda r: (0, 0))
    return queries, keys, sums, seg_row, seg_col, base


def self_attention(q, k, v, segments, base):
    rows, length, q_width = q.shape
    heads, strip_width = base.shape
    queries, keys, sums, seg_row, seg_col, base_spec = self_specs(
        length, q_width, k.shape[2], heads, strip_width
    )
    work = rows * heads * length * length * 3 // 8
    return pl.pallas_call(
        self_fwd_kernel,
        grid=(rows,),
        in_specs=[queries, keys, keys, seg_row, seg_col, base_spec],
        out_specs=[queries, sums],
        out_shape=[
            jax.ShapeDtypeStruct(q.shape, BF16),
            jax.ShapeDtypeStruct((rows, length, heads), F32),
        ],
        scratch_shapes=[pltpu.VMEM((heads, BQ, strip_width), F32)],
        compiler_params=pltpu.CompilerParams(vmem_limit_bytes=48 << 20),
        cost_estimate=pl.CostEstimate(
            flops=work * 4 * HEAD_SIZE, transcendentals=work, bytes_accessed=q.size * 8
        ),
        name="self_attention",
    )(q, k, v, segments[:, None, :], segments[:, :, None], base)


def self_attention_back(q, k, v, cots, lse, segments, base):
    rows, length, q_width = q.shape
    heads, strip_width = base.shape
    k_width = k.shape[2]
    queries, keys, sums, seg_row, seg_col, base_spec = self_specs(
        length, q_width, k_width, heads, strip_width
    )
    work = rows * heads * length * length * 3 // 8
    return pl.pallas_call(
        self_bwd_kernel,
        grid=(rows,),
        in_specs=[queries, keys, keys, queries, sums, seg_row, seg_col, base_spec],
        out_specs=[queries, keys, keys, base_spec],
        out_shape=[
            jax.ShapeDtypeStruct(q.shape, BF16),
            jax.ShapeDtypeStruct(k.shape, BF16),
            jax.ShapeDtypeStruct(k.shape, BF16),
            jax.ShapeDtypeStruct((heads, strip_width), F32),
        ],
        scratch_shapes=[
            pltpu.VMEM((heads, BQ, strip_width), F32),
            pltpu.VMEM((heads, BQ, strip_width), F32),
            pltpu.VMEM((k_width, length), F32),
            pltpu.VMEM((k_width, length), F32),
        ],
        compiler_params=pltpu.CompilerParams(vmem_limit_bytes=48 << 20),
        cost_estimate=pl.CostEstimate(
            flops=work * 10 * HEAD_SIZE, transcendentals=work, bytes_accessed=q.size * 12
        ),
        name="self_attention_back",
    )(q, k, v, cots, lse, segments[:, None, :], segments[:, :, None], base)


def cross_fwd_kernel(q_ref, k_ref, v_ref, seg_row_ref, seg_col_ref, o_ref, *lse_refs):
    block, keys, values = q_ref[0], k_ref[0], v_ref[0]
    count = block.shape[0]
    groups = keys.shape[1] // HEAD_SIZE
    per = block.shape[1] // keys.shape[1]
    same = seg_col_ref[0] == seg_row_ref[0]
    outs = []
    for g in range(groups):
        scores = nt(stacked(block, g, per), lanes(keys, g))
        probs = []
        for c in range(per):
            s = jnp.where(same, scores[c * count : (c + 1) * count], NEGATIVE)
            top = jnp.max(s, axis=-1, keepdims=True)
            e = jnp.exp(s - top)
            total = jnp.sum(e, axis=-1, keepdims=True)
            probs.append((e * (1.0 / total)).astype(BF16))
        ctx = nn(jnp.concatenate(probs, axis=0), lanes(values, g)).astype(BF16)
        outs += [ctx[c * count : (c + 1) * count] for c in range(per)]
    o_ref[0] = jnp.concatenate(outs, axis=1)


def cross_bwd_kernel(q_ref, k_ref, v_ref, c_ref, seg_row_ref, seg_col_ref, dq_ref, dk_ref, dv_ref):
    block, keys, values, cots = q_ref[0], k_ref[0], v_ref[0], c_ref[0]
    count = block.shape[0]
    groups = keys.shape[1] // HEAD_SIZE
    per = block.shape[1] // keys.shape[1]
    same = seg_col_ref[0] == seg_row_ref[0]
    outs, dkeys, dvalues = [], [], []
    for g in range(groups):
        q2, c2 = stacked(block, g, per), stacked(cots, g, per)
        scores = nt(q2, lanes(keys, g))
        dprobs = nt(c2, lanes(values, g))
        probs, dscores = [], []
        for c in range(per):
            s = jnp.where(same, scores[c * count : (c + 1) * count], NEGATIVE)
            top = jnp.max(s, axis=-1, keepdims=True)
            e = jnp.exp(s - top)
            p = e * (1.0 / jnp.sum(e, axis=-1, keepdims=True))
            dp = dprobs[c * count : (c + 1) * count]
            dscores.append((p * (dp - jnp.sum(p * dp, axis=-1, keepdims=True))).astype(BF16))
            probs.append(p.astype(BF16))
        p2, ds2 = jnp.concatenate(probs, axis=0), jnp.concatenate(dscores, axis=0)
        dq2 = nn(ds2, lanes(keys, g)).astype(BF16)
        outs += [dq2[c * count : (c + 1) * count] for c in range(per)]
        dkeys.append(tn(q2, ds2))
        dvalues.append(tn(c2, p2))
    dq_ref[0] = jnp.concatenate(outs, axis=1)
    dk_ref[0] = jnp.concatenate(dkeys, axis=0).T.astype(dk_ref.dtype)
    dv_ref[0] = jnp.concatenate(dvalues, axis=0).T.astype(dv_ref.dtype)


def cross_specs(q, k):
    rows, count, q_width = q.shape
    memory, k_width = k.shape[1:]
    step = 2 * HEAD_SIZE
    q_step = step * (q_width // k_width)
    queries = pl.BlockSpec((1, count, q_step), lambda r, g: (r, 0, g))
    keys = pl.BlockSpec((1, memory, step), lambda r, g: (r, 0, g))
    seg_row = pl.BlockSpec((1, 1, memory), lambda r, g: (r, 0, 0))
    seg_col = pl.BlockSpec((1, count, 1), lambda r, g: (r, 0, 0))
    return (rows, k_width // step), queries, keys, seg_row, seg_col


def cross_attention(q, k, v, segments, memory_segments):
    grid, queries, keys, seg_row, seg_col = cross_specs(q, k)
    work = q.size // HEAD_SIZE * k.shape[1]
    return pl.pallas_call(
        cross_fwd_kernel,
        grid=grid,
        in_specs=[queries, keys, keys, seg_row, seg_col],
        out_specs=queries,
        out_shape=jax.ShapeDtypeStruct(q.shape, BF16),
        compiler_params=pltpu.CompilerParams(vmem_limit_bytes=48 << 20),
        cost_estimate=pl.CostEstimate(
            flops=work * 4 * HEAD_SIZE, transcendentals=work, bytes_accessed=q.size * 4 + k.size * 4
        ),
        name="cross_attention",
    )(q, k, v, memory_segments[:, None, :], segments[:, :, None])


def cross_attention_back(q, k, v, cots, segments, memory_segments):
    grid, queries, keys, seg_row, seg_col = cross_specs(q, k)
    work = q.size // HEAD_SIZE * k.shape[1]
    return pl.pallas_call(
        cross_bwd_kernel,
        grid=grid,
        in_specs=[queries, keys, keys, queries, seg_row, seg_col],
        out_specs=[queries, keys, keys],
        out_shape=[
            jax.ShapeDtypeStruct(q.shape, BF16),
            jax.ShapeDtypeStruct(k.shape, BF16),
            jax.ShapeDtypeStruct(k.shape, BF16),
        ],
        compiler_params=pltpu.CompilerParams(vmem_limit_bytes=48 << 20),
        cost_estimate=pl.CostEstimate(
            flops=work * 10 * HEAD_SIZE, transcendentals=work, bytes_accessed=q.size * 6 + k.size * 8
        ),
        name="cross_attention_back",
    )(q, k, v, cots, memory_segments[:, None, :], segments[:, :, None])


def bit_count(axis):
    return lax.axis_size(axis).bit_length() - 1


def flip(value, axis, bit):
    count = lax.axis_size(axis)
    return lax.ppermute(value, axis, [(i, i ^ (1 << bit)) for i in range(count)])


def scatter_order(first):
    seq_bits = list(range(bit_count("seq")))
    if first:
        seq_bits.reverse()
    return [("batch", 0)] + [("seq", b) for b in seq_bits] + [("batch", b) for b in range(1, bit_count("batch"))]


def scatter_sum(full, turned):
    batch_bits, seq_bits = bit_count("batch"), bit_count("seq")
    left = [("batch", b) for b in reversed(range(batch_bits))] + [("seq", b) for b in reversed(range(seq_bits))]
    own_rows = full.shape[0] >> len(left)
    parts = [full.reshape((2,) * len(left) + (own_rows,) + full.shape[1:])]
    for axis, bit in scatter_order(turned):
        where = left.index((axis, bit))
        mine = (lax.axis_index(axis) >> bit) & 1
        away = sum(lax.dynamic_index_in_dim(p, 1 - mine, where, False).astype(F32) for p in parts)
        came = flip(away.astype(BF16), axis, bit)
        parts = [lax.dynamic_index_in_dim(p, mine, where, False) for p in parts] + [came]
        left.pop(where)
    return sum(p.astype(F32) for p in parts)


def small_sum(values):
    got = lax.all_to_all(values, ("batch", "seq"), 0, 0, tiled=True)
    return jnp.sum(got, axis=0)


def inverse_rms(values):
    return lax.rsqrt(jnp.mean(values * values, axis=-1, keepdims=True) + EPSILON)


def norm_back(values, inverse, gain, upstream):
    weighted = gain * upstream
    dot = jnp.mean(weighted * values, axis=-1, keepdims=True)
    grad = inverse * weighted - values * (inverse * inverse * inverse) * dot
    return grad, jnp.sum(upstream * values * inverse, axis=0)


def gelu_parts(v):
    scale = 0.7978845608028654
    inner = scale * (v + 0.044715 * (v * v * v))
    t = jnp.tanh(inner)
    value = 0.5 * v * (1.0 + t)
    slope = 0.5 * (1.0 + t) + 0.5 * v * (1.0 - t * t) * (scale * (1.0 + 3 * 0.044715 * (v * v)))
    return value, slope


def shards(
    tokens, memory, output_grad, segments, memory_segments, buckets,
    w_query, keyvalue_weight, w_output, w_expand, w_reduce, gains, position_bias,
    momentum_query, keyvalue_momentum, momentum_output, momentum_expand, momentum_reduce,
    momentum_gains, momentum_position,
    average_query, keyvalue_average, average_output, average_expand, average_reduce,
    average_gains, average_position,
):
    every = ("batch", "seq")
    seq_count, seq_index = lax.axis_size("seq"), lax.axis_index("seq")
    devices = lax.axis_size("batch") * seq_count
    rows, part, width = tokens.shape
    length = part * seq_count
    memory_part = memory.shape[1]
    own = w_query.shape[1]
    kv_width = keyvalue_weight.shape[3]
    heads_local = QUERY_HEADS // seq_count
    q_local, kv_local = width // seq_count, kv_width // seq_count

    wq, wkv = w_query.astype(BF16), keyvalue_weight.astype(BF16)
    wo, we, wr = w_output.astype(BF16), w_expand.astype(BF16), w_reduce.astype(BF16)
    first = jnp.concatenate(
        [
            wq[0].reshape(own, seq_count, q_local),
            wkv[0, 0].reshape(own, seq_count, kv_local),
            wkv[0, 1].reshape(own, seq_count, kv_local),
        ],
        axis=2,
    ).reshape(own, -1)
    bias_own = position_bias.shape[0]
    small = jnp.concatenate([gains.astype(BF16).reshape(-1), position_bias.astype(BF16)])
    small = jnp.pad(small, (0, -small.shape[0] % 128))
    small_rows = lax.all_gather(small, every, axis=0)
    gain_values = (
        small_rows[:, : 3 * own].reshape(devices, 3, own).transpose(1, 0, 2).reshape(3, width).astype(F32)
    )
    table = small_rows[:, 3 * own : 3 * own + bias_own].reshape(NB, QUERY_HEADS).astype(F32)
    w_first = lax.all_gather(first, every, axis=0, tiled=True)
    middle = jnp.stack([jnp.concatenate([wkv[1, 0], wkv[1, 1]], axis=1), wo[0], wq[1], wo[1]])
    w_middle = lax.all_gather(middle, every, axis=1, tiled=True)
    w_kv1, w_o0, w_q1, w_o1 = w_middle[0], w_middle[1], w_middle[2], w_middle[3]
    w_exp = lax.all_gather(jnp.concatenate([we[0], we[1]], axis=1), every, axis=0, tiled=True)
    w_red = lax.all_gather(wr, every, axis=0, tiled=True)
    all_segments = lax.all_gather(segments, "seq", axis=1, tiled=True)
    all_memory_segments = lax.all_gather(memory_segments, "seq", axis=1, tiled=True)

    reach = length // 2
    strip_width = 2 * reach + BQ
    lag = reach - jnp.arange(strip_width, dtype=jnp.int32)
    lag_ok = lag >= 0
    lag_bucket = jnp.where(lag_ok, jnp.take(buckets, jnp.clip(lag, 0, length - 1)), -1)
    picks = (lag_bucket[None, :] == jnp.arange(NB, dtype=jnp.int32)[:, None]).astype(F32)
    table_local = lax.dynamic_slice_in_dim(table, seq_index * heads_local, heads_local, 1)
    base = jnp.dot(table_local.T, picks, precision=lax.Precision.HIGHEST)
    base = jnp.where(lag_ok[None, :], base, NEGATIVE)

    x = tokens.astype(F32).reshape(rows * part, width)
    inv_zero = inverse_rms(x)
    normed = (x * inv_zero * gain_values[0]).astype(BF16)
    qkv = nn(normed, w_first).astype(BF16).reshape(rows, part, -1)
    head_qkv = lax.all_to_all(qkv, "seq", split_axis=2, concat_axis=1, tiled=True)
    hq = head_qkv[:, :, :q_local]
    hk = head_qkv[:, :, q_local : q_local + kv_local]
    hv = head_qkv[:, :, q_local + kv_local :]
    head_context, lse = self_attention(hq, hk, hv, all_segments, base)
    context = lax.all_to_all(head_context, "seq", split_axis=1, concat_axis=2, tiled=True).reshape(-1, width)

    mem = memory.reshape(rows * memory_part, width)
    mkv = nn(mem, w_kv1).astype(BF16).reshape(rows, memory_part, -1)
    all_mkv = lax.all_gather(mkv, "seq", axis=1, tiled=True)
    mk, mv = all_mkv[:, :, :kv_width], all_mkv[:, :, kv_width:]
    hidden_one = x + nn(context, w_o0)
    inv_one = inverse_rms(hidden_one)
    normed_one = (hidden_one * inv_one * gain_values[1]).astype(BF16)
    cross_q = nn(normed_one, w_q1).astype(BF16).reshape(rows, part, width)
    cross_context = cross_attention(cross_q, mk, mv, segments, all_memory_segments)
    cross_flat = cross_context.reshape(-1, width)
    hidden_two = hidden_one + nn(cross_flat, w_o1)
    inv_two = inverse_rms(hidden_two)
    normed_two = (hidden_two * inv_two * gain_values[2]).astype(BF16)

    ff = we.shape[2]
    gate = nn(normed_two, w_exp[:, :ff])
    up = nn(normed_two, w_exp[:, ff:])
    gelu_value, gelu_slope = gelu_parts(gate)
    activated = (gelu_value * up).astype(BF16)
    og = output_grad.reshape(rows * part, width)
    result = (hidden_two + nn(activated, w_red)).astype(BF16).reshape(tokens.shape)
    grad_reduce = scatter_sum(tn(activated, og).astype(BF16), False)
    activated_grad = nt(og, w_red)
    gate_grad = (activated_grad * up * gelu_slope).astype(BF16)
    up_grad = (activated_grad * gelu_value).astype(BF16)
    grad_gate = scatter_sum(tn(normed_two, gate_grad).astype(BF16), False)
    grad_up = scatter_sum(tn(normed_two, up_grad).astype(BF16), True)
    normed_two_grad = nt(gate_grad, w_exp[:, :ff]) + nt(up_grad, w_exp[:, ff:])
    part_two, gain_two = norm_back(hidden_two, inv_two, gain_values[2], normed_two_grad)
    hidden_two_grad = og.astype(F32) + part_two

    cross_out_grad = hidden_two_grad.astype(BF16)
    grad_o1 = scatter_sum(tn(cross_flat, cross_out_grad).astype(BF16), True)
    cross_cots = nt(cross_out_grad, w_o1).astype(BF16).reshape(rows, part, width)
    cross_dq, mdk, mdv = cross_attention_back(cross_q, mk, mv, cross_cots, segments, all_memory_segments)
    mdkv = jnp.concatenate([mdk, mdv], axis=2).reshape(rows, seq_count, memory_part, -1)
    mdkv = lax.all_to_all(mdkv, "seq", split_axis=1, concat_axis=1, tiled=True)
    mdkv = jnp.sum(mdkv.astype(F32), axis=1).astype(BF16).reshape(rows * memory_part, -1)
    memory_grad = nt(mdkv, w_kv1).reshape(memory.shape)
    grad_kv1 = scatter_sum(tn(mem, mdkv).astype(BF16), False)
    cross_dq = cross_dq.reshape(-1, width)
    grad_q1 = scatter_sum(tn(normed_one, cross_dq).astype(BF16), True)
    part_one, gain_one = norm_back(hidden_one, inv_one, gain_values[1], nt(cross_dq, w_q1))
    hidden_one_grad = hidden_two_grad + part_one

    self_out_grad = hidden_one_grad.astype(BF16)
    grad_o0 = scatter_sum(tn(context, self_out_grad).astype(BF16), False)
    cots = nt(self_out_grad, w_o0).astype(BF16).reshape(rows, part, width)
    head_cots = lax.all_to_all(cots, "seq", split_axis=2, concat_axis=1, tiled=True)
    hdq, hdk, hdv, lag_sums = self_attention_back(hq, hk, hv, head_cots, lse, all_segments, base)
    head_grads = jnp.concatenate([hdq, hdk, hdv], axis=2)
    dqkv = lax.all_to_all(head_grads, "seq", split_axis=1, concat_axis=2, tiled=True).reshape(rows * part, -1)
    grad_first = scatter_sum(tn(normed, dqkv).astype(BF16), False)
    part_zero, gain_zero = norm_back(x, inv_zero, gain_values[0], nt(dqkv, w_first))
    input_grad = (hidden_one_grad + part_zero).reshape(tokens.shape)

    table_part = jnp.dot(picks, lag_sums.T, precision=lax.Precision.HIGHEST)
    table_grad = lax.dynamic_update_slice(
        jnp.zeros((NB, QUERY_HEADS), F32), table_part, (0, seq_index * heads_local)
    ).reshape(devices, -1)
    gains_grad = jnp.stack([gain_zero, gain_one, gain_two]).reshape(3, devices, own)
    gains_grad = gains_grad.transpose(1, 0, 2).reshape(devices, -1)
    small_grads = small_sum(jnp.concatenate([gains_grad, table_grad], axis=1))
    shard_gains = small_grads[: 3 * own].reshape(3, own)
    shard_table = small_grads[3 * own :]

    first_grads = grad_first.reshape(own, seq_count, -1)
    shard_query = jnp.stack([first_grads[:, :, :q_local].reshape(own, width), grad_q1])
    shard_keyval = jnp.stack(
        [
            jnp.stack(
                [
                    first_grads[:, :, q_local : q_local + kv_local].reshape(own, kv_width),
                    first_grads[:, :, q_local + kv_local :].reshape(own, kv_width),
                ]
            ),
            jnp.stack([grad_kv1[:, :kv_width], grad_kv1[:, kv_width:]]),
        ]
    )
    gradients = (
        shard_query,
        shard_keyval,
        jnp.stack([grad_o0, grad_o1]),
        jnp.stack([grad_gate, grad_up]),
        grad_reduce,
        shard_gains,
        shard_table,
    )
    token_scale = (rows * part * devices) ** (-0.5)
    masters = (w_query, keyvalue_weight, w_output, w_expand, w_reduce, gains, position_bias)
    momenta = (
        momentum_query, keyvalue_momentum, momentum_output, momentum_expand, momentum_reduce,
        momentum_gains, momentum_position,
    )
    averages = (
        average_query, keyvalue_average, average_output, average_expand, average_reduce,
        average_gains, average_position,
    )
    renewals, states = [], []
    for gradient, master, momentum, average, step_rate in zip(gradients, masters, momenta, averages, STEP_RATES):
        renewed = MOMENTUM * momentum + gradient
        weight = master - step_rate * token_scale * (gradient + MOMENTUM * renewed)
        renewals.append(renewed)
        states.append(jnp.stack([weight, AVERAGE * average + (1.0 - AVERAGE) * weight]))
    return (result, input_grad, memory_grad.astype(F32), *gradients, *renewals, *states)


def solution(mesh):
    every = ("batch", "seq")
    params = (
        P(None, every, None),
        P(None, None, every, None),
        P(None, every, None),
        P(None, every, None),
        P(every, None),
        P(None, every),
        P(every),
    )
    stacked_params = (
        P(None, None, every, None),
        P(None, None, None, every, None),
        P(None, None, every, None),
        P(None, None, every, None),
        P(None, every, None),
        P(None, None, every),
        P(None, every),
    )
    acts = P("batch", "seq", None)
    return jax.shard_map(
        shards,
        mesh=mesh,
        in_specs=(acts, acts, acts, P("batch", "seq"), P("batch", "seq"), P(), *params, *params, *params),
        out_specs=(acts, acts, acts, *params, *params, *stacked_params),
        check_vma=False,
    )
```

time: 3390 us -> 793 us (0.23)
  waiting for transfers between devices: 1380 us -> 265 us
  local copies, waits for them, and re-layouts: 1180 us -> 79 us
  matrix products: 278 us -> 102 us
  other arithmetic: 219 us -> 78.1 us
  blocking collectives: 206 us -> 107 us
  Pallas kernels: 0 us -> 71.5 us
  loops' own time: 41.1 us -> 0 us
    reduce_scatter x5 -> x0, waiting for transfers between devices: 1290 us -> none  [the longest x1 490 us: shards(): lax.psum_scatter(grad_expand_full, ('batch', 'seq'), scatter_dimension=1,...]
    while x107 -> x0, local copies, waits for them, and re-layouts: 590 us -> none
    reshape x34 -> x7, local copies, waits for them, and re-layouts: 244 us -> 10.5 us  [the longest x1 3.84 us: shards(): qkv = nn(normed, w_first).astype(BF16).reshape(rows, part, -1)]
    dot_general x101 -> x26, matrix products: 278 us -> 102 us  [the longest x8 40.4 us: nn(): lax.dot_general(a, b, (((1,), (0,)), ((), ())), preferred_element_type=F32)]
    ppermute x0 -> x40, waiting for transfers between devices: none -> 125 us  [flip(): return lax.ppermute(value, axis, [(i, i ^ 1 << bit) for i in range(count)])]
    all_gather x5, waiting for transfers between devices: 39.1 us -> 140 us  [the longest x1 78.9 us: shards(): w_middle = lax.all_gather(middle, every, axis=1, tiled=True)]
    slice x21 -> x8, local copies, waits for them, and re-layouts: 96.1 us -> 3.27 us  [the longest x1 1.46 us: shards(): hq = head_qkv[:, :, :q_local]]
    unnamed x2 -> x0, blocking collectives: 86.2 us -> none
  transfers between devices with their start and end apart: 25 -> 51, of which waited for: 16 -> 23; matrix products, arithmetic and copies ran while one was open for 20% -> 23% of each run, Pallas kernels for 0% -> 7%
where the time goes in v1:
time: 793 us; the launch traced here: 786 us
  waiting for transfers between devices  265 us (33%)
  blocking collectives  107 us (13%)
  matrix products  102 us (13%)
  local copies, waits for them, and re-layouts  79 us (10%)
  other arithmetic  78.1 us (10%)
  Pallas kernels  71.5 us (9%)
  starting transfers between devices  67.3 us (8%)
  between operations  15.7 us (2%)
    ppermute x40, waiting for transfers between devices, flip(): return lax.ppermute(value, axis, [(i, i ^ 1 << bit) for i in range(count)])  125 us
    all_gather x1, waiting for transfers between devices, shards(): w_middle = lax.all_gather(middle, every, axis=1, tiled=True)  78.9 us
    all_gather x1, blocking collectives, shards(): small_rows = lax.all_gather(small, every, axis=0)  65.7 us
    all_gather x1, waiting for transfers between devices, shards(): lax.all_gather(jnp.concatenate([we[0], we[1]], axis=1), every, axis=0, ti...  61.2 us
    convert_element_type x32, other arithmetic, scatter_sum(): came = flip(away.astype(BF16), axis, bit)  44 us
    ppermute x40, starting transfers between devices, flip(): return lax.ppermute(value, axis, [(i, i ^ 1 << bit) for i in range(count)])  41.9 us
    dot_general x8, matrix products, nn(): lax.dot_general(a, b, (((1,), (0,)), ((), ())), preferred_element_type=F32)  40.4 us
    dot_general x8, matrix products, nt(): lax.dot_general(a, b, (((1,), (1,)), ((), ())), preferred_element_type=F32)  33.2 us
  transfers between devices with their start and end apart: 51, of which 23 were waited for; matrix products, arithmetic and copies ran while one was open for 23% of the time, Pallas kernels for 7%

profile of v1, /device:TPU:0, one launch (start us, length us, event | category | flops | bytes accessed | tf_op | source)
XLA Modules:
  0.0 785.8 jit_solution(2565932802142267520)
XLA Ops:
  12.8 78.9 %all-gather.11.cloned.1.call-done = bf16[4,1024,1024]{2,1,0:T(8,128)(2,1)} async-done(((bf16[4,32,1024]{2,1,0:T(8,128)(2,1)}), bf16[4,1024,1024]{2,1,0:T(8,128)(2,1)}) %all-gather.11.cloned.1.call-update) | async-done | bytes 8388624 | tf_op jit(solution)/shard_map/all_gather | solution.py:417
  95.6 65.7 %all-gather.1 = bf16[32,1,128]{2,1,0:T(2,128)(2,1)S(1)} all-gather(bf16[1,1,128]{2,1,0:T(2,128)(2,1)S(1)} %fusion.109), channel_id=2, replica_groups=mesh['batch'=8,'seq'=4] {'batch','seq'}, dimensions={0}, use_global_device_ids=true | all-gather | bytes 8448 | tf_op jit(solution)/shard_map/all_gather | solution.py:410
  174.4 28.7 %all_gather.30 = s32[2,1024]{1,0:T(2,128)S(1)} all-gather(s32[2,256]{1,0:T(2,128)S(1)} %copy-done.73), channel_id=1, replica_groups=mesh['batch'=8,'seq'=4] {'seq'}, dimensions={1}, use_global_device_ids=true | all-gather | bytes 10240 | tf_op jit(solution)/shard_map/all_gather | solution.py:421
  203.9 4.6 gather_fusion
  216.7 18.2 %self_attention.1 = (bf16[2,1024,256]{2,1,0:T(8,128)(2,1)S(1)}, f32[2,1024,4]{2,1,0:T(8,128)S(1)}) custom-call(bf16[2,1024,256]{2,1,0:T(8,128)(2,1)S(1)} %slice.147.q_ref, bf16[2,1024,128]{2,1,0:T(8,128)(2,1)S(1)} %get-tuple-element.148.k_ref, bf16[2,1024,128]{2,1,0:T(8,128)(2,1)S(1)} %get-tuple-element.147.v_ref, ...), custom_call_target="tpu_custom_call" | custom-call | flops 805306368 | bytes 4194304 | tf_op jit(solution)/shard_map/self_attention/pallas_call | solution.py:170
  242.5 12.8 %all-gather.2 = s32[4,64,2]{1,2,0:T(2,128)S(1)} all-gather(s32[1,64,2]{1,2,0:T(2,128)S(1)} %bitcast.874), channel_id=1, replica_groups=mesh['batch'=8,'seq'=4] {'seq'}, dimensions={0}, use_global_device_ids=true | all-gather | bytes 2560 | tf_op jit(solution)/shard_map/all_gather | solution.py:422
  261.2 8.8 %fusion.123 = f32[512,2816]{1,0:T(8,128)} fusion(bf16[512,1024]{1,0:T(8,128)(2,1)} %bitcast.852, bf16[2816,1024]{1,0:T(8,128)(2,1)} %all-gather.17.cloned.1.call-done), kind=kOutput, calls=%fused_computation.365 | convolution fusion | flops 2952790016 | bytes 12582912 | tf_op jit(solution)/shard_map/dot_general | solution.py:24
  279.8 11.3 %cross_attention.1 = bf16[2,256,1024]{2,1,0:T(8,128)(2,1)S(1)} custom-call(bf16[2,256,1024]{2,1,0:T(8,128)(2,1)S(1)} %bitcast.784, bf16[2,256,512]{2,1,0:T(8,128)(2,1)S(1)} %get-tuple-element.150.k_ref, bf16[2,256,512]{2,1,0:T(8,128)(2,1)S(1)} %get-tuple-element.149.v_ref, s32[2,1,256]{2,1,0:T(1,128)S(1)} %broadcast_in_dim.56.seg_row_ref, ...), custom_call_target="tpu_custom_call" | custom-call | flops 536870912 | bytes 3145728 | tf_op jit(solution)/shard_map/cross_attention/pallas_call | solution.py:287
  296.1 61.2 %all-gather.15.cloned.1.call-done = bf16[1024,5632]{1,0:T(8,128)(2,1)} async-done(((bf16[32,5632]{1,0:T(8,128)(2,1)}), bf16[1024,5632]{1,0:T(8,128)(2,1)}) %all-gather.15.cloned.1.call-update) | async-done | bytes 11534352 | tf_op jit(solution)/shard_map/all_gather | solution.py:419
  357.3 7.6 fusion.12
  364.9 11.1 %fusion.9 = (bf16[512,2816]{1,0:T(8,128)(2,1)S(1)}, bf16[512,2816]{1,0:T(8,128)(2,1)S(1)}, bf16[512,2816]{1,0:T(8,128)(2,1)}) fusion(f32[512,2816]{1,0:T(8,128)} %fusion.123, f32[512,2816]{1,0:T(8,128)} %fusion.12, bf16[512,1024]{1,0:T(8,128)(2,1)S(1)} %multiply_convert_fusion.2, bf16[1024,5632]{1,0:T(8,128)(2,1)S(1)} %copy-done.81), kind=kOutput, calls=%fused_computation.12 | convolution fusion | flops 2987393024 | bytes 27000832 | tf_op jit(solution)/shard_map/dot_general | solution.py:28
  376.1 5.3 convolution_convert_fusion.2
  397.1 15.2 %cross_attention_back.1 = (bf16[2,256,1024]{2,1,0:T(8,128)(2,1)S(1)}, bf16[2,256,512]{2,1,0:T(8,128)(2,1)S(1)}, bf16[2,256,512]{2,1,0:T(8,128)(2,1)S(1)}) custom-call(bf16[2,256,1024]{2,1,0:T(8,128)(2,1)S(1)} %bitcast.785, bf16[2,256,512]{2,1,0:T(8,128)(2,1)S(1)} %copy-done.5, bf16[2,256,512]{2,1,0:T(8,128)(2,1)S(1)} %copy-done.3, ...), custom_call_target="tpu_custom_call" | custom-call | flops 1342177280 | bytes 5242880 | tf_op jit(solution)/shard_map/cross_attention_back/pallas_call | solution.py:304
  433.7 5.3 convolution_convert_fusion
  461.7 5.3 convolution_convert_fusion.1
  479.3 26.8 %self_attention_back.1 = (bf16[2,1024,256]{2,1,0:T(8,128)(2,1)S(1)}, bf16[2,1024,128]{2,1,0:T(8,128)(2,1)S(1)}, bf16[2,1024,128]{2,1,0:T(8,128)(2,1)S(1)}, f32[4,1152]{1,0:T(4,128)S(1)}) custom-call(bf16[2,1024,256]{2,1,0:T(8,128)(2,1)S(1)} %slice.147.q_ref, bf16[2,1024,128]{2,1,0:T(8,128)(2,1)S(1)} %get-tuple-element.148.k_ref, ...), custom_call_target="tpu_custom_call" | custom-call | flops 2013265920 | bytes 6291456 | tf_op jit(solution)/shard_map/self_attention_back/pallas_call | solution.py:196
  530.1 21.0 %collective-permute-done.16 = bf16[2,2,2,32,1024]{4,3,2,1,0:T(8,128)(2,1)S(1)} collective-permute-done((bf16[2,2,2,32,1024]{4,3,2,1,0:T(8,128)(2,1)S(1)}, bf16[2,2,2,32,1024]{4,3,2,1,0:T(8,128)(2,1)S(1)}, u32[]{:S(2)}, u32[]{:S(2)}) %collective-permute-start.16) | collective-permute-done | bytes 524320 | tf_op jit(solution)/shard_map/ppermute | solution.py:328
  556.0 7.0 collective-permute-done.6
  657.2 15.0 %collective-permute-done.36 = bf16[2,2,2,88,1024]{4,3,2,1,0:T(8,128)(2,1)S(1)} collective-permute-done((bf16[2,2,2,88,1024]{4,3,2,1,0:T(8,128)(2,1)S(1)}, bf16[2,2,2,88,1024]{4,3,2,1,0:T(8,128)(2,1)S(1)}, u32[]{:S(2)}, u32[]{:S(2)}) %collective-permute-start.36) | collective-permute-done | bytes 1441824 | tf_op jit(solution)/shard_map/ppermute | solution.py:328
  674.1 27.9 %collective-permute-done.26 = bf16[2,2,2,32,2816]{4,3,2,1,0:T(8,128)(2,1)S(1)} collective-permute-done((bf16[2,2,2,32,2816]{4,3,2,1,0:T(8,128)(2,1)S(1)}, bf16[2,2,2,32,2816]{4,3,2,1,0:T(8,128)(2,1)S(1)}, u32[]{:S(2)}, u32[]{:S(2)}) %collective-permute-start.26) | collective-permute-done | bytes 1441824 | tf_op jit(solution)/shard_map/ppermute | solution.py:328
  712.2 8.7 %collective-permute-done.27 = bf16[2,2,32,2816]{3,2,0,1:T(8,128)(2,1)S(1)} collective-permute-done((bf16[2,2,32,2816]{3,2,0,1:T(8,128)(2,1)S(1)}, bf16[2,2,32,2816]{3,2,0,1:T(8,128)(2,1)S(1)}, u32[]{:S(2)}, u32[]{:S(2)}) %collective-permute-start.27) | collective-permute-done | bytes 720928 | tf_op jit(solution)/shard_map/ppermute | solution.py:328
  730.8 8.5 %collective-permute-done.28 = bf16[2,32,2816]{2,1,0:T(8,128)(2,1)S(1)} collective-permute-done((bf16[2,32,2816]{2,1,0:T(8,128)(2,1)S(1)}, bf16[2,32,2816]{2,1,0:T(8,128)(2,1)S(1)}, u32[]{:S(2)}, u32[]{:S(2)}) %collective-permute-start.28) | collective-permute-done | bytes 360480 | tf_op jit(solution)/shard_map/ppermute | solution.py:328
  747.9 6.8 collective-permute-done.29
  769.9 5.4 collective-permute-done.4
  (466 shorter events, 303.1 us)
Async XLA Ops:
  7.2 84.5 %all-gather.11.cloned.1.call-start = ((), (), s32[]{:S(2)}) async-start(), calls=%async_computation.7 | async-start | bytes 8650752 | tf_op jit(solution)/shard_map/all_gather | solution.py:417
  11.1 151.2 %all-gather.9.cloned.1.call-start = ((), (), s32[]{:S(2)}) async-start(), calls=%async_computation.6 | async-start | bytes 4325376 | tf_op jit(solution)/shard_map/all_gather | solution.py:415
  12.0 249.2 %all-gather.17.cloned.1.call-start = ((), (), s32[]{:S(2)}) async-start(), calls=%async_computation.10 | async-start | bytes 5947392 | tf_op jit(solution)/shard_map/all_gather | solution.py:420
  12.8 265.5 %all-gather.13.cloned.1.call-start = ((), (), s32[]{:S(2)}) async-start(), calls=%async_computation.8 | async-start | bytes 1310720 | tf_op jit(solution)/shard_map/all_gather | solution.py:447
  94.5 262.8 %all-gather.15.cloned.1.call-start = ((), (), s32[]{:S(2)}) async-start(), calls=%async_computation.9 | async-start | bytes 11894784 | tf_op jit(solution)/shard_map/all_gather | solution.py:419
  170.6 38.2 %all-to-all-start = ((bf16[2,256,2048]{1,0,2:T(2,128)(2,1)}), bf16[2,256,2048]{1,0,2:T(2,128)(2,1)S(1)}, u32[]{:S(2)}, u32[]{:S(2)}) async-start(bf16[2,256,2048]{1,0,2:T(2,128)(2,1)} %copy.162), calls=%async_computation | async-start | bytes 4194304 | tf_op jit(solution)/shard_map/all_to_all | solution.py:438
  442.4 192.8 %collective-permute-start.35 = (bf16[2,2,2,2,88,1024]{5,4,3,2,1,0:T(8,128)(2,1)}, bf16[2,2,2,2,88,1024]{5,4,3,2,1,0:T(8,128)(2,1)}, u32[]{:S(2)}, u32[]{:S(2)}) collective-permute-start(bf16[2,2,2,2,88,1024]{5,4,3,2,1,0:T(8,128)(2,1)} %dynamic-slice_bitcast_fusion), channel_id=1, source_target_pairs={{0,4},{4,0},{8,12},{12,8},{16,20},{20,16},{24,28},{28,24},{1,5},{5... | collective-permute-start | bytes 8650760 | tf_op jit(solution)/shard_map/ppermute | solution.py:328
  447.6 70.3 %collective-permute-start.15 = (bf16[2,2,2,2,32,1024]{5,4,0,3,2,1:T(8,128)(2,1)}, bf16[2,2,2,2,32,1024]{5,4,0,3,2,1:T(8,128)(2,1)}, u32[]{:S(2)}, u32[]{:S(2)}) collective-permute-start(bf16[2,2,2,2,32,1024]{5,4,0,3,2,1:T(8,128)(2,1)} %copy.198), channel_id=1, source_target_pairs={{0,4},{4,0},{8,12},{12,8},{16,20},{20,16},{24,28},{28,24},{1,5},{5... | collective-permute-start | bytes 3145736 | tf_op jit(solution)/shard_map/ppermute | solution.py:328
  449.5 71.7 %collective-permute-start.20 = (bf16[2,2,2,2,32,1024]{5,4,0,3,2,1:T(8,128)(2,1)}, bf16[2,2,2,2,32,1024]{5,4,0,3,2,1:T(8,128)(2,1)}, u32[]{:S(2)}, u32[]{:S(2)}) collective-permute-start(bf16[2,2,2,2,32,1024]{5,4,0,3,2,1:T(8,128)(2,1)} %copy.204), channel_id=1, source_target_pairs={{0,4},{4,0},{8,12},{12,8},{16,20},{20,16},{24,28},{28,24},{1,5},{5... | collective-permute-start | bytes 3145736 | tf_op jit(solution)/shard_map/ppermute | solution.py:328
  452.9 71.3 %collective-permute-start.5 = (bf16[2,2,2,2,32,1024]{5,4,3,2,1,0:T(8,128)(2,1)}, bf16[2,2,2,2,32,1024]{5,4,3,2,1,0:T(8,128)(2,1)}, u32[]{:S(2)}, u32[]{:S(2)}) collective-permute-start(bf16[2,2,2,2,32,1024]{5,4,3,2,1,0:T(8,128)(2,1)} %dynamic-slice_bitcast_fusion.6), channel_id=1, source_target_pairs={{0,4},{4,0},{8,12},{12,8},{16,20},{20,16},{24,28},{28,24},{1,5},{5... | collective-permute-start | bytes 3145736 | tf_op jit(solution)/shard_map/ppermute | solution.py:328
  457.3 52.4 %all-to-all-start.4 = ((bf16[2,4,64,1024]{3,2,0,1:T(8,128)(2,1)}), bf16[2,4,64,1024]{3,2,0,1:T(8,128)(2,1)}, u32[]{:S(2)}, u32[]{:S(2)}) async-start(bf16[2,4,64,1024]{3,2,0,1:T(8,128)(2,1)} %copy.177), calls=%async_computation.4 | async-start | bytes 2097152 | tf_op jit(solution)/shard_map/all_to_all | solution.py:481
  509.7 91.3 %all-to-all-start.3 = ((bf16[2,1024,512]{2,0,1:T(2,128)(2,1)}), bf16[2,1024,512]{2,0,1:T(2,128)(2,1)}, u32[]{:S(2)}, u32[]{:S(2)}) async-start(bf16[2,1024,512]{2,0,1:T(2,128)(2,1)} %copy.175), calls=%async_computation.3 | async-start | bytes 4194304 | tf_op jit(solution)/shard_map/all_to_all | solution.py:496
  517.6 53.0 %collective-permute-start.10 = (bf16[2,2,2,2,32,1024]{5,4,3,2,1,0:T(8,128)(2,1)}, bf16[2,2,2,2,32,1024]{5,4,3,2,1,0:T(8,128)(2,1)}, u32[]{:S(2)}, u32[]{:S(2)}) collective-permute-start(bf16[2,2,2,2,32,1024]{5,4,3,2,1,0:T(8,128)(2,1)} %dynamic-slice_bitcast_fusion.5), channel_id=1, source_target_pairs={{0,4},{4,0},{8,12},{12,8},{16,20},{20,16},{24,28},{28,24},{1,5},{5... | collective-permute-start | bytes 3145736 | tf_op jit(solution)/shard_map/ppermute | solution.py:328
  526.4 36.5 %collective-permute-start.6 = (bf16[2,2,2,32,1024]{4,3,2,1,0:T(8,128)(2,1)}, bf16[2,2,2,32,1024]{4,3,2,1,0:T(8,128)(2,1)}, u32[]{:S(2)}, u32[]{:S(2)}) collective-permute-start(bf16[2,2,2,32,1024]{4,3,2,1,0:T(8,128)(2,1)} %fusion.61), channel_id=1, source_target_pairs={{0,2},{1,3},{2,0},{3,1},{4,6},{5,7},{6,4},{7,5},{8,10},{9,11},{10,... | collective-permute-start | bytes 1572872 | tf_op jit(solution)/shard_map/ppermute | solution.py:328
  554.6 83.9 %collective-permute-start.25 = (bf16[2,2,2,2,32,2816]{5,4,3,2,1,0:T(8,128)(2,1)}, bf16[2,2,2,2,32,2816]{5,4,3,2,1,0:T(8,128)(2,1)}, u32[]{:S(2)}, u32[]{:S(2)}) collective-permute-start(bf16[2,2,2,2,32,2816]{5,4,3,2,1,0:T(8,128)(2,1)} %dynamic-slice_bitcast_fusion.2), channel_id=1, source_target_pairs={{0,4},{4,0},{8,12},{12,8},{16,20},{20,16},{24,28},{28,24},{1,5},{5... | collective-permute-start | bytes 8650760 | tf_op jit(solution)/shard_map/ppermute | solution.py:328
  570.5 71.5 %collective-permute-start.30 = (bf16[2,2,2,2,32,2816]{5,4,0,3,2,1:T(8,128)(2,1)}, bf16[2,2,2,2,32,2816]{5,4,0,3,2,1:T(8,128)(2,1)}, u32[]{:S(2)}, u32[]{:S(2)}) collective-permute-start(bf16[2,2,2,2,32,2816]{5,4,0,3,2,1:T(8,128)(2,1)} %copy.217), channel_id=1, source_target_pairs={{0,4},{4,0},{8,12},{12,8},{16,20},{20,16},{24,28},{28,24},{1,5},{5... | collective-permute-start | bytes 8650760 | tf_op jit(solution)/shard_map/ppermute | solution.py:328
  581.9 44.5 %collective-permute-start.11 = (bf16[2,2,2,32,1024]{4,3,2,1,0:T(8,128)(2,1)}, bf16[2,2,2,32,1024]{4,3,2,1,0:T(8,128)(2,1)}, u32[]{:S(2)}, u32[]{:S(2)}) collective-permute-start(bf16[2,2,2,32,1024]{4,3,2,1,0:T(8,128)(2,1)} %fusion.60), channel_id=1, source_target_pairs={{0,1},{1,0},{2,3},{3,2},{4,5},{5,4},{6,7},{7,6},{8,9},{9,8},{10,11... | collective-permute-start | bytes 1572872 | tf_op jit(solution)/shard_map/ppermute | solution.py:328
  626.2 80.9 %collective-permute-start = (bf16[2,2,2,2,32,2048]{5,4,0,3,2,1:T(8,128)(2,1)}, bf16[2,2,2,2,32,2048]{5,4,0,3,2,1:T(8,128)(2,1)}, u32[]{:S(2)}, u32[]{:S(2)}) collective-permute-start(bf16[2,2,2,2,32,2048]{5,4,0,3,2,1:T(8,128)(2,1)} %copy_bitcast_fusion), channel_id=1, source_target_pairs={{0,4},{4,0},{8,12},{12,8},{16,20},{20,16},{24,28},{28,24},{1,5},{5... | collective-permute-start | bytes 6291464 | tf_op jit(solution)/shard_map/ppermute | solution.py:328
  637.7 34.5 %collective-permute-start.36 = (bf16[2,2,2,88,1024]{4,3,2,1,0:T(8,128)(2,1)S(1)}, bf16[2,2,2,88,1024]{4,3,2,1,0:T(8,128)(2,1)S(1)}, u32[]{:S(2)}, u32[]{:S(2)}) collective-permute-start(bf16[2,2,2,88,1024]{4,3,2,1,0:T(8,128)(2,1)S(1)} %fusion.18), channel_id=1, source_target_pairs={{0,1},{1,0},{2,3},{3,2},{4,5},{5,4},{6,7},{7,6},{8,9},{9,8},{10,11... | collective-permute-start | bytes 4325384 | tf_op jit(solution)/shard_map/ppermute | solution.py:328
  640.7 61.4 %collective-permute-start.26 = (bf16[2,2,2,32,2816]{4,3,2,1,0:T(8,128)(2,1)S(1)}, bf16[2,2,2,32,2816]{4,3,2,1,0:T(8,128)(2,1)S(1)}, u32[]{:S(2)}, u32[]{:S(2)}) collective-permute-start(bf16[2,2,2,32,2816]{4,3,2,1,0:T(8,128)(2,1)S(1)} %fusion.20), channel_id=1, source_target_pairs={{0,1},{1,0},{2,3},{3,2},{4,5},{5,4},{6,7},{7,6},{8,9},{9,8},{10,11... | collective-permute-start | bytes 4325384 | tf_op jit(solution)/shard_map/ppermute | solution.py:328
  643.8 60.3 %collective-permute-start.31 = (bf16[2,2,2,32,2816]{4,3,2,1,0:T(8,128)(2,1)S(1)}, bf16[2,2,2,32,2816]{4,3,2,1,0:T(8,128)(2,1)S(1)}, u32[]{:S(2)}, u32[]{:S(2)}) collective-permute-start(bf16[2,2,2,32,2816]{4,3,2,1,0:T(8,128)(2,1)S(1)} %fusion.19), channel_id=1, source_target_pairs={{0,2},{1,3},{2,0},{3,1},{4,6},{5,7},{6,4},{7,5},{8,10},{9,11},{10,... | collective-permute-start | bytes 4325384 | tf_op jit(solution)/shard_map/ppermute | solution.py:328
  674.0 35.7 %collective-permute-start.37 = (bf16[2,2,88,1024]{3,2,0,1:T(8,128)(2,1)S(1)}, bf16[2,2,88,1024]{3,2,0,1:T(8,128)(2,1)S(1)}, u32[]{:S(2)}, u32[]{:S(2)}) collective-permute-start(bf16[2,2,88,1024]{3,2,0,1:T(8,128)(2,1)S(1)} %copy.227), channel_id=1, source_target_pairs={{0,2},{1,3},{2,0},{3,1},{4,6},{5,7},{6,4},{7,5},{8,10},{9,11},{10,... | collective-permute-start | bytes 2162696 | tf_op jit(solution)/shard_map/ppermute | solution.py:328
  708.9 37.1 %collective-permute-start.1 = (bf16[2,2,2,32,2048]{4,3,2,1,0:T(8,128)(2,1)S(1)}, bf16[2,2,2,32,2048]{4,3,2,1,0:T(8,128)(2,1)S(1)}, u32[]{:S(2)}, u32[]{:S(2)}) collective-permute-start(bf16[2,2,2,32,2048]{4,3,2,1,0:T(8,128)(2,1)S(1)} %copy.180), channel_id=1, source_target_pairs={{0,1},{1,0},{2,3},{3,2},{4,5},{5,4},{6,7},{7,6},{8,9},{9,8},{10,11... | collective-permute-start | bytes 3145736 | tf_op jit(solution)/shard_map/ppermute | solution.py:328
  728.4 34.5 %collective-permute-start.39 = (bf16[88,1024]{1,0:T(8,128)(2,1)S(1)}, bf16[88,1024]{1,0:T(8,128)(2,1)S(1)}, u32[]{:S(2)}, u32[]{:S(2)}) collective-permute-start(bf16[88,1024]{1,0:T(8,128)(2,1)S(1)} %fusion.75), channel_id=1, source_target_pairs={{0,16},{4,20},{8,24},{12,28},{16,0},{20,4},{24,8},{28,12},{1,17},{... | collective-permute-start | bytes 540680 | tf_op jit(solution)/shard_map/ppermute | solution.py:328
  (117 other events, 1291.9 us)
Sparse Core Ops, SparseCore 0:
  11.6 80.0 all-gather.10
  95.1 60.6 all-gather.8
  159.3 69.4 all-gather.16
  231.1 31.5 all-gather.12
  266.0 91.2 all-gather.14

commit v2 on v1

--- a/solution.py
+++ b/solution.py
@@ -69,18 +69,24 @@
         yield here, slice(start, (step + 1) * BQ), slice(lead, lead + (step + 1) * BQ - start)
 
 
-def self_fwd_kernel(q_ref, k_ref, v_ref, seg_row_ref, seg_col_ref, base_ref, o_ref, lse_ref, strip_ref):
+def head_layout(heads, width):
+    q_width = heads * HEAD_SIZE
+    k_width = (width - q_width) // 2
+    return slice(0, q_width), slice(q_width, q_width + k_width), slice(q_width + k_width, width), k_width // HEAD_SIZE
+
+
+def self_fwd_kernel(qkv_ref, seg_row_ref, seg_col_ref, base_ref, o_ref, lse_ref, strip_ref):
     heads = strip_ref.shape[0]
-    groups = k_ref.shape[2] // HEAD_SIZE
+    in_q, in_k, in_v, groups = head_layout(heads, qkv_ref.shape[2])
     per = heads // groups
 
     @pl.when(pl.program_id(0) == 0)
     def _():
         make_strips(base_ref, strip_ref)
 
-    for here, seen, strip in windows(k_ref.shape[1]):
+    for here, seen, strip in windows(qkv_ref.shape[1]):
         same = seg_col_ref[0, here, :] == seg_row_ref[0, :, seen]
-        block, keys, values = q_ref[0, here, :], k_ref[0, seen, :], v_ref[0, seen, :]
+        block, keys, values = qkv_ref[0, here, in_q], qkv_ref[0, seen, in_k], qkv_ref[0, seen, in_v]
         outs, sums = [], []
         for g in range(groups):
             scores = nt(stacked(block, g, per), lanes(keys, g))
@@ -100,11 +106,11 @@
 
 
 def self_bwd_kernel(
-    q_ref, k_ref, v_ref, c_ref, lse_ref, seg_row_ref, seg_col_ref, base_ref,
-    dq_ref, dk_ref, dv_ref, lag_ref, strip_ref, grad_ref, dk_acc, dv_acc,
+    qkv_ref, c_ref, lse_ref, seg_row_ref, seg_col_ref, base_ref,
+    d_ref, lag_ref, strip_ref, grad_ref, dk_acc, dv_acc,
 ):
     heads = strip_ref.shape[0]
-    groups = k_ref.shape[2] // HEAD_SIZE
+    in_q, in_k, in_v, groups = head_layout(heads, qkv_ref.shape[2])
     per = heads // groups
 
     @pl.when(pl.program_id(0) == 0)
@@ -114,9 +120,9 @@
 
     dk_acc[...] = jnp.zeros_like(dk_acc)
     dv_acc[...] = jnp.zeros_like(dv_acc)
-    for here, seen, strip in windows(k_ref.shape[1]):
+    for here, seen, strip in windows(qkv_ref.shape[1]):
         same = seg_col_ref[0, here, :] == seg_row_ref[0, :, seen]
-        block, keys, values = q_ref[0, here, :], k_ref[0, seen, :], v_ref[0, seen, :]
+        block, keys, values = qkv_ref[0, here, in_q], qkv_ref[0, seen, in_k], qkv_ref[0, seen, in_v]
         cots, lse = c_ref[0, here, :], lse_ref[0, here, :]
         outs = []
         for g in range(groups):
@@ -140,9 +146,9 @@
             mine = slice(g * HEAD_SIZE, (g + 1) * HEAD_SIZE)
             dk_acc[mine, seen] += tn(q2, ds2)
             dv_acc[mine, seen] += tn(c2, p2)
-        dq_ref[0, here, :] = jnp.concatenate(outs, axis=1)
-    dk_ref[0] = dk_acc[...].T.astype(BF16)
-    dv_ref[0] = dv_acc[...].T.astype(BF16)
+        d_ref[0, here, in_q] = jnp.concatenate(outs, axis=1)
+    d_ref[0, :, in_k] = dk_acc[...].T.astype(BF16)
+    d_ref[0, :, in_v] = dv_acc[...].T.astype(BF16)
 
     @pl.when(pl.program_id(0) == pl.num_programs(0) - 1)
     def _():
@@ -150,58 +156,52 @@
             lag_ref[h : h + 1, :] = jnp.sum(skew(grad_ref[h], True), axis=0, keepdims=True)
 
 
-def self_specs(length, q_width, k_width, heads, strip_width):
-    queries = pl.BlockSpec((1, length, q_width), lambda r: (r, 0, 0))
-    keys = pl.BlockSpec((1, length, k_width), lambda r: (r, 0, 0))
+def self_specs(length, width, heads, strip_width):
+    qkv = pl.BlockSpec((1, length, width), lambda r: (r, 0, 0))
+    queries = pl.BlockSpec((1, length, heads * HEAD_SIZE), lambda r: (r, 0, 0))
     sums = pl.BlockSpec((1, length, heads), lambda r: (r, 0, 0))
     seg_row = pl.BlockSpec((1, 1, length), lambda r: (r, 0, 0))
     seg_col = pl.BlockSpec((1, length, 1), lambda r: (r, 0, 0))
     base = pl.BlockSpec((heads, strip_width), lambda r: (0, 0))
-    return queries, keys, sums, seg_row, seg_col, base
-
-
-def self_attention(q, k, v, segments, base):
-    rows, length, q_width = q.shape
+    return qkv, queries, sums, seg_row, seg_col, base
+
+
+def self_attention(qkv, segments, base):
+    rows, length, width = qkv.shape
     heads, strip_width = base.shape
-    queries, keys, sums, seg_row, seg_col, base_spec = self_specs(
-        length, q_width, k.shape[2], heads, strip_width
-    )
+    all_spec, queries, sums, seg_row, seg_col, base_spec = self_specs(length, width, heads, strip_width)
     work = rows * heads * length * length * 3 // 8
     return pl.pallas_call(
         self_fwd_kernel,
         grid=(rows,),
-        in_specs=[queries, keys, keys, seg_row, seg_col, base_spec],
+        in_specs=[all_spec, seg_row, seg_col, base_spec],
         out_specs=[queries, sums],
         out_shape=[
-            jax.ShapeDtypeStruct(q.shape, BF16),
+            jax.ShapeDtypeStruct((rows, length, heads * HEAD_SIZE), BF16),
             jax.ShapeDtypeStruct((rows, length, heads), F32),
         ],
         scratch_shapes=[pltpu.VMEM((heads, BQ, strip_width), F32)],
         compiler_params=pltpu.CompilerParams(vmem_limit_bytes=48 << 20),
         cost_estimate=pl.CostEstimate(
-            flops=work * 4 * HEAD_SIZE, transcendentals=work, bytes_accessed=q.size * 8
+            flops=work * 4 * HEAD_SIZE, transcendentals=work, bytes_accessed=qkv.size * 4
         ),
         name="self_attention",
-    )(q, k, v, segments[:, None, :], segments[:, :, None], base)
-
-
-def self_attention_back(q, k, v, cots, lse, segments, base):
-    rows, length, q_width = q.shape
+    )(qkv, segments[:, None, :], segments[:, :, None], base)
+
+
+def self_attention_back(qkv, cots, lse, segments, base):
+    rows, length, width = qkv.shape
     heads, strip_width = base.shape
-    k_width = k.shape[2]
-    queries, keys, sums, seg_row, seg_col, base_spec = self_specs(
-        length, q_width, k_width, heads, strip_width
-    )
+    all_spec, queries, sums, seg_row, seg_col, base_spec = self_specs(length, width, heads, strip_width)
+    k_width = (width - heads * HEAD_SIZE) // 2
     work = rows * heads * length * length * 3 // 8
     return pl.pallas_call(
         self_bwd_kernel,
         grid=(rows,),
-        in_specs=[queries, keys, keys, queries, sums, seg_row, seg_col, base_spec],
-        out_specs=[queries, keys, keys, base_spec],
+        in_specs=[all_spec, queries, sums, seg_row, seg_col, base_spec],
+        out_specs=[all_spec, base_spec],
         out_shape=[
-            jax.ShapeDtypeStruct(q.shape, BF16),
-            jax.ShapeDtypeStruct(k.shape, BF16),
-            jax.ShapeDtypeStruct(k.shape, BF16),
+            jax.ShapeDtypeStruct(qkv.shape, BF16),
             jax.ShapeDtypeStruct((heads, strip_width), F32),
         ],
         scratch_shapes=[
@@ -212,10 +212,10 @@
         ],
         compiler_params=pltpu.CompilerParams(vmem_limit_bytes=48 << 20),
         cost_estimate=pl.CostEstimate(
-            flops=work * 10 * HEAD_SIZE, transcendentals=work, bytes_accessed=q.size * 12
+            flops=work * 10 * HEAD_SIZE, transcendentals=work, bytes_accessed=qkv.size * 6
         ),
         name="self_attention_back",
-    )(q, k, v, cots, lse, segments[:, None, :], segments[:, :, None], base)
+    )(qkv, cots, lse, segments[:, None, :], segments[:, :, None], base)
 
 
 def cross_fwd_kernel(q_ref, k_ref, v_ref, seg_row_ref, seg_col_ref, o_ref, *lse_refs):
@@ -323,31 +323,125 @@
     return lax.axis_size(axis).bit_length() - 1
 
 
-def flip(value, axis, bit):
-    count = lax.axis_size(axis)
-    return lax.ppermute(value, axis, [(i, i ^ (1 << bit)) for i in range(count)])
-
-
-def scatter_order(first):
-    seq_bits = list(range(bit_count("seq")))
-    if first:
-        seq_bits.reverse()
-    return [("batch", 0)] + [("seq", b) for b in seq_bits] + [("batch", b) for b in range(1, bit_count("batch"))]
-
-
-def scatter_sum(full, turned):
-    batch_bits, seq_bits = bit_count("batch"), bit_count("seq")
-    left = [("batch", b) for b in reversed(range(batch_bits))] + [("seq", b) for b in reversed(range(seq_bits))]
-    own_rows = full.shape[0] >> len(left)
-    parts = [full.reshape((2,) * len(left) + (own_rows,) + full.shape[1:])]
-    for axis, bit in scatter_order(turned):
-        where = left.index((axis, bit))
-        mine = (lax.axis_index(axis) >> bit) & 1
-        away = sum(lax.dynamic_index_in_dim(p, 1 - mine, where, False).astype(F32) for p in parts)
-        came = flip(away.astype(BF16), axis, bit)
-        parts = [lax.dynamic_index_in_dim(p, mine, where, False) for p in parts] + [came]
-        left.pop(where)
-    return sum(p.astype(F32) for p in parts)
+def my_bit(axis, bit):
+    return (lax.axis_index(axis) >> bit) & 1
+
+
+def flip(value, axis, mask):
+    return lax.ppermute(value, axis, [(i, i ^ mask) for i in range(lax.axis_size(axis))])
+
+
+def gather_pieces(value, axis, order):
+    pieces = {0: value}
+    for bit in order:
+        for j in list(pieces):
+            pieces[j | (1 << bit)] = flip(pieces[j], axis, 1 << bit)
+    return [pieces[j] for j in range(len(pieces))]
+
+
+def gather_direct(value, axis):
+    return [value] + [flip(value, axis, j) for j in range(1, lax.axis_size(axis))]
+
+
+def absolute(values, axis):
+    place = lax.axis_index(axis)
+    values = jnp.stack(values) if isinstance(values, list) else values
+    return [lax.dynamic_index_in_dim(values, j ^ place, 0, False) for j in range(values.shape[0])]
+
+
+def settle(*groups):
+    flat, tree = jax.tree.flatten(groups)
+    return jax.tree.unflatten(tree, lax.optimization_barrier(flat))
+
+
+class Chain:
+    def __init__(self, full, bits, order):
+        shape = (2,) * len(bits) + (full.shape[0] >> len(bits),) + full.shape[1:]
+        self.parts, self.left, self.order, self.flying = [full.reshape(shape)], list(bits), list(order), None
+
+    def half(self, choice):
+        where = self.left.index(self.order[0])
+        return [lax.dynamic_index_in_dim(p, choice, where, False) for p in self.parts]
+
+    def outgoing(self):
+        return sum(p.astype(F32) for p in self.half(1 - my_bit(*self.order[0]))).astype(BF16)
+
+    def launch(self, away):
+        self.parts = self.half(my_bit(*self.order[0]))
+        axis, bit = self.order.pop(0)
+        self.left.remove((axis, bit))
+        self.flying = flip(away, axis, 1 << bit)
+
+    def land(self):
+        self.parts = self.parts + [self.flying]
+        self.flying = None
+
+    def result(self):
+        return sum(p.astype(F32) for p in self.parts)
+
+
+def joined(chains, order):
+    chain = Chain.__new__(Chain)
+    chain.left, chain.order, chain.flying = list(chains[0].left), list(order), None
+    chain.parts = [jnp.concatenate(parts, axis=-1) for parts in zip(*[c.parts for c in chains])]
+    return chain
+
+
+class Gather:
+    def __init__(self, value, order, lead=0):
+        self.held, self.order, self.lead, self.done, self.flying, self.last = value, list(order), lead, [], None, None
+
+    def outgoing(self):
+        return self.held
+
+    def launch(self, value):
+        self.held = value
+        self.last = self.order.pop(0)
+        self.flying = flip(value, self.last[0], 1 << self.last[1])
+
+    def land(self):
+        self.done = [bit for bit in place_bits() if bit in self.done or bit == self.last]
+        where = self.lead + self.done.index(self.last)
+        pair = jnp.arange(2).reshape((2,) + (1,) * (self.held.ndim - where))
+        own, came = jnp.expand_dims(self.held, where), jnp.expand_dims(self.flying, where)
+        self.held = jnp.where(pair == my_bit(*self.last), own, came)
+        self.flying = None
+
+
+def land(main, *chains):
+    arrive = [c for c in chains if c.flying is not None]
+    main, flown = settle(main, [c.flying for c in arrive])
+    for chain, value in zip(arrive, flown):
+        chain.flying = value
+        chain.land()
+    return main
+
+
+def tick(main, *chains):
+    main = land(main, *chains)
+    depart = [c for c in chains if c.order]
+    main, sends = settle(main, [c.outgoing() for c in depart])
+    for chain, value in zip(depart, sends):
+        chain.launch(value)
+    return main
+
+
+def place_bits():
+    return [("batch", b) for b in reversed(range(bit_count("batch")))] + [
+        ("seq", b) for b in reversed(range(bit_count("seq")))
+    ]
+
+
+def hops(seq_first, turned):
+    seq = [("seq", b) for b in range(bit_count("seq"))]
+    far = [("batch", b) for b in range(1, bit_count("batch"))]
+    if turned:
+        seq.reverse()
+    return [("batch", 0)] + (seq + far if seq_first else far + seq)
+
+
+def chain_of(full, seq_first=True, turned=False):
+    return Chain(full, place_bits(), hops(seq_first, turned))
 
 
 def small_sum(values):
@@ -403,23 +497,53 @@
             wkv[0, 1].reshape(own, seq_count, kv_local),
         ],
         axis=2,
-    ).reshape(own, -1)
+    )
+    cols = first.shape[2]
     bias_own = position_bias.shape[0]
     small = jnp.concatenate([gains.astype(BF16).reshape(-1), position_bias.astype(BF16)])
-    small = jnp.pad(small, (0, -small.shape[0] % 128))
-    small_rows = lax.all_gather(small, every, axis=0)
+    small = jnp.pad(small, (0, 8 * cols - small.shape[0])).reshape(1, 8, cols)
+    packet = jnp.concatenate([first.transpose(1, 0, 2), jnp.broadcast_to(small, (seq_count, 8, cols))], axis=1)
+    packet = lax.all_to_all(packet, "seq", 0, 0, tiled=True)
+    batch_far = [("batch", b) for b in reversed(range(1, bit_count("batch")))]
+    seq_up = [("seq", b) for b in range(bit_count("seq"))]
+    core = [("batch", 0)]
+    gather_p = Gather(packet, batch_far + core)
+    for _ in batch_far + core:
+        gather_p.launch(gather_p.held)
+        gather_p.land()
+    orders = [[b for _, b in (seq_up if r % 2 == 0 else seq_up[::-1])] for r in range(rows)]
+    first_hop = [flip(tokens[r], "seq", 1 << orders[r][0]) for r in range(rows)]
+    token_pieces = []
+    for r in range(rows):
+        pieces = {0: tokens[r], 1 << orders[r][0]: first_hop[r]}
+        for bit in orders[r][1:]:
+            for j in list(pieces):
+                pieces[j | (1 << bit)] = flip(pieces[j], "seq", 1 << bit)
+        token_pieces.append([pieces[j] for j in range(seq_count)])
+    ids = jnp.concatenate([segments, memory_segments], axis=1)
+    all_ids = jnp.stack(absolute(gather_direct(ids, "seq"), "seq"), axis=1)
+    all_segments = all_ids[:, :, :part].reshape(rows, length)
+    all_memory_segments = all_ids[:, :, part:].reshape(rows, -1)
+    packets = gather_p.held.reshape(-1, seq_count, own + 8, cols)
+    w_heads = packets[:, :, :own].reshape(width, cols)
+    small_rows = packets[:, :, own:].reshape(devices, -1)
     gain_values = (
         small_rows[:, : 3 * own].reshape(devices, 3, own).transpose(1, 0, 2).reshape(3, width).astype(F32)
     )
     table = small_rows[:, 3 * own : 3 * own + bias_own].reshape(NB, QUERY_HEADS).astype(F32)
-    w_first = lax.all_gather(first, every, axis=0, tiled=True)
-    middle = jnp.stack([jnp.concatenate([wkv[1, 0], wkv[1, 1]], axis=1), wo[0], wq[1], wo[1]])
-    w_middle = lax.all_gather(middle, every, axis=1, tiled=True)
-    w_kv1, w_o0, w_q1, w_o1 = w_middle[0], w_middle[1], w_middle[2], w_middle[3]
+
+    mid_a = jnp.stack([jnp.concatenate([wkv[1, 0], wkv[1, 1]], axis=1), wo[0]])
+    mid_b = jnp.stack([wq[1], wo[1]])
+    _, _, mid_a, mid_b = settle(packet, first_hop, mid_a, mid_b)
+    gather_a = Gather(mid_a, batch_far + seq_up + core, 1)
+    gather_b = Gather(mid_b, batch_far + seq_up[::-1] + core, 1)
+    gather_r = Gather(wr, seq_up + batch_far + core)
+    for _ in batch_far:
+        for gather in (gather_a, gather_b):
+            if gather.flying is not None:
+                gather.land()
+            gather.launch(gather.held)
     w_exp = lax.all_gather(jnp.concatenate([we[0], we[1]], axis=1), every, axis=0, tiled=True)
-    w_red = lax.all_gather(wr, every, axis=0, tiled=True)
-    all_segments = lax.all_gather(segments, "seq", axis=1, tiled=True)
-    all_memory_segments = lax.all_gather(memory_segments, "seq", axis=1, tiled=True)
 
     reach = length // 2
     strip_width = 2 * reach + BQ
@@ -431,72 +555,114 @@
     base = jnp.dot(table_local.T, picks, precision=lax.Precision.HIGHEST)
     base = jnp.where(lag_ok[None, :], base, NEGATIVE)
 
+    token_pieces = tick(token_pieces, gather_a, gather_b, gather_r)
+    all_tokens = jnp.stack([jnp.stack(p) for p in token_pieces], axis=1).astype(F32)
+    all_normed = (all_tokens * inverse_rms(all_tokens) * gain_values[0]).astype(BF16).reshape(-1, width)
+    head_qkv = nn(all_normed, w_heads).astype(BF16).reshape(seq_count, rows, part, cols)
+    head_qkv = jnp.stack(absolute(head_qkv, "seq"), axis=1).reshape(rows, length, cols)
+    head_qkv = tick(head_qkv, gather_a, gather_b)
+    head_context, lse = self_attention(head_qkv, all_segments, base)
+    while gather_r.order[0][0] == "seq":
+        head_context = tick(head_context, gather_r)
+    head_context = tick(head_context, gather_r)
+    context = lax.all_to_all(head_context, "seq", split_axis=1, concat_axis=2, tiled=True).reshape(-1, width)
+    while gather_a.order:
+        context = tick(context, gather_a, gather_b)
+    context = land(context, gather_a, gather_b)
+    w_mid_a, w_mid_b = gather_a.held.reshape(2, width, width), gather_b.held.reshape(2, width, width)
+    w_kv1, w_o0, w_q1, w_o1 = w_mid_a[0], w_mid_a[1], w_mid_b[0], w_mid_b[1]
+
+    mem = memory.reshape(rows * memory_part, width)
+    mkv = nn(mem, w_kv1).astype(BF16).reshape(rows, memory_part, -1)
+    all_mkv = jnp.stack(absolute(gather_direct(mkv, "seq"), "seq"), axis=1).reshape(rows, -1, 2 * kv_width)
+    mk, mv = all_mkv[:, :, :kv_width], all_mkv[:, :, kv_width:]
     x = tokens.astype(F32).reshape(rows * part, width)
     inv_zero = inverse_rms(x)
-    normed = (x * inv_zero * gain_values[0]).astype(BF16)
-    qkv = nn(normed, w_first).astype(BF16).reshape(rows, part, -1)
-    head_qkv = lax.all_to_all(qkv, "seq", split_axis=2, concat_axis=1, tiled=True)
-    hq = head_qkv[:, :, :q_local]
-    hk = head_qkv[:, :, q_local : q_local + kv_local]
-    hv = head_qkv[:, :, q_local + kv_local :]
-    head_context, lse = self_attention(hq, hk, hv, all_segments, base)
-    context = lax.all_to_all(head_context, "seq", split_axis=1, concat_axis=2, tiled=True).reshape(-1, width)
-
-    mem = memory.reshape(rows * memory_part, width)
-    mkv = nn(mem, w_kv1).astype(BF16).reshape(rows, memory_part, -1)
-    all_mkv = lax.all_gather(mkv, "seq", axis=1, tiled=True)
-    mk, mv = all_mkv[:, :, :kv_width], all_mkv[:, :, kv_width:]
     hidden_one = x + nn(context, w_o0)
     inv_one = inverse_rms(hidden_one)
     normed_one = (hidden_one * inv_one * gain_values[1]).astype(BF16)
     cross_q = nn(normed_one, w_q1).astype(BF16).reshape(rows, part, width)
+    while len(gather_r.order) > 1:
+        cross_q = tick(cross_q, gather_r)
     cross_context = cross_attention(cross_q, mk, mv, segments, all_memory_segments)
+    cross_context, first = settle(cross_context, first)
+    w_first = lax.all_gather(first.reshape(own, -1), every, axis=0, tiled=True)
     cross_flat = cross_context.reshape(-1, width)
     hidden_two = hidden_one + nn(cross_flat, w_o1)
     inv_two = inverse_rms(hidden_two)
     normed_two = (hidden_two * inv_two * gain_values[2]).astype(BF16)
 
     ff = we.shape[2]
+    normed_two = tick(normed_two, gather_r)
     gate = nn(normed_two, w_exp[:, :ff])
     up = nn(normed_two, w_exp[:, ff:])
     gelu_value, gelu_slope = gelu_parts(gate)
     activated = (gelu_value * up).astype(BF16)
     og = output_grad.reshape(rows * part, width)
+    activated = land(activated, gather_r)
+    w_red = gather_r.held.reshape(-1, width)
+    wide_og = jnp.pad(og, ((0, 0), (0, -width % 384)))
+    reduce_part = tn(activated, wide_og).astype(BF16)
+    activated, reduce_part = settle(activated, reduce_part)
+    (grad_reduce,) = settle(lax.psum_scatter(reduce_part, every, scatter_dimension=0, tiled=True))
+    grad_reduce = grad_reduce[:, :width].astype(F32)
     result = (hidden_two + nn(activated, w_red)).astype(BF16).reshape(tokens.shape)
-    grad_reduce = scatter_sum(tn(activated, og).astype(BF16), False)
     activated_grad = nt(og, w_red)
     gate_grad = (activated_grad * up * gelu_slope).astype(BF16)
     up_grad = (activated_grad * gelu_value).astype(BF16)
-    grad_gate = scatter_sum(tn(normed_two, gate_grad).astype(BF16), False)
-    grad_up = scatter_sum(tn(normed_two, up_grad).astype(BF16), True)
+    gate_grad, up_grad, result = settle(gate_grad, up_grad, result)
+    chain_g = chain_of(tn(normed_two, gate_grad).astype(BF16))
+    chain_u = chain_of(tn(normed_two, up_grad).astype(BF16), turned=True)
+    gate_grad, up_grad = tick((gate_grad, up_grad), chain_g, chain_u)
     normed_two_grad = nt(gate_grad, w_exp[:, :ff]) + nt(up_grad, w_exp[:, ff:])
     part_two, gain_two = norm_back(hidden_two, inv_two, gain_values[2], normed_two_grad)
     hidden_two_grad = og.astype(F32) + part_two
+    hidden_two_grad = tick(hidden_two_grad, chain_g, chain_u)
 
     cross_out_grad = hidden_two_grad.astype(BF16)
-    grad_o1 = scatter_sum(tn(cross_flat, cross_out_grad).astype(BF16), True)
     cross_cots = nt(cross_out_grad, w_o1).astype(BF16).reshape(rows, part, width)
     cross_dq, mdk, mdv = cross_attention_back(cross_q, mk, mv, cross_cots, segments, all_memory_segments)
     mdkv = jnp.concatenate([mdk, mdv], axis=2).reshape(rows, seq_count, memory_part, -1)
     mdkv = lax.all_to_all(mdkv, "seq", split_axis=1, concat_axis=1, tiled=True)
+    cross_dq = cross_dq.reshape(-1, width)
+    part_one, gain_one = norm_back(hidden_one, inv_one, gain_values[1], nt(cross_dq, w_q1))
+    hidden_one_grad = hidden_two_grad + part_one
+
+    self_out_grad = hidden_one_grad.astype(BF16)
+    cots = nt(self_out_grad, w_o0).astype(BF16).reshape(rows, part, width)
+    chain_o1 = chain_of(tn(cross_flat, cross_out_grad).astype(BF16))
+    chain_q1 = chain_of(tn(normed_one, cross_dq).astype(BF16))
+    chain_a = joined([chain_o1, chain_q1], chain_o1.order)
+    chain_o0 = chain_of(tn(context, self_out_grad).astype(BF16), turned=True)
+    cots = tick(cots, chain_g, chain_u, chain_a, chain_o0)
+    head_cots = lax.all_to_all(cots, "seq", split_axis=2, concat_axis=1, tiled=True)
+    head_cots, mdkv = settle(head_cots, mdkv)
     mdkv = jnp.sum(mdkv.astype(F32), axis=1).astype(BF16).reshape(rows * memory_part, -1)
     memory_grad = nt(mdkv, w_kv1).reshape(memory.shape)
-    grad_kv1 = scatter_sum(tn(mem, mdkv).astype(BF16), False)
-    cross_dq = cross_dq.reshape(-1, width)
-    grad_q1 = scatter_sum(tn(normed_one, cross_dq).astype(BF16), True)
-    part_one, gain_one = norm_back(hidden_one, inv_one, gain_values[1], nt(cross_dq, w_q1))
-    hidden_one_grad = hidden_two_grad + part_one
-
-    self_out_grad = hidden_one_grad.astype(BF16)
-    grad_o0 = scatter_sum(tn(context, self_out_grad).astype(BF16), False)
-    cots = nt(self_out_grad, w_o0).astype(BF16).reshape(rows, part, width)
-    head_cots = lax.all_to_all(cots, "seq", split_axis=2, concat_axis=1, tiled=True)
-    hdq, hdk, hdv, lag_sums = self_attention_back(hq, hk, hv, head_cots, lse, all_segments, base)
-    head_grads = jnp.concatenate([hdq, hdk, hdv], axis=2)
+    chain_k1 = chain_of(tn(mem, mdkv).astype(BF16), turned=True)
+    head_cots, memory_grad = tick((head_cots, memory_grad), chain_a, chain_o0, chain_k1)
+    head_grads, lag_sums = self_attention_back(head_qkv, head_cots, lse, all_segments, base)
+    relative = jnp.stack(absolute(head_grads.reshape(rows, seq_count, part, cols).swapaxes(0, 1), "seq"))
+    batch_bits = [("batch", b) for b in reversed(range(bit_count("batch")))]
+    chain_f = Chain(tn(all_normed, relative.reshape(-1, cols)).astype(BF16), batch_bits, hops(False, False)[: len(batch_bits)])
+    head_grads = land(head_grads, chain_g, chain_u)
+    while chain_g.order[0][0] == "seq":
+        head_grads = land(tick(head_grads, chain_g, chain_u), chain_g, chain_u)
+    chain_gu = joined([chain_g, chain_u], chain_g.order)
+    chains = (chain_f, chain_gu, chain_a, chain_o0, chain_k1)
+    head_grads, lag_sums = tick((head_grads, lag_sums), *chains)
     dqkv = lax.all_to_all(head_grads, "seq", split_axis=1, concat_axis=2, tiled=True).reshape(rows * part, -1)
-    grad_first = scatter_sum(tn(normed, dqkv).astype(BF16), False)
+    dqkv = tick(dqkv, chain_f)
     part_zero, gain_zero = norm_back(x, inv_zero, gain_values[0], nt(dqkv, w_first))
     input_grad = (hidden_one_grad + part_zero).reshape(tokens.shape)
+    while any(c.order or c.flying is not None for c in chains):
+        input_grad = tick(input_grad, *chains)
+    grad_gu, grad_a = chain_gu.result(), chain_a.result()
+    grad_o0, grad_k1 = chain_o0.result(), chain_k1.result()
+    grad_gate, grad_up = grad_gu[:, :ff], grad_gu[:, ff:]
+    grad_o1, grad_q1 = grad_a[:, :width], grad_a[:, width:]
+    first_grads = lax.all_to_all(chain_f.result().reshape(seq_count, own, cols), "seq", 0, 0, tiled=True)
+    first_grads = first_grads.transpose(1, 0, 2)
 
     table_part = jnp.dot(picks, lag_sums.T, precision=lax.Precision.HIGHEST)
     table_grad = lax.dynamic_update_slice(
@@ -508,7 +674,6 @@
     shard_gains = small_grads[: 3 * own].reshape(3, own)
     shard_table = small_grads[3 * own :]
 
-    first_grads = grad_first.reshape(own, seq_count, -1)
     shard_query = jnp.stack([first_grads[:, :, :q_local].reshape(own, width), grad_q1])
     shard_keyval = jnp.stack(
         [
@@ -518,7 +683,7 @@
                     first_grads[:, :, q_local + kv_local :].reshape(own, kv_width),
                 ]
             ),
-            jnp.stack([grad_kv1[:, :kv_width], grad_kv1[:, kv_width:]]),
+            jnp.stack([grad_k1[:, :kv_width], grad_k1[:, kv_width:]]),
         ]
     )
     gradients = (

time: 793 us -> 650 us (0.82)
  blocking collectives: 107 us -> 30.1 us
  waiting for transfers between devices: 265 us -> 196 us
  other arithmetic: 78.1 us -> 103 us
  matrix products: 102 us -> 83.8 us
  local copies, waits for them, and re-layouts: 79 us -> 67 us
    all_gather x3 -> x0, blocking collectives: 107 us -> none  [the longest x1 65.7 us: shards(): small_rows = lax.all_gather(small, every, axis=0)]
    all_gather x4 -> x1, waiting for transfers between devices: 78.9 us -> 0.02 us  [shards(): w_first = lax.all_gather(first.reshape(own, -1), every, axis=0, tiled=True)]
    all_gather x1, waiting for transfers between devices: 61.2 us -> 0.01 us  [shards(): lax.all_gather(jnp.concatenate([we[0], we[1]], axis=1), every, axis=0, ti...]
    ppermute x40 -> x56, waiting for transfers between devices: 125 us -> 156 us  [flip(): lax.ppermute(value, axis, [(i, i ^ mask) for i in range(lax.axis_size(axi...]
    all_to_all x0 -> x1, blocking collectives: none -> 30.1 us  [shards(): lax.all_to_all(head_context, 'seq', split_axis=1, concat_axis=2, tiled=True)]
    select_n x0 -> x16, other arithmetic: none -> 28.2 us  [land(): self.held = jnp.where(pair == my_bit(*self.last), own, came)]
    all_to_all x1, waiting for transfers between devices: 0.01 us -> 12.8 us  [shards(): lax.all_to_all(head_grads, 'seq', split_axis=1, concat_axis=2, tiled=True)]
    all_to_all x1, waiting for transfers between devices: 0.01 us -> 12.7 us  [shards(): lax.all_to_all(cots, 'seq', split_axis=2, concat_axis=1, tiled=True)]
  transfers between devices with their start and end apart: 51 -> 65, of which waited for: 23 -> 23; matrix products, arithmetic and copies ran while one was open for 23% -> 34% of each run, Pallas kernels for 7% -> 11%
where the time goes in v2:
time: 650 us; the launch traced here: 641 us
  waiting for transfers between devices  196 us (30%)
  other arithmetic  103 us (16%)
  matrix products  83.8 us (13%)
  starting transfers between devices  74.5 us (11%)
  Pallas kernels  71 us (11%)
  local copies, waits for them, and re-layouts  67 us (10%)
  blocking collectives  30.1 us (5%)
  between operations  16.9 us (3%)
    ppermute x56, waiting for transfers between devices, flip(): lax.ppermute(value, axis, [(i, i ^ mask) for i in range(lax.axis_size(axi...  156 us
    ppermute x56, starting transfers between devices, flip(): lax.ppermute(value, axis, [(i, i ^ mask) for i in range(lax.axis_size(axi...  48.1 us
    dot_general x8, matrix products, nt(): lax.dot_general(a, b, (((1,), (1,)), ((), ())), preferred_element_type=F32)  34.4 us
    convert_element_type x19, other arithmetic, outgoing(): sum((p.astype(F32) for p in self.half(1 - my_bit(*self.order[0]))))  33.4 us
    all_to_all x1, blocking collectives, shards(): lax.all_to_all(head_context, 'seq', split_axis=1, concat_axis=2, tiled=True)  30.1 us
    dot_general x8, matrix products, nn(): lax.dot_general(a, b, (((1,), (0,)), ((), ())), preferred_element_type=F32)  28.9 us
    select_n x16, other arithmetic, land(): self.held = jnp.where(pair == my_bit(*self.last), own, came)  28.2 us
    pallas_call x1, Pallas kernels, self_attention_back(): pl.pallas_call(self_bwd_kernel, grid=(rows,), in_specs=[all_spec, queries...  26.3 us
  transfers between devices with their start and end apart: 65, of which 23 were waited for; matrix products, arithmetic and copies ran while one was open for 34% of the time, Pallas kernels for 11%

profile of v2, /device:TPU:0, one launch (start us, length us, event | category | flops | bytes accessed | tf_op | source)
XLA Modules:
  0.0 641.4 jit_solution(3609023830044646807)
XLA Ops:
  42.6 7.1 %collective-permute-done.10 = bf16[4,40,512]{2,1,0:T(8,128)(2,1)S(1)} collective-permute-done((bf16[4,40,512]{2,1,0:T(8,128)(2,1)S(1)}, bf16[4,40,512]{2,1,0:T(8,128)(2,1)S(1)}, u32[]{:S(2)}, u32[]{:S(2)}) %collective-permute-start.10) | collective-permute-done | bytes 163872 | tf_op jit(solution)/shard_map/ppermute | solution.py:331
  58.6 17.3 %collective-permute-done.11 = bf16[2,4,40,512]{3,2,1,0:T(8,128)(2,1)S(1)} collective-permute-done((bf16[2,4,40,512]{3,2,1,0:T(8,128)(2,1)S(1)}, bf16[2,4,40,512]{3,2,1,0:T(8,128)(2,1)S(1)}, u32[]{:S(2)}, u32[]{:S(2)}) %collective-permute-start.11) | collective-permute-done | bytes 327712 | tf_op jit(solution)/shard_map/ppermute | solution.py:331
  82.9 7.6 %collective-permute-done.9 = bf16[2,2,32,1024]{3,2,1,0:T(8,128)(2,1)S(1)} collective-permute-done((bf16[2,2,32,1024]{3,2,1,0:T(8,128)(2,1)S(1)}, bf16[2,2,32,1024]{3,2,1,0:T(8,128)(2,1)S(1)}, u32[]{:S(2)}, u32[]{:S(2)}) %collective-permute-start.9) | collective-permute-done | bytes 262176 | tf_op jit(solution)/shard_map/ppermute | solution.py:331
  106.7 11.3 %collective-permute-done.13 = bf16[2,2,2,32,1024]{4,3,2,1,0:T(8,128)(2,1)} collective-permute-done((bf16[2,2,2,32,1024]{4,3,2,1,0:T(8,128)(2,1)}, bf16[2,2,2,32,1024]{4,3,2,1,0:T(8,128)(2,1)}, u32[]{:S(2)}, u32[]{:S(2)}) %collective-permute-start.13) | collective-permute-done | bytes 524320 | tf_op jit(solution)/shard_map/ppermute | solution.py:331
  120.7 18.4 %self_attention.1 = (bf16[2,1024,256]{2,1,0:T(8,128)(2,1)S(1)}, f32[2,1024,4]{2,1,0:T(8,128)S(1)}) custom-call(bf16[2,1024,512]{2,1,0:T(8,128)(2,1)S(1)} %bitcast.527, s32[2,1,1024]{2,1,0:T(1,128)S(1)} %broadcast_in_dim_reshape.12.seg_row_ref, s32[2,1024,1]{2,1,0:T(8,128)S(1)} %broadcast_in_dim_reshape.15.seg_col_ref, ...), custom_call_target="tpu_custom_call" | custom-call | flops 805306368 | bytes 4194304 | tf_op jit(solution)/shard_map/self_attention/pallas_call | solution.py:174
  144.2 7.8 %collective-permute-done.19 = bf16[2,88,1024]{2,1,0:T(8,128)(2,1)S(1)} collective-permute-done((bf16[2,88,1024]{2,1,0:T(8,128)(2,1)S(1)}, bf16[2,88,1024]{2,1,0:T(8,128)(2,1)S(1)}, u32[]{:S(2)}, u32[]{:S(2)}) %collective-permute-start.19) | collective-permute-done | bytes 360480 | tf_op jit(solution)/shard_map/ppermute | solution.py:331
  153.2 30.1 %all_to_all.72 = bf16[2,1024,256]{2,0,1:T(2,128)(2,1)S(1)} all-to-all(bf16[2,1024,256]{2,0,1:T(2,128)(2,1)S(1)} %copy.170), channel_id=1, replica_groups=mesh['batch'=8,'seq'=4] {'seq'}, dimensions={1} | all-to-all | bytes 2097152 | tf_op jit(solution)/shard_map/all_to_all | solution.py:568
  209.1 14.5 %collective-permute-done.24 = bf16[2,2,88,1024]{3,2,1,0:T(8,128)(2,1)S(1)} collective-permute-done((bf16[2,2,88,1024]{3,2,1,0:T(8,128)(2,1)S(1)}, bf16[2,2,88,1024]{3,2,1,0:T(8,128)(2,1)S(1)}, u32[]{:S(2)}, u32[]{:S(2)}) %collective-permute-start.24) | collective-permute-done | bytes 720928 | tf_op jit(solution)/shard_map/ppermute | solution.py:331
  224.4 11.2 %cross_attention.1 = bf16[2,256,1024]{2,1,0:T(8,128)(2,1)S(1)} custom-call(bf16[2,256,1024]{2,1,0:T(8,128)(2,1)S(1)} %bitcast.530, bf16[2,256,512]{2,1,0:T(8,128)(2,1)S(1)} %get-tuple-element.465.k_ref, bf16[2,256,512]{2,1,0:T(8,128)(2,1)S(1)} %get-tuple-element.464.v_ref, s32[2,1,256]{2,1,0:T(1,128)S(1)} %broadcast_in_dim_reshape.14.seg_row_ref, ...), custom_call_target="tpu_custom_call" | custom-call | flops 536870912 | bytes 3145728 | tf_op jit(solution)/shard_map/cross_attention/pallas_call | solution.py:287
  237.8 19.5 %collective-permute-done.28 = bf16[2,2,2,88,1024]{4,3,2,1,0:T(8,128)(2,1)S(1)} collective-permute-done((bf16[2,2,2,88,1024]{4,3,2,1,0:T(8,128)(2,1)S(1)}, bf16[2,2,2,88,1024]{4,3,2,1,0:T(8,128)(2,1)S(1)}, u32[]{:S(2)}, u32[]{:S(2)}) %collective-permute-start.28) | collective-permute-done | bytes 1441824 | tf_op jit(solution)/shard_map/ppermute | solution.py:331
  265.4 9.0 %multiply_convert_fusion = (bf16[512,2816]{1,0:T(8,128)(2,1)S(1)}, f32[512,2816]{1,0:T(8,128)}) fusion(f32[512,2816]{1,0:T(8,128)S(1)} %fusion.20, bf16[512,1024]{1,0:T(8,128)(2,1)} %copy-done.80, bf16[1024,5632]{1,0:T(8,128)(2,1)S(1)} %copy-done.142), kind=kOutput, calls=%fused_computation.35 | convolution fusion | flops 2967207936 | bytes 21233664 | tf_op jit(solution)/shard_map/dot_general | solution.py:28
  288.1 6.1 broadcast_select_fusion
  294.2 7.2 %add_convert_fusion = bf16[512,1024]{1,0:T(8,128)(2,1)} fusion(f32[512,1024]{1,0:T(8,128)S(1)} %copy-done.36, bf16[512,2816]{1,0:T(8,128)(2,1)S(1)} %copy-done.148, bf16[2816,1024]{1,0:T(8,128)(2,1)} %bitcast_select_fusion), kind=kOutput, calls=%fused_computation.95 | convolution fusion | flops 2953838592 | bytes 11796480 | tf_op jit(solution)/shard_map/dot_general | solution.py:28
  301.3 10.0 %fusion.13 = (bf16[512,2816]{1,0:T(8,128)(2,1)S(1)}, bf16[512,2816]{1,0:T(8,128)(2,1)S(1)}) fusion(f32[512,2816]{1,0:T(8,128)} %copy-done.143, f32[512,2816]{1,0:T(8,128)} %get-tuple-element.509, bf16[2816,1024]{1,0:T(8,128)(2,1)S(1)} %bitcast.566, bf16[512,1024]{1,0:T(8,128)(2,1)S(1)} %bitcast.591), kind=kOutput, calls=%fused_computation.34 | convolution fusion | flops 2984509440 | bytes 24117248 | tf_op jit(solution)/shard_map/dot_general | solution.py:24
  327.8 6.2 fusion.14
  349.6 15.2 %cross_attention_back.1 = (bf16[2,256,1024]{2,1,0:T(8,128)(2,1)S(1)}, bf16[2,256,512]{2,1,0:T(8,128)(2,1)S(1)}, bf16[2,256,512]{2,1,0:T(8,128)(2,1)S(1)}) custom-call(bf16[2,256,1024]{2,1,0:T(8,128)(2,1)S(1)} %bitcast.531, bf16[2,256,512]{2,1,0:T(8,128)(2,1)S(1)} %get-tuple-element.465.k_ref, bf16[2,256,512]{2,1,0:T(8,128)(2,1)S(1)} %get-tuple-element.464.v_ref, ...), custom_call_target="tpu_custom_call" | custom-call | flops 1342177280 | bytes 5242880 | tf_op jit(solution)/shard_map/cross_attention_back/pallas_call | solution.py:304
  380.4 21.7 %collective-permute-done.32 = bf16[2,2,2,32,2816]{4,3,1,0,2:T(8,128)(2,1)S(1)} collective-permute-done((bf16[2,2,2,32,2816]{4,3,1,0,2:T(8,128)(2,1)}, bf16[2,2,2,32,2816]{4,3,1,0,2:T(8,128)(2,1)S(1)}, u32[]{:S(2)}, u32[]{:S(2)}) %collective-permute-start.32) | collective-permute-done | bytes 1441824 | tf_op jit(solution)/shard_map/ppermute | solution.py:331
  419.4 12.7 %all-to-all-done.2 = bf16[2,256,1024]{1,0,2:T(2,128)(2,1)} async-done(((bf16[2,256,1024]{1,0,2:T(2,128)(2,1)}), bf16[2,256,1024]{1,0,2:T(2,128)(2,1)}, u32[]{:S(2)}, u32[]{:S(2)}) %all-to-all-start.2) | async-done | bytes 1048608 | tf_op jit(solution)/shard_map/all_to_all | solution.py:638
  447.6 11.4 %all-to-all-done.3 = bf16[2,4,64,1024]{3,2,0,1:T(8,128)(2,1)} async-done(((bf16[2,4,64,1024]{3,2,0,1:T(8,128)(2,1)}), bf16[2,4,64,1024]{3,2,0,1:T(8,128)(2,1)}, u32[]{:S(2)}, u32[]{:S(2)}) %all-to-all-start.3) | async-done | bytes 1048608 | tf_op jit(solution)/shard_map/all_to_all | solution.py:626
  469.0 26.3 %self_attention_back.1 = (bf16[2,1024,512]{2,1,0:T(8,128)(2,1)S(1)}, f32[4,1152]{1,0:T(4,128)S(1)}) custom-call(bf16[2,1024,512]{2,1,0:T(8,128)(2,1)} %bitcast.528, bf16[2,1024,256]{2,1,0:T(8,128)(2,1)S(1)} %bitcast.529, f32[2,1024,4]{2,1,0:T(8,128)S(1)} %copy-done.13, s32[2,1,1024]{2,1,0:T(1,128)S(1)} %copy-done.5, ...), custom_call_target="tpu_custom_call" | custom-call | flops 2013265920 | bytes 6291456 | tf_op jit(solution)/shard_map/self_attention_back/pallas_call | solution.py:198
  506.4 6.8 %collective-permute-done.38 = bf16[2,2,2,32,2048]{4,3,2,1,0:T(8,128)(2,1)S(1)} collective-permute-done((bf16[2,2,2,32,2048]{4,3,2,1,0:T(8,128)(2,1)}, bf16[2,2,2,32,2048]{4,3,2,1,0:T(8,128)(2,1)S(1)}, u32[]{:S(2)}, u32[]{:S(2)}) %collective-permute-start.38) | collective-permute-done | bytes 1048608 | tf_op jit(solution)/shard_map/ppermute | solution.py:331
  534.7 12.8 %all-to-all-done.4 = bf16[2,1024,512]{2,0,1:T(2,128)(2,1)} async-done(((bf16[2,1024,512]{2,0,1:T(2,128)(2,1)}), bf16[2,1024,512]{2,0,1:T(2,128)(2,1)}, u32[]{:S(2)}, u32[]{:S(2)}) %all-to-all-start.4) | async-done | bytes 2097184 | tf_op jit(solution)/shard_map/all_to_all | solution.py:654
  553.9 6.8 %fusion.41 = (f32[1024]{0:T(1024)S(1)}, f32[512]{0:T(512)S(1)}, f32[512,1024]{1,0:T(8,128)}) fusion(bf16[2,256,1024]{2,1,0:T(8,128)(2,1)S(1)} %copy-done.33, f32[512]{0:T(512)S(1)} %bitcast.618, f32[1024]{0:T(1024)S(1)} %copy-done.112, bf16[512,2048]{1,0:T(8,128)(2,1)} %bitcast.580, bf16[1024,2048]{1,0:T(8,128)(2,1)} %all-gather.5.cloned.1.call-done), kind=kOutput, calls=%fused_computation.88 | convolution fusion | flops 2151152128 | bytes 9449472 | tf_op jit(solution)/shard_map/dot_general | solution.py:24
  589.5 17.1 %collective-permute-done.47 = bf16[128,512]{1,0:T(8,128)(2,1)S(1)} collective-permute-done((bf16[128,512]{1,0:T(8,128)(2,1)S(1)}, bf16[128,512]{1,0:T(8,128)(2,1)S(1)}, u32[]{:S(2)}, u32[]{:S(2)}) %collective-permute-start.47) | collective-permute-done | bytes 131104 | tf_op jit(solution)/shard_map/ppermute | solution.py:331
  (643 shorter events, 310.2 us)
Async XLA Ops:
  7.3 252.1 %all-gather.3.cloned.1.call-start = ((), (), s32[]{:S(2)}) async-start(), calls=%async_computation.8 | async-start | bytes 11894784 | tf_op jit(solution)/shard_map/all_gather | solution.py:546
  20.2 511.0 %reduce-scatter.4.cloned.1.call-start = ((), (), s32[]{:S(2)}) async-start(), calls=%async_computation.10 | async-start | bytes 6690816
  34.8 44.0 %collective-permute-start.3 = (bf16[256,1024]{1,0:T(8,128)(2,1)S(1)}, bf16[256,1024]{1,0:T(8,128)(2,1)}, u32[]{:S(2)}, u32[]{:S(2)}) collective-permute-start(bf16[256,1024]{1,0:T(8,128)(2,1)S(1)} %get-tuple-element.190), channel_id=1, source_target_pairs={{0,1},{1,0},{2,3},{3,2},{4,5},{5,4},{6,7},{7,6},{8,9},{9,8},{10,11... | collective-permute-start | bytes 1572872 | tf_op jit(solution)/shard_map/ppermute | solution.py:331
  52.6 37.9 %collective-permute-start.2 = (bf16[256,1024]{1,0:T(8,128)(2,1)}, bf16[256,1024]{1,0:T(8,128)(2,1)}, u32[]{:S(2)}, u32[]{:S(2)}) collective-permute-start(bf16[256,1024]{1,0:T(8,128)(2,1)} %collective-permute-done), channel_id=1, source_target_pairs={{0,2},{1,3},{2,0},{3,1},{4,6},{5,7},{6,4},{7,5},{8,10},{9,11},{10,... | collective-permute-start | bytes 1572872 | tf_op jit(solution)/shard_map/ppermute | solution.py:331
  58.1 32.4 %collective-permute-start.5 = (bf16[256,1024]{1,0:T(8,128)(2,1)}, bf16[256,1024]{1,0:T(8,128)(2,1)}, u32[]{:S(2)}, u32[]{:S(2)}) collective-permute-start(bf16[256,1024]{1,0:T(8,128)(2,1)} %collective-permute-done.4), channel_id=1, source_target_pairs={{0,1},{1,0},{2,3},{3,2},{4,5},{5,4},{6,7},{7,6},{8,9},{9,8},{10,11... | collective-permute-start | bytes 1572872 | tf_op jit(solution)/shard_map/ppermute | solution.py:331
  91.6 26.3 %collective-permute-start.13 = (bf16[2,2,2,32,1024]{4,3,2,1,0:T(8,128)(2,1)}, bf16[2,2,2,32,1024]{4,3,2,1,0:T(8,128)(2,1)}, u32[]{:S(2)}, u32[]{:S(2)}) collective-permute-start(bf16[2,2,2,32,1024]{4,3,2,1,0:T(8,128)(2,1)} %get-tuple-element.194), channel_id=1, source_target_pairs={{0,1},{1,0},{2,3},{3,2},{4,5},{5,4},{6,7},{7,6},{8,9},{9,8},{10,11... | collective-permute-start | bytes 1572872 | tf_op jit(solution)/shard_map/ppermute | solution.py:331
  91.6 26.3 %collective-permute-start.14 = (bf16[2,2,2,32,1024]{4,3,2,1,0:T(8,128)(2,1)}, bf16[2,2,2,32,1024]{4,3,2,1,0:T(8,128)(2,1)}, u32[]{:S(2)}, u32[]{:S(2)}) collective-permute-start(bf16[2,2,2,32,1024]{4,3,2,1,0:T(8,128)(2,1)} %get-tuple-element.195), channel_id=1, source_target_pairs={{0,2},{1,3},{2,0},{3,1},{4,6},{5,7},{6,4},{7,5},{8,10},{9,11},{10,... | collective-permute-start | bytes 1572872 | tf_op jit(solution)/shard_map/ppermute | solution.py:331
  91.6 47.4 %collective-permute-start.18 = (bf16[88,1024]{1,0:T(8,128)(2,1)}, bf16[88,1024]{1,0:T(8,128)(2,1)}, u32[]{:S(2)}, u32[]{:S(2)}) collective-permute-start(bf16[88,1024]{1,0:T(8,128)(2,1)} %convert_element_type.742), channel_id=1, source_target_pairs={{0,1},{1,0},{2,3},{3,2},{4,5},{5,4},{6,7},{7,6},{8,9},{9,8},{10,11... | collective-permute-start | bytes 540680 | tf_op jit(solution)/shard_map/ppermute | solution.py:331
  140.7 44.7 %collective-permute-start.20 = (bf16[2,2,2,2,32,1024]{5,4,3,2,1,0:T(8,128)(2,1)S(1)}, bf16[2,2,2,2,32,1024]{5,4,3,2,1,0:T(8,128)(2,1)S(1)}, u32[]{:S(2)}, u32[]{:S(2)}) collective-permute-start(bf16[2,2,2,2,32,1024]{5,4,3,2,1,0:T(8,128)(2,1)S(1)} %broadcast_select_fusion.8), channel_id=1, source_target_pairs={{0,2},{1,3},{2,0},{3,1},{4,6},{5,7},{6,4},{7,5},{8,10},{9,11},{10,... | collective-permute-start | bytes 3145736 | tf_op jit(solution)/shard_map/ppermute | solution.py:331
  142.7 42.7 %collective-permute-start.21 = (bf16[2,2,2,2,32,1024]{5,4,3,2,1,0:T(8,128)(2,1)S(1)}, bf16[2,2,2,2,32,1024]{5,4,3,2,1,0:T(8,128)(2,1)S(1)}, u32[]{:S(2)}, u32[]{:S(2)}) collective-permute-start(bf16[2,2,2,2,32,1024]{5,4,3,2,1,0:T(8,128)(2,1)S(1)} %broadcast_select_fusion.7), channel_id=1, source_target_pairs={{0,1},{1,0},{2,3},{3,2},{4,5},{5,4},{6,7},{7,6},{8,9},{9,8},{10,11... | collective-permute-start | bytes 3145736 | tf_op jit(solution)/shard_map/ppermute | solution.py:331
  189.5 34.1 %collective-permute-start.24 = (bf16[2,2,88,1024]{3,2,1,0:T(8,128)(2,1)S(1)}, bf16[2,2,88,1024]{3,2,1,0:T(8,128)(2,1)S(1)}, u32[]{:S(2)}, u32[]{:S(2)}) collective-permute-start(bf16[2,2,88,1024]{3,2,1,0:T(8,128)(2,1)S(1)} %broadcast_select_fusion.9), channel_id=1, source_target_pairs={{0,16},{4,20},{8,24},{12,28},{16,0},{20,4},{24,8},{28,12},{1,17},{... | collective-permute-start | bytes 2162696 | tf_op jit(solution)/shard_map/ppermute | solution.py:331
  223.8 33.6 %collective-permute-start.28 = (bf16[2,2,2,88,1024]{4,3,2,1,0:T(8,128)(2,1)S(1)}, bf16[2,2,2,88,1024]{4,3,2,1,0:T(8,128)(2,1)S(1)}, u32[]{:S(2)}, u32[]{:S(2)}) collective-permute-start(bf16[2,2,2,88,1024]{4,3,2,1,0:T(8,128)(2,1)S(1)} %broadcast_select_fusion.6), channel_id=1, source_target_pairs={{0,8},{4,12},{8,0},{12,4},{16,24},{20,28},{24,16},{28,20},{1,9},{5... | collective-permute-start | bytes 4325384 | tf_op jit(solution)/shard_map/ppermute | solution.py:331
  281.9 271.9 %all-gather.5.cloned.1.call-start = ((), (), s32[]{:S(2)}) async-start(), calls=%async_computation.9 | async-start | bytes 4325376 | tf_op jit(solution)/shard_map/all_gather | solution.py:589
  366.4 35.7 %collective-permute-start.32 = (bf16[2,2,2,32,2816]{4,3,1,0,2:T(8,128)(2,1)}, bf16[2,2,2,32,2816]{4,3,1,0,2:T(8,128)(2,1)S(1)}, u32[]{:S(2)}, u32[]{:S(2)}) collective-permute-start(bf16[2,2,2,32,2816]{4,3,1,0,2:T(8,128)(2,1)} %fusion.23), channel_id=1, source_target_pairs={{0,1},{1,0},{2,3},{3,2},{4,5},{5,4},{6,7},{7,6},{8,9},{9,8},{10,11... | collective-permute-start | bytes 4325384 | tf_op jit(solution)/shard_map/ppermute | solution.py:331
  368.0 35.1 %collective-permute-start.33 = (bf16[2,2,2,32,2816]{4,3,1,0,2:T(8,128)(2,1)S(1)}, bf16[2,2,2,32,2816]{4,3,1,0,2:T(8,128)(2,1)S(1)}, u32[]{:S(2)}, u32[]{:S(2)}) collective-permute-start(bf16[2,2,2,32,2816]{4,3,1,0,2:T(8,128)(2,1)S(1)} %fusion.22), channel_id=1, source_target_pairs={{0,2},{1,3},{2,0},{3,1},{4,6},{5,7},{6,4},{7,5},{8,10},{9,11},{10,... | collective-permute-start | bytes 4325384 | tf_op jit(solution)/shard_map/ppermute | solution.py:331
  418.3 45.9 %collective-permute-start.34 = (bf16[2,2,2,2,32,2048]{5,4,3,2,1,0:T(8,128)(2,1)}, bf16[2,2,2,2,32,2048]{5,4,3,2,1,0:T(8,128)(2,1)}, u32[]{:S(2)}, u32[]{:S(2)}) collective-permute-start(bf16[2,2,2,2,32,2048]{5,4,3,2,1,0:T(8,128)(2,1)} %fusion.25), channel_id=1, source_target_pairs={{0,4},{4,0},{8,12},{12,8},{16,20},{20,16},{24,28},{28,24},{1,5},{5... | collective-permute-start | bytes 6291464 | tf_op jit(solution)/shard_map/ppermute | solution.py:331
  432.1 26.9 %all-to-all-start.3 = ((bf16[2,4,64,1024]{3,2,0,1:T(8,128)(2,1)}), bf16[2,4,64,1024]{3,2,0,1:T(8,128)(2,1)}, u32[]{:S(2)}, u32[]{:S(2)}) async-start(bf16[2,4,64,1024]{3,2,0,1:T(8,128)(2,1)} %copy.184), calls=%async_computation.3 | async-start | bytes 2097152 | tf_op jit(solution)/shard_map/all_to_all | solution.py:626
  438.6 56.8 %collective-permute-start.36 = (bf16[2,2,32,2816]{3,2,1,0:T(8,128)(2,1)}, bf16[2,2,32,2816]{3,2,1,0:T(8,128)(2,1)}, u32[]{:S(2)}, u32[]{:S(2)}) collective-permute-start(bf16[2,2,32,2816]{3,2,1,0:T(8,128)(2,1)} %fusion.48), channel_id=1, source_target_pairs={{0,2},{1,3},{2,0},{3,1},{4,6},{5,7},{6,4},{7,5},{8,10},{9,11},{10,... | collective-permute-start | bytes 2162696 | tf_op jit(solution)/shard_map/ppermute | solution.py:331
  440.6 54.8 %collective-permute-start.37 = (bf16[2,2,32,2816]{3,2,1,0:T(8,128)(2,1)}, bf16[2,2,32,2816]{3,2,1,0:T(8,128)(2,1)}, u32[]{:S(2)}, u32[]{:S(2)}) collective-permute-start(bf16[2,2,32,2816]{3,2,1,0:T(8,128)(2,1)} %fusion.47), channel_id=1, source_target_pairs={{0,1},{1,0},{2,3},{3,2},{4,5},{5,4},{6,7},{7,6},{8,9},{9,8},{10,11... | collective-permute-start | bytes 2162696 | tf_op jit(solution)/shard_map/ppermute | solution.py:331
  526.5 26.3 %collective-permute-start.41 = (bf16[2,2,128,512]{3,2,0,1:T(8,128)(2,1)}, bf16[2,2,128,512]{3,2,0,1:T(8,128)(2,1)}, u32[]{:S(2)}, u32[]{:S(2)}) collective-permute-start(bf16[2,2,128,512]{3,2,0,1:T(8,128)(2,1)} %copy_bitcast_fusion.4), channel_id=1, source_target_pairs={{0,4},{4,0},{8,12},{12,8},{16,20},{20,16},{24,28},{28,24},{1,5},{5... | collective-permute-start | bytes 1572872 | tf_op jit(solution)/shard_map/ppermute | solution.py:331
  526.5 48.1 %collective-permute-start.43 = (bf16[2,32,5632]{2,1,0:T(8,128)(2,1)}, bf16[2,32,5632]{2,1,0:T(8,128)(2,1)}, u32[]{:S(2)}, u32[]{:S(2)}) collective-permute-start(bf16[2,32,5632]{2,1,0:T(8,128)(2,1)} %fusion.55), channel_id=1, source_target_pairs={{0,8},{4,12},{8,0},{12,4},{16,24},{20,28},{24,16},{28,20},{1,9},{5... | collective-permute-start | bytes 2162696 | tf_op jit(solution)/shard_map/ppermute | solution.py:331
  526.7 47.9 %collective-permute-start.44 = (bf16[2,2,32,2048]{3,2,1,0:T(8,128)(2,1)}, bf16[2,2,32,2048]{3,2,1,0:T(8,128)(2,1)}, u32[]{:S(2)}, u32[]{:S(2)}) collective-permute-start(bf16[2,2,32,2048]{3,2,1,0:T(8,128)(2,1)} %fusion.53), channel_id=1, source_target_pairs={{0,2},{1,3},{2,0},{3,1},{4,6},{5,7},{6,4},{7,5},{8,10},{9,11},{10,... | collective-permute-start | bytes 1572872 | tf_op jit(solution)/shard_map/ppermute | solution.py:331
  528.6 45.9 %collective-permute-start.45 = (bf16[2,2,32,1024]{3,2,1,0:T(8,128)(2,1)S(1)}, bf16[2,2,32,1024]{3,2,1,0:T(8,128)(2,1)}, u32[]{:S(2)}, u32[]{:S(2)}) collective-permute-start(bf16[2,2,32,1024]{3,2,1,0:T(8,128)(2,1)S(1)} %fusion.65), channel_id=1, source_target_pairs={{0,1},{1,0},{2,3},{3,2},{4,5},{5,4},{6,7},{7,6},{8,9},{9,8},{10,11... | collective-permute-start | bytes 786440 | tf_op jit(solution)/shard_map/ppermute | solution.py:331
  530.1 44.5 %collective-permute-start.46 = (bf16[2,2,2,32,1024]{4,3,2,1,0:T(8,128)(2,1)}, bf16[2,2,2,32,1024]{4,3,2,1,0:T(8,128)(2,1)}, u32[]{:S(2)}, u32[]{:S(2)}) collective-permute-start(bf16[2,2,2,32,1024]{4,3,2,1,0:T(8,128)(2,1)} %fusion.52), channel_id=1, source_target_pairs={{0,2},{1,3},{2,0},{3,1},{4,6},{5,7},{6,4},{7,5},{8,10},{9,11},{10,... | collective-permute-start | bytes 1572872 | tf_op jit(solution)/shard_map/ppermute | solution.py:331
  (190 other events, 2114.1 us)
Sparse Core Ops, SparseCore 0:
  11.5 127.5 all-gather.2
  282.1 108.8 reduce-scatter.3
  394.4 72.2 all-gather.4

commit v3 on v2

--- a/solution.py
+++ b/solution.py
@@ -18,6 +18,7 @@
 BF16 = jnp.bfloat16
 F32 = jnp.float32
 BQ = 128
+FF_BLOCK = 256
 
 
 def nt(a, b):
@@ -376,6 +377,13 @@
         self.parts = self.parts + [self.flying]
         self.flying = None
 
+    def finish(self):
+        if self.flying is not None:
+            self.land()
+        while self.order:
+            self.launch(self.outgoing())
+            self.land()
+
     def result(self):
         return sum(p.astype(F32) for p in self.parts)
 
@@ -444,6 +452,12 @@
     return Chain(full, place_bits(), hops(seq_first, turned))
 
 
+def chain_of_halves(away, kept, seq_first=True, turned=False):
+    chain = Chain(kept, [b for b in place_bits() if b != ("batch", 0)], hops(seq_first, turned)[1:])
+    chain.flying = flip(away, "batch", 1).reshape(chain.parts[0].shape)
+    return chain
+
+
 def small_sum(values):
     got = lax.all_to_all(values, ("batch", "seq"), 0, 0, tiled=True)
     return jnp.sum(got, axis=0)
@@ -467,6 +481,102 @@
     value = 0.5 * v * (1.0 + t)
     slope = 0.5 * (1.0 + t) + 0.5 * v * (1.0 - t * t) * (scale * (1.0 + 3 * 0.044715 * (v * v)))
     return value, slope
+
+
+def hidden_rows(x, core_rows):
+    turned = x.T
+    blocks = [turned[i : i + core_rows] for i in range(0, turned.shape[0], core_rows)]
+    return jnp.concatenate(blocks[0::2], axis=0), jnp.concatenate(blocks[1::2], axis=0)
+
+
+def ffn_kernel(
+    core_ref, h_ref, gain_ref, og_ref, wg_ref, wu_ref, wr_ref,
+    out_ref, hgrad_ref, gain_grad_ref, dg_away_ref, dg_ref, du_away_ref, du_ref, dr_ref,
+    x_ref, xt_ref, res_ref, back_ref, *, core_rows,
+):
+    half = dg_ref.shape[0]
+    step = pl.program_id(0)
+
+    @pl.when(step == 0)
+    def _():
+        hidden = h_ref[...]
+        x = (hidden * inverse_rms(hidden) * gain_ref[...]).astype(BF16)
+        x_ref[...] = x
+        flipped = hidden_rows(x, core_rows)
+        first_core = core_ref[0] == 0
+        xt_ref[:half] = jnp.where(first_core, flipped[1], flipped[0])
+        xt_ref[half:] = jnp.where(first_core, flipped[0], flipped[1])
+        res_ref[...] = jnp.zeros_like(res_ref)
+        back_ref[...] = jnp.zeros_like(back_ref)
+
+    x, og = x_ref[...], og_ref[...]
+    wg, wu, wr = wg_ref[...], wu_ref[...], wr_ref[...]
+    gelu_value, gelu_slope = gelu_parts(nn(x, wg))
+    up = nn(x, wu)
+    activated = (gelu_value * up).astype(BF16)
+    upstream = nt(og, wr)
+    gate_grad = (upstream * up * gelu_slope).astype(BF16)
+    up_grad = (upstream * gelu_value).astype(BF16)
+    res_ref[...] += nn(activated, wr)
+    back_ref[...] += nt(gate_grad, wg) + nt(up_grad, wu)
+    dr_ref[...] = tn(activated, og).astype(BF16)
+    xt = xt_ref[...]
+    gate_product, up_product = nn(xt, gate_grad).astype(BF16), nn(xt, up_grad).astype(BF16)
+    dg_away_ref[...], dg_ref[...] = gate_product[:half], gate_product[half:]
+    du_away_ref[...], du_ref[...] = up_product[:half], up_product[half:]
+
+    @pl.when(step == pl.num_programs(0) - 1)
+    def _():
+        hidden = h_ref[...]
+        out_ref[...] = (hidden + res_ref[...]).astype(BF16)
+        inverse = inverse_rms(hidden)
+        upward = back_ref[...]
+        weighted = gain_ref[...] * upward
+        dot = jnp.mean(weighted * hidden, axis=-1, keepdims=True)
+        part = inverse * weighted - hidden * (inverse * inverse * inverse) * dot
+        hgrad_ref[...] = og_ref[...].astype(F32) + part
+        gain_grad_ref[...] = jnp.sum(upward * hidden * inverse, axis=0, keepdims=True)
+
+
+def feed_forward(hidden, gain, og, w_rest, w_red, ff_first):
+    count, width = hidden.shape
+    ff = w_red.shape[0]
+    steps, gate_first = ff // FF_BLOCK, ff_first // FF_BLOCK
+    whole = pl.BlockSpec((count, width), lambda j: (0, 0))
+    row = pl.BlockSpec((1, width), lambda j: (0, 0))
+    down = pl.BlockSpec((FF_BLOCK, width), lambda j: (j, 0))
+    cols = pl.BlockSpec((width // 2, FF_BLOCK), lambda j: (0, j))
+    core_rows = width // lax.axis_size("batch")
+    return pl.pallas_call(
+        functools.partial(ffn_kernel, core_rows=core_rows),
+        grid=(steps,),
+        in_specs=[
+            pl.BlockSpec(memory_space=pltpu.SMEM),
+            whole, row, whole,
+            pl.BlockSpec((width, FF_BLOCK), lambda j: (0, j + gate_first)),
+            pl.BlockSpec((width, FF_BLOCK), lambda j: (0, j + gate_first + steps)),
+            down,
+        ],
+        out_specs=[whole, whole, row, cols, cols, cols, cols, down],
+        out_shape=[
+            jax.ShapeDtypeStruct((count, width), BF16),
+            jax.ShapeDtypeStruct((count, width), F32),
+            jax.ShapeDtypeStruct((1, width), F32),
+            *[jax.ShapeDtypeStruct((width // 2, ff), BF16)] * 4,
+            jax.ShapeDtypeStruct((ff, width), BF16),
+        ],
+        scratch_shapes=[
+            pltpu.VMEM((count, width), BF16),
+            pltpu.VMEM((width, count), BF16),
+            pltpu.VMEM((count, width), F32),
+            pltpu.VMEM((count, width), F32),
+        ],
+        compiler_params=pltpu.CompilerParams(vmem_limit_bytes=56 << 20),
+        cost_estimate=pl.CostEstimate(
+            flops=18 * count * width * ff, transcendentals=count * ff, bytes_accessed=12 * width * ff
+        ),
+        name="feed_forward",
+    )(my_bit("batch", 0).reshape(1).astype(jnp.int32), hidden, gain, og, w_rest, w_rest, w_red)
 
 
 def shards(
@@ -532,18 +642,21 @@
     )
     table = small_rows[:, 3 * own : 3 * own + bias_own].reshape(NB, QUERY_HEADS).astype(F32)
 
-    mid_a = jnp.stack([jnp.concatenate([wkv[1, 0], wkv[1, 1]], axis=1), wo[0]])
-    mid_b = jnp.stack([wq[1], wo[1]])
-    _, _, mid_a, mid_b = settle(packet, first_hop, mid_a, mid_b)
-    gather_a = Gather(mid_a, batch_far + seq_up + core, 1)
-    gather_b = Gather(mid_b, batch_far + seq_up[::-1] + core, 1)
-    gather_r = Gather(wr, seq_up + batch_far + core)
-    for _ in batch_far:
-        for gather in (gather_a, gather_b):
-            if gather.flying is not None:
-                gather.land()
-            gather.launch(gather.held)
-    w_exp = lax.all_gather(jnp.concatenate([we[0], we[1]], axis=1), every, axis=0, tiled=True)
+    ff, ff_own = we.shape[2], wr.shape[0]
+    folds = -(-ff_own // own)
+    wr_rows = jnp.pad(wr, ((0, folds * own - ff_own), (0, 0))).reshape(folds, own, width)
+    pieces = [wkv[1, 0], wkv[1, 1], wo[0], wq[1], wo[1], we[0], we[1], *[wr_rows[i] for i in range(folds)]]
+    w_rest = lax.all_gather(jnp.concatenate(pieces, axis=1), every, axis=0, tiled=True)
+    w_kv1, w_o0, w_q1, w_o1 = (w_rest[:, i * width : (i + 1) * width] for i in range(4))
+    ff_first = 4 * width
+    down_first = ff_first + 2 * ff
+    w_red = jnp.concatenate(
+        [
+            w_rest[:, down_first + i * width : down_first + (i + 1) * width].reshape(devices, own, width)
+            for i in range(folds)
+        ],
+        axis=1,
+    )[:, :ff_own].reshape(ff, width)
 
     reach = length // 2
     strip_width = 2 * reach + BQ
@@ -555,22 +668,12 @@
     base = jnp.dot(table_local.T, picks, precision=lax.Precision.HIGHEST)
     base = jnp.where(lag_ok[None, :], base, NEGATIVE)
 
-    token_pieces = tick(token_pieces, gather_a, gather_b, gather_r)
     all_tokens = jnp.stack([jnp.stack(p) for p in token_pieces], axis=1).astype(F32)
     all_normed = (all_tokens * inverse_rms(all_tokens) * gain_values[0]).astype(BF16).reshape(-1, width)
     head_qkv = nn(all_normed, w_heads).astype(BF16).reshape(seq_count, rows, part, cols)
     head_qkv = jnp.stack(absolute(head_qkv, "seq"), axis=1).reshape(rows, length, cols)
-    head_qkv = tick(head_qkv, gather_a, gather_b)
     head_context, lse = self_attention(head_qkv, all_segments, base)
-    while gather_r.order[0][0] == "seq":
-        head_context = tick(head_context, gather_r)
-    head_context = tick(head_context, gather_r)
     context = lax.all_to_all(head_context, "seq", split_axis=1, concat_axis=2, tiled=True).reshape(-1, width)
-    while gather_a.order:
-        context = tick(context, gather_a, gather_b)
-    context = land(context, gather_a, gather_b)
-    w_mid_a, w_mid_b = gather_a.held.reshape(2, width, width), gather_b.held.reshape(2, width, width)
-    w_kv1, w_o0, w_q1, w_o1 = w_mid_a[0], w_mid_a[1], w_mid_b[0], w_mid_b[1]
 
     mem = memory.reshape(rows * memory_part, width)
     mkv = nn(mem, w_kv1).astype(BF16).reshape(rows, memory_part, -1)
@@ -582,48 +685,28 @@
     inv_one = inverse_rms(hidden_one)
     normed_one = (hidden_one * inv_one * gain_values[1]).astype(BF16)
     cross_q = nn(normed_one, w_q1).astype(BF16).reshape(rows, part, width)
-    while len(gather_r.order) > 1:
-        cross_q = tick(cross_q, gather_r)
     cross_context = cross_attention(cross_q, mk, mv, segments, all_memory_segments)
-    cross_context, first = settle(cross_context, first)
-    w_first = lax.all_gather(first.reshape(own, -1), every, axis=0, tiled=True)
     cross_flat = cross_context.reshape(-1, width)
     hidden_two = hidden_one + nn(cross_flat, w_o1)
-    inv_two = inverse_rms(hidden_two)
-    normed_two = (hidden_two * inv_two * gain_values[2]).astype(BF16)
-
-    ff = we.shape[2]
-    normed_two = tick(normed_two, gather_r)
-    gate = nn(normed_two, w_exp[:, :ff])
-    up = nn(normed_two, w_exp[:, ff:])
-    gelu_value, gelu_slope = gelu_parts(gate)
-    activated = (gelu_value * up).astype(BF16)
+    hidden_two, w_red, w_heads = settle(hidden_two, w_red, w_heads)
+    w_first = jnp.concatenate(gather_direct(w_heads, "seq"), axis=1)
     og = output_grad.reshape(rows * part, width)
-    activated = land(activated, gather_r)
-    w_red = gather_r.held.reshape(-1, width)
-    wide_og = jnp.pad(og, ((0, 0), (0, -width % 384)))
-    reduce_part = tn(activated, wide_og).astype(BF16)
-    activated, reduce_part = settle(activated, reduce_part)
-    (grad_reduce,) = settle(lax.psum_scatter(reduce_part, every, scatter_dimension=0, tiled=True))
-    grad_reduce = grad_reduce[:, :width].astype(F32)
-    result = (hidden_two + nn(activated, w_red)).astype(BF16).reshape(tokens.shape)
-    activated_grad = nt(og, w_red)
-    gate_grad = (activated_grad * up * gelu_slope).astype(BF16)
-    up_grad = (activated_grad * gelu_value).astype(BF16)
-    gate_grad, up_grad, result = settle(gate_grad, up_grad, result)
-    chain_g = chain_of(tn(normed_two, gate_grad).astype(BF16))
-    chain_u = chain_of(tn(normed_two, up_grad).astype(BF16), turned=True)
-    gate_grad, up_grad = tick((gate_grad, up_grad), chain_g, chain_u)
-    normed_two_grad = nt(gate_grad, w_exp[:, :ff]) + nt(up_grad, w_exp[:, ff:])
-    part_two, gain_two = norm_back(hidden_two, inv_two, gain_values[2], normed_two_grad)
-    hidden_two_grad = og.astype(F32) + part_two
-    hidden_two_grad = tick(hidden_two_grad, chain_g, chain_u)
+    result, hidden_two_grad, gain_two, *part_gu, part_reduce = feed_forward(
+        hidden_two, gain_values[2:3], og, w_rest, w_red, ff_first
+    )
+    result, gain_two = result.reshape(tokens.shape), gain_two[0]
+    chain_g = chain_of_halves(part_gu[0], part_gu[1])
+    chain_u = chain_of_halves(part_gu[2], part_gu[3], turned=True)
+    chain_r = chain_of(part_reduce, seq_first=False)
+    hidden_two_grad, w_first = tick((hidden_two_grad, w_first), chain_r)
 
     cross_out_grad = hidden_two_grad.astype(BF16)
     cross_cots = nt(cross_out_grad, w_o1).astype(BF16).reshape(rows, part, width)
+    cross_cots = tick(cross_cots, chain_r, chain_g, chain_u)
     cross_dq, mdk, mdv = cross_attention_back(cross_q, mk, mv, cross_cots, segments, all_memory_segments)
     mdkv = jnp.concatenate([mdk, mdv], axis=2).reshape(rows, seq_count, memory_part, -1)
-    mdkv = lax.all_to_all(mdkv, "seq", split_axis=1, concat_axis=1, tiled=True)
+    mdkv = absolute(mdkv.swapaxes(0, 1), "seq")
+    mdkv = [mdkv[0]] + [flip(mdkv[j], "seq", j) for j in range(1, seq_count)]
     cross_dq = cross_dq.reshape(-1, width)
     part_one, gain_one = norm_back(hidden_one, inv_one, gain_values[1], nt(cross_dq, w_q1))
     hidden_one_grad = hidden_two_grad + part_one
@@ -634,32 +717,37 @@
     chain_q1 = chain_of(tn(normed_one, cross_dq).astype(BF16))
     chain_a = joined([chain_o1, chain_q1], chain_o1.order)
     chain_o0 = chain_of(tn(context, self_out_grad).astype(BF16), turned=True)
-    cots = tick(cots, chain_g, chain_u, chain_a, chain_o0)
+    cots = tick(cots, chain_r, chain_g, chain_u, chain_a, chain_o0)
     head_cots = lax.all_to_all(cots, "seq", split_axis=2, concat_axis=1, tiled=True)
     head_cots, mdkv = settle(head_cots, mdkv)
-    mdkv = jnp.sum(mdkv.astype(F32), axis=1).astype(BF16).reshape(rows * memory_part, -1)
+    mdkv = sum(m.astype(F32) for m in mdkv).astype(BF16).reshape(rows * memory_part, -1)
     memory_grad = nt(mdkv, w_kv1).reshape(memory.shape)
     chain_k1 = chain_of(tn(mem, mdkv).astype(BF16), turned=True)
     head_cots, memory_grad = tick((head_cots, memory_grad), chain_a, chain_o0, chain_k1)
     head_grads, lag_sums = self_attention_back(head_qkv, head_cots, lse, all_segments, base)
-    relative = jnp.stack(absolute(head_grads.reshape(rows, seq_count, part, cols).swapaxes(0, 1), "seq"))
+    relative = absolute(head_grads.reshape(rows, seq_count, part, cols).swapaxes(0, 1), "seq")
+    lag_sums, *relative = settle(lag_sums, *relative)
+    came = [relative[0]] + [flip(relative[j], "seq", j) for j in range(1, seq_count)]
     batch_bits = [("batch", b) for b in reversed(range(bit_count("batch")))]
-    chain_f = Chain(tn(all_normed, relative.reshape(-1, cols)).astype(BF16), batch_bits, hops(False, False)[: len(batch_bits)])
-    head_grads = land(head_grads, chain_g, chain_u)
+    all_grads = jnp.stack(relative).reshape(-1, cols)
+    chain_f = Chain(tn(all_normed, all_grads).astype(BF16), batch_bits, hops(False, False)[: len(batch_bits)])
+    lag_sums = land(lag_sums, chain_g, chain_u)
     while chain_g.order[0][0] == "seq":
-        head_grads = land(tick(head_grads, chain_g, chain_u), chain_g, chain_u)
+        lag_sums = land(tick(lag_sums, chain_g, chain_u), chain_g, chain_u)
     chain_gu = joined([chain_g, chain_u], chain_g.order)
-    chains = (chain_f, chain_gu, chain_a, chain_o0, chain_k1)
-    head_grads, lag_sums = tick((head_grads, lag_sums), *chains)
-    dqkv = lax.all_to_all(head_grads, "seq", split_axis=1, concat_axis=2, tiled=True).reshape(rows * part, -1)
+    chains = (chain_f, chain_gu, chain_r, chain_a, chain_o0, chain_k1)
+    lag_sums = tick(lag_sums, *chains)
+    dqkv = jnp.concatenate(came, axis=-1).reshape(rows * part, -1)
     dqkv = tick(dqkv, chain_f)
     part_zero, gain_zero = norm_back(x, inv_zero, gain_values[0], nt(dqkv, w_first))
     input_grad = (hidden_one_grad + part_zero).reshape(tokens.shape)
-    while any(c.order or c.flying is not None for c in chains):
-        input_grad = tick(input_grad, *chains)
-    grad_gu, grad_a = chain_gu.result(), chain_a.result()
+    input_grad = tick(input_grad, *chains)
+    for chain in chains:
+        chain.finish()
+    grad_gu, grad_reduce = chain_gu.result(), chain_r.result()
+    grad_gate, grad_up = grad_gu[:, :ff], grad_gu[:, ff:]
+    grad_a = chain_a.result()
     grad_o0, grad_k1 = chain_o0.result(), chain_k1.result()
-    grad_gate, grad_up = grad_gu[:, :ff], grad_gu[:, ff:]
     grad_o1, grad_q1 = grad_a[:, :width], grad_a[:, width:]
     first_grads = lax.all_to_all(chain_f.result().reshape(seq_count, own, cols), "seq", 0, 0, tiled=True)
     first_grads = first_grads.transpose(1, 0, 2)

time: 650 us -> 612 us (0.942)
  Pallas kernels: 71 us -> 110 us
  matrix products: 83.8 us -> 47.9 us
  blocking collectives: 30.1 us -> 0 us
  local copies, waits for them, and re-layouts: 67 us -> 55.5 us
  other arithmetic: 103 us -> 95.3 us
    all_gather x2 -> x1, waiting for transfers between devices: 0.02 us -> 49.9 us  [shards(): lax.all_gather(jnp.concatenate(pieces, axis=1), every, axis=0, tiled=True)]
    pallas_call x0 -> x1, Pallas kernels: none -> 38.8 us  [feed_forward(): pl.pallas_call(functools.partial(ffn_kernel, core_rows=core_rows), grid=(...]
    ppermute x56 -> x55, waiting for transfers between devices: 156 us -> 120 us  [flip(): lax.ppermute(value, axis, [(i, i ^ mask) for i in range(lax.axis_size(axi...]
    all_to_all x1 -> x0, blocking collectives: 30.1 us -> none  [shards(): lax.all_to_all(head_context, 'seq', split_axis=1, concat_axis=2, tiled=True)]
    select_n x16 -> x3, other arithmetic: 28.2 us -> 1.38 us  [land(): self.held = jnp.where(pair == my_bit(*self.last), own, came)]
    dot_general x8 -> x5, matrix products: 28.9 us -> 14.9 us  [nn(): lax.dot_general(a, b, (((1,), (0,)), ((), ())), preferred_element_type=F32)]
    dot_general x8 -> x5, matrix products: 34.4 us -> 22 us  [nt(): lax.dot_general(a, b, (((1,), (1,)), ((), ())), preferred_element_type=F32)]
    unnamed x308 -> x235, local copies, waits for them, and re-layouts: 21.9 us -> 9.77 us
  transfers between devices with their start and end apart: 65 -> 61, of which waited for: 23 -> 23; matrix products, arithmetic and copies ran while one was open for 34% -> 25% of each run, Pallas kernels for 11% -> 14%
where the time goes in v3:
time: 612 us; the launch traced here: 604 us
  waiting for transfers between devices  202 us (33%)
  Pallas kernels  110 us (18%)
  other arithmetic  95.3 us (16%)
  starting transfers between devices  77.3 us (13%)
  local copies, waits for them, and re-layouts  55.5 us (9%)
  matrix products  47.9 us (8%)
  between operations  16.4 us (3%)
    ppermute x55, waiting for transfers between devices, flip(): lax.ppermute(value, axis, [(i, i ^ mask) for i in range(lax.axis_size(axi...  120 us
    ppermute x55, starting transfers between devices, flip(): lax.ppermute(value, axis, [(i, i ^ mask) for i in range(lax.axis_size(axi...  59 us
    all_gather x1, waiting for transfers between devices, shards(): lax.all_gather(jnp.concatenate(pieces, axis=1), every, axis=0, tiled=True)  49.9 us
    convert_element_type x22, other arithmetic, outgoing(): sum((p.astype(F32) for p in self.half(1 - my_bit(*self.order[0]))))  44 us
    pallas_call x1, Pallas kernels, feed_forward(): pl.pallas_call(functools.partial(ffn_kernel, core_rows=core_rows), grid=(...  38.8 us
    pallas_call x1, Pallas kernels, self_attention_back(): pl.pallas_call(self_bwd_kernel, grid=(rows,), in_specs=[all_spec, queries...  26.4 us
    all_to_all x1, waiting for transfers between devices, shards(): lax.all_to_all(head_context, 'seq', split_axis=1, concat_axis=2, tiled=True)  22.7 us
    dot_general x5, matrix products, nt(): lax.dot_general(a, b, (((1,), (1,)), ((), ())), preferred_element_type=F32)  22 us
  transfers between devices with their start and end apart: 61, of which 23 were waited for; matrix products, arithmetic and copies ran while one was open for 25% of the time, Pallas kernels for 14%

profile of v3, /device:TPU:0, one launch (start us, length us, event | category | flops | bytes accessed | tf_op | source)
XLA Modules:
  0.0 603.6 jit_solution(1249982509759240901)
XLA Ops:
  25.3 4.6 gather_fusion
  33.8 16.4 %collective-permute-done.6 = bf16[4,40,512]{2,1,0:T(8,128)(2,1)S(1)} collective-permute-done((bf16[4,40,512]{2,1,0:T(8,128)(2,1)S(1)}, bf16[4,40,512]{2,1,0:T(8,128)(2,1)S(1)}, u32[]{:S(2)}, u32[]{:S(2)}) %collective-permute-start.6) | collective-permute-done | bytes 163872 | tf_op jit(solution)/shard_map/ppermute | solution.py:332
  58.0 18.9 %collective-permute-done.7 = bf16[2,4,40,512]{3,2,1,0:T(8,128)(2,1)} collective-permute-done((bf16[2,4,40,512]{3,2,1,0:T(8,128)(2,1)S(1)}, bf16[2,4,40,512]{3,2,1,0:T(8,128)(2,1)}, u32[]{:S(2)}, u32[]{:S(2)}) %collective-permute-start.7) | collective-permute-done | bytes 327712 | tf_op jit(solution)/shard_map/ppermute | solution.py:332
  78.1 9.0 %collective-permute-done.2 = bf16[256,1024]{1,0:T(8,128)(2,1)} collective-permute-done((bf16[256,1024]{1,0:T(8,128)(2,1)S(1)}, bf16[256,1024]{1,0:T(8,128)(2,1)}, u32[]{:S(2)}, u32[]{:S(2)}) %collective-permute-start.2) | collective-permute-done | bytes 524320 | tf_op jit(solution)/shard_map/ppermute | solution.py:332
  89.0 7.4 %collective-permute-done.5 = bf16[256,1024]{1,0:T(8,128)(2,1)} collective-permute-done((bf16[256,1024]{1,0:T(8,128)(2,1)}, bf16[256,1024]{1,0:T(8,128)(2,1)}, u32[]{:S(2)}, u32[]{:S(2)}) %collective-permute-start.5) | collective-permute-done | bytes 524320 | tf_op jit(solution)/shard_map/ppermute | solution.py:332
  107.8 18.3 %self_attention.1 = (bf16[2,1024,256]{2,1,0:T(8,128)(2,1)S(1)}, f32[2,1024,4]{2,1,0:T(8,128)S(1)}) custom-call(bf16[2,1024,512]{2,1,0:T(8,128)(2,1)S(1)} %bitcast.567, s32[2,1,1024]{2,1,0:T(1,128)S(1)} %broadcast_in_dim_reshape.12.seg_row_ref, s32[2,1024,1]{2,1,0:T(8,128)S(1)} %broadcast_in_dim_reshape.15.seg_col_ref, ...), custom_call_target="tpu_custom_call" | custom-call | flops 805306368 | bytes 4194304 | tf_op jit(solution)/shard_map/self_attention/pallas_call | solution.py:175
  133.2 22.7 %all-to-all-done.1 = bf16[2,1024,256]{2,0,1:T(2,128)(2,1)S(1)} async-done(((bf16[2,1024,256]{2,0,1:T(2,128)(2,1)}), bf16[2,1024,256]{2,0,1:T(2,128)(2,1)S(1)}, u32[]{:S(2)}, u32[]{:S(2)}) %all-to-all-start.1) | async-done | bytes 1048608 | tf_op jit(solution)/shard_map/all_to_all | solution.py:676
  157.9 49.9 %all-gather.2.cloned.1.call-done.wg_ref.wu_ref = bf16[1024,12800]{1,0:T(8,128)(2,1)} async-done(((bf16[32,12800]{1,0:T(8,128)(2,1)}), bf16[1024,12800]{1,0:T(8,128)(2,1)}) %all-gather.2.cloned.1.call-update) | async-done | bytes 26214416 | tf_op jit(solution)/shard_map/all_gather | solution.py:649
  216.5 4.3 fusion.133
  227.5 11.2 %cross_attention.1 = bf16[2,256,1024]{2,1,0:T(8,128)(2,1)S(1)} custom-call(bf16[2,256,1024]{2,1,0:T(8,128)(2,1)S(1)} %bitcast.571, bf16[2,256,512]{2,1,0:T(8,128)(2,1)S(1)} %get-tuple-element.350.k_ref, bf16[2,256,512]{2,1,0:T(8,128)(2,1)S(1)} %get-tuple-element.349.v_ref, s32[2,1,256]{2,1,0:T(1,128)S(1)} %broadcast_in_dim_reshape.14.seg_row_ref, ...), custom_call_target="tpu_custom_call" | custom-call | flops 536870912 | bytes 3145728 | tf_op jit(solution)/shard_map/cross_attention/pallas_call | solution.py:288
  238.7 4.6 fusion.43.h_ref
  246.8 38.8 %feed_forward.1 = (bf16[512,1024]{1,0:T(8,128)(2,1)}, f32[512,1024]{1,0:T(8,128)}, f32[1,1024]{1,0:T(1,128)}, bf16[512,2816]{1,0:T(8,128)(2,1)}, bf16[512,2816]{...) custom-call(s32[1]{0:T(128)} %bitcast.core_ref, ...), custom_call_target="tpu_custom_call" | custom-call | flops 26575110144 | bytes 34603008 | tf_op jit(solution)/shard_map/feed_forward/pallas_call | solution.py:550
  310.9 14.9 %cross_attention_back.1 = (bf16[2,256,1024]{2,1,0:T(8,128)(2,1)S(1)}, bf16[2,256,512]{2,1,0:T(8,128)(2,1)S(1)}, bf16[2,256,512]{2,1,0:T(8,128)(2,1)S(1)}) custom-call(bf16[2,256,1024]{2,1,0:T(8,128)(2,1)S(1)} %bitcast.572, bf16[2,256,512]{2,1,0:T(8,128)(2,1)S(1)} %get-tuple-element.350.k_ref, bf16[2,256,512]{2,1,0:T(8,128)(2,1)S(1)} %get-tuple-element.349.v_ref, ...), custom_call_target="tpu_custom_call" | custom-call | flops 1342177280 | bytes 5242880 | tf_op jit(solution)/shard_map/cross_attention_back/pallas_call | solution.py:305
  344.9 18.3 %collective-permute-done.21 = bf16[2,2,2,88,1024]{4,3,2,1,0:T(8,128)(2,1)S(1)} collective-permute-done((bf16[2,2,2,88,1024]{4,3,2,1,0:T(8,128)(2,1)S(1)}, bf16[2,2,2,88,1024]{4,3,2,1,0:T(8,128)(2,1)S(1)}, u32[]{:S(2)}, u32[]{:S(2)}) %collective-permute-start.21) | collective-permute-done | bytes 1441824 | tf_op jit(solution)/shard_map/ppermute | solution.py:332
  388.2 6.8 %all-to-all-done.2 = bf16[2,256,1024]{1,0,2:T(2,128)(2,1)} async-done(((bf16[2,256,1024]{1,0,2:T(2,128)(2,1)}), bf16[2,256,1024]{1,0,2:T(2,128)(2,1)}, u32[]{:S(2)}, u32[]{:S(2)}) %all-to-all-start.2) | async-done | bytes 1048608 | tf_op jit(solution)/shard_map/all_to_all | solution.py:721
  402.6 4.5 collective-permute-done.26
  412.9 4.4 fusion.15
  422.3 26.4 %self_attention_back.1 = (bf16[2,1024,512]{2,1,0:T(8,128)(2,1)S(1)}, f32[4,1152]{1,0:T(4,128)S(1)}) custom-call(bf16[2,1024,512]{2,1,0:T(8,128)(2,1)} %bitcast.568, bf16[2,1024,256]{2,1,0:T(8,128)(2,1)S(1)} %bitcast.570, f32[2,1024,4]{2,1,0:T(8,128)S(1)} %copy-done.6, s32[2,1,1024]{2,1,0:T(1,128)S(1)} %broadcast_in_dim_reshape.12.seg_row_ref, ...), custom_call_target="tpu_custom_call" | custom-call | flops 2013265920 | bytes 6291456 | tf_op jit(solution)/shard_map/self_attention_back/pallas_call | solution.py:199
  467.0 9.2 %collective-permute-done.35 = bf16[2,2,2,32,2048]{4,3,2,1,0:T(8,128)(2,1)S(1)} collective-permute-done((bf16[2,2,2,32,2048]{4,3,2,1,0:T(8,128)(2,1)}, bf16[2,2,2,32,2048]{4,3,2,1,0:T(8,128)(2,1)S(1)}, u32[]{:S(2)}, u32[]{:S(2)}) %collective-permute-start.35) | collective-permute-done | bytes 1048608 | tf_op jit(solution)/shard_map/ppermute | solution.py:332
  487.6 9.2 %collective-permute-done.31 = bf16[2,256,512]{2,1,0:T(8,128)(2,1)} collective-permute-done((bf16[2,256,512]{2,1,0:T(8,128)(2,1)}, bf16[2,256,512]{2,1,0:T(8,128)(2,1)}, u32[]{:S(2)}, u32[]{:S(2)}) %collective-permute-start.31) | collective-permute-done | bytes 524320 | tf_op jit(solution)/shard_map/ppermute | solution.py:332
  507.5 6.8 %fusion.23 = (f32[1024]{0:T(1024)S(1)}, f32[512]{0:T(512)S(1)}, f32[512,1024]{1,0:T(8,128)}) fusion(bf16[2,256,1024]{2,1,0:T(8,128)(2,1)S(1)} %copy-done.28, f32[512]{0:T(512)S(1)} %bitcast.656, f32[1024]{0:T(1024)S(1)} %mul.332, bf16[512,2048]{1,0:T(8,128)(2,1)} %bitcast.630, bf16[1024,2048]{1,0:T(8,128)(2,1)} %pad_maximum_fusion.3), kind=kOutput, calls=%fused_computation.60 | convolution fusion | flops 2151152128 | bytes 9449472 | tf_op jit(solution)/shard_map/dot_general | solution.py:25
  517.8 4.6 fusion.20
  526.3 6.9 %collective-permute-done.39 = bf16[2,128,512]{2,1,0:T(8,128)(2,1)S(1)} collective-permute-done((bf16[2,128,512]{2,1,0:T(8,128)(2,1)}, bf16[2,128,512]{2,1,0:T(8,128)(2,1)S(1)}, u32[]{:S(2)}, u32[]{:S(2)}) %collective-permute-start.39) | collective-permute-done | bytes 262176 | tf_op jit(solution)/shard_map/ppermute | solution.py:332
  552.9 6.8 %collective-permute-done.45 = bf16[128,512]{1,0:T(8,128)(2,1)S(1)} collective-permute-done((bf16[128,512]{1,0:T(8,128)(2,1)S(1)}, bf16[128,512]{1,0:T(8,128)(2,1)S(1)}, u32[]{:S(2)}, u32[]{:S(2)}) %collective-permute-start.45) | collective-permute-done | bytes 131104 | tf_op jit(solution)/shard_map/ppermute | solution.py:332
  (530 shorter events, 262.2 us)
Async XLA Ops:
  7.2 200.6 %all-gather.2.cloned.1.call-start = ((), (), s32[]{:S(2)}) async-start(), calls=%async_computation.5 | async-start | bytes 27033600 | tf_op jit(solution)/shard_map/all_gather | solution.py:649
  11.6 40.3 %collective-permute-start.9 = (s32[2,320]{1,0:T(2,128)S(1)}, s32[2,320]{1,0:T(2,128)S(1)}, u32[]{:S(2)}, u32[]{:S(2)}) collective-permute-start(s32[2,320]{1,0:T(2,128)S(1)} %constant_dynamic-update-slice_fusion), channel_id=1, source_target_pairs={{0,1},{1,0},{2,3},{3,2},{4,5},{5,4},{6,7},{7,6},{8,9},{9,8},{10,11... | collective-permute-start | bytes 7688 | tf_op jit(solution)/shard_map/ppermute | solution.py:332
  14.6 38.5 %collective-permute-start.10 = (s32[2,320]{1,0:T(2,128)S(1)}, s32[2,320]{1,0:T(2,128)S(1)}, u32[]{:S(2)}, u32[]{:S(2)}) collective-permute-start(s32[2,320]{1,0:T(2,128)S(1)} %constant_dynamic-update-slice_fusion), channel_id=1, source_target_pairs={{0,2},{1,3},{2,0},{3,1},{4,6},{5,7},{6,4},{7,5},{8,10},{9,11},{10,... | collective-permute-start | bytes 7688 | tf_op jit(solution)/shard_map/ppermute | solution.py:332
  21.8 33.0 %collective-permute-start = (bf16[256,1024]{1,0:T(8,128)(2,1)S(1)}, bf16[256,1024]{1,0:T(8,128)(2,1)S(1)}, u32[]{:S(2)}, u32[]{:S(2)}) collective-permute-start(bf16[256,1024]{1,0:T(8,128)(2,1)S(1)} %get-tuple-element.357), channel_id=1, source_target_pairs={{0,1},{1,0},{2,3},{3,2},{4,5},{5,4},{6,7},{7,6},{8,9},{9,8},{10,11... | collective-permute-start | bytes 1572872 | tf_op jit(solution)/shard_map/ppermute | solution.py:332
  23.8 32.4 %collective-permute-start.4 = (bf16[256,1024]{1,0:T(8,128)(2,1)}, bf16[256,1024]{1,0:T(8,128)(2,1)}, u32[]{:S(2)}, u32[]{:S(2)}) collective-permute-start(bf16[256,1024]{1,0:T(8,128)(2,1)} %get-tuple-element.356), channel_id=1, source_target_pairs={{0,2},{1,3},{2,0},{3,1},{4,6},{5,7},{6,4},{7,5},{8,10},{9,11},{10,... | collective-permute-start | bytes 1572872 | tf_op jit(solution)/shard_map/ppermute | solution.py:332
  53.0 36.0 %collective-permute-start.3 = (bf16[256,1024]{1,0:T(8,128)(2,1)}, bf16[256,1024]{1,0:T(8,128)(2,1)}, u32[]{:S(2)}, u32[]{:S(2)}) collective-permute-start(bf16[256,1024]{1,0:T(8,128)(2,1)} %get-tuple-element.356), channel_id=1, source_target_pairs={{0,1},{1,0},{2,3},{3,2},{4,5},{5,4},{6,7},{7,6},{8,9},{9,8},{10,11... | collective-permute-start | bytes 1572872 | tf_op jit(solution)/shard_map/ppermute | solution.py:332
  54.8 32.3 %collective-permute-start.2 = (bf16[256,1024]{1,0:T(8,128)(2,1)S(1)}, bf16[256,1024]{1,0:T(8,128)(2,1)}, u32[]{:S(2)}, u32[]{:S(2)}) collective-permute-start(bf16[256,1024]{1,0:T(8,128)(2,1)S(1)} %collective-permute-done), channel_id=1, source_target_pairs={{0,2},{1,3},{2,0},{3,1},{4,6},{5,7},{6,4},{7,5},{8,10},{9,11},{10,... | collective-permute-start | bytes 1572872 | tf_op jit(solution)/shard_map/ppermute | solution.py:332
  56.2 40.2 %collective-permute-start.5 = (bf16[256,1024]{1,0:T(8,128)(2,1)}, bf16[256,1024]{1,0:T(8,128)(2,1)}, u32[]{:S(2)}, u32[]{:S(2)}) collective-permute-start(bf16[256,1024]{1,0:T(8,128)(2,1)} %collective-permute-done.4), channel_id=1, source_target_pairs={{0,1},{1,0},{2,3},{3,2},{4,5},{5,4},{6,7},{7,6},{8,9},{9,8},{10,11... | collective-permute-start | bytes 1572872 | tf_op jit(solution)/shard_map/ppermute | solution.py:332
  128.2 27.7 %all-to-all-start.1 = ((bf16[2,1024,256]{2,0,1:T(2,128)(2,1)}), bf16[2,1024,256]{2,0,1:T(2,128)(2,1)S(1)}, u32[]{:S(2)}, u32[]{:S(2)}) async-start(bf16[2,1024,256]{2,0,1:T(2,128)(2,1)} %copy.191), calls=%async_computation.1 | async-start | bytes 2097152 | tf_op jit(solution)/shard_map/all_to_all | solution.py:676
  243.3 46.5 %collective-permute-start.15 = (bf16[1024,512]{1,0:T(8,128)(2,1)S(1)}, bf16[1024,512]{1,0:T(8,128)(2,1)S(1)}, u32[]{:S(2)}, u32[]{:S(2)}) collective-permute-start(bf16[1024,512]{1,0:T(8,128)(2,1)S(1)} %bitcast.613), channel_id=1, source_target_pairs={{0,1},{1,0},{2,3},{3,2},{4,5},{5,4},{6,7},{7,6},{8,9},{9,8},{10,11... | collective-permute-start | bytes 3145736 | tf_op jit(solution)/shard_map/ppermute | solution.py:332
  244.5 45.3 %collective-permute-start.16 = (bf16[1024,512]{1,0:T(8,128)(2,1)S(1)}, bf16[1024,512]{1,0:T(8,128)(2,1)S(1)}, u32[]{:S(2)}, u32[]{:S(2)}) collective-permute-start(bf16[1024,512]{1,0:T(8,128)(2,1)S(1)} %bitcast.614), channel_id=1, source_target_pairs={{0,2},{1,3},{2,0},{3,1},{4,6},{5,7},{6,4},{7,5},{8,10},{9,11},{10,... | collective-permute-start | bytes 3145736 | tf_op jit(solution)/shard_map/ppermute | solution.py:332
  245.3 45.9 %collective-permute-start.17 = (bf16[1024,512]{1,0:T(8,128)(2,1)S(1)}, bf16[1024,512]{1,0:T(8,128)(2,1)S(1)}, u32[]{:S(2)}, u32[]{:S(2)}) collective-permute-start(bf16[1024,512]{1,0:T(8,128)(2,1)S(1)} %bitcast.615), channel_id=1, source_target_pairs={{0,3},{1,2},{2,1},{3,0},{4,7},{5,6},{6,5},{7,4},{8,11},{9,10},{10,... | collective-permute-start | bytes 3145736 | tf_op jit(solution)/shard_map/ppermute | solution.py:332
  329.2 34.1 %collective-permute-start.21 = (bf16[2,2,2,88,1024]{4,3,2,1,0:T(8,128)(2,1)S(1)}, bf16[2,2,2,88,1024]{4,3,2,1,0:T(8,128)(2,1)S(1)}, u32[]{:S(2)}, u32[]{:S(2)}) collective-permute-start(bf16[2,2,2,88,1024]{4,3,2,1,0:T(8,128)(2,1)S(1)} %copy-done.58), channel_id=1, source_target_pairs={{0,8},{4,12},{8,0},{12,4},{16,24},{20,28},{24,16},{28,20},{1,9},{5... | collective-permute-start | bytes 4325384 | tf_op jit(solution)/shard_map/ppermute | solution.py:332
  330.5 33.7 %collective-permute-start.22 = (bf16[2,2,2,32,2816]{4,3,1,0,2:T(8,128)(2,1)S(1)}, bf16[2,2,2,32,2816]{4,3,1,0,2:T(8,128)(2,1)S(1)}, u32[]{:S(2)}, u32[]{:S(2)}) collective-permute-start(bf16[2,2,2,32,2816]{4,3,1,0,2:T(8,128)(2,1)S(1)} %copy-done.57), channel_id=1, source_target_pairs={{0,1},{1,0},{2,3},{3,2},{4,5},{5,4},{6,7},{7,6},{8,9},{9,8},{10,11... | collective-permute-start | bytes 4325384 | tf_op jit(solution)/shard_map/ppermute | solution.py:332
  331.3 33.4 %collective-permute-start.23 = (bf16[2,2,2,32,2816]{4,3,1,0,2:T(8,128)(2,1)S(1)}, bf16[2,2,2,32,2816]{4,3,1,0,2:T(8,128)(2,1)S(1)}, u32[]{:S(2)}, u32[]{:S(2)}) collective-permute-start(bf16[2,2,2,32,2816]{4,3,1,0,2:T(8,128)(2,1)S(1)} %fusion.56), channel_id=1, source_target_pairs={{0,2},{1,3},{2,0},{3,1},{4,6},{5,7},{6,4},{7,5},{8,10},{9,11},{10,... | collective-permute-start | bytes 4325384 | tf_op jit(solution)/shard_map/ppermute | solution.py:332
  370.8 46.5 %collective-permute-start.27 = (bf16[2,2,2,2,32,2048]{5,4,3,2,1,0:T(8,128)(2,1)}, bf16[2,2,2,2,32,2048]{5,4,3,2,1,0:T(8,128)(2,1)}, u32[]{:S(2)}, u32[]{:S(2)}) collective-permute-start(bf16[2,2,2,2,32,2048]{5,4,3,2,1,0:T(8,128)(2,1)} %fusion.5), channel_id=1, source_target_pairs={{0,4},{4,0},{8,12},{12,8},{16,20},{20,16},{24,28},{28,24},{1,5},{5... | collective-permute-start | bytes 6291464 | tf_op jit(solution)/shard_map/ppermute | solution.py:332
  386.9 30.4 %collective-permute-start.28 = (bf16[2,2,2,2,32,1024]{5,4,3,2,1,0:T(8,128)(2,1)}, bf16[2,2,2,2,32,1024]{5,4,3,2,1,0:T(8,128)(2,1)}, u32[]{:S(2)}, u32[]{:S(2)}) collective-permute-start(bf16[2,2,2,2,32,1024]{5,4,3,2,1,0:T(8,128)(2,1)} %dynamic-slice_bitcast_fusion.2), channel_id=1, source_target_pairs={{0,4},{4,0},{8,12},{12,8},{16,20},{20,16},{24,28},{28,24},{1,5},{5... | collective-permute-start | bytes 3145736 | tf_op jit(solution)/shard_map/ppermute | solution.py:332
  400.6 49.3 %collective-permute-start.32 = (bf16[2,2,32,2816]{3,2,1,0:T(8,128)(2,1)}, bf16[2,2,32,2816]{3,2,1,0:T(8,128)(2,1)}, u32[]{:S(2)}, u32[]{:S(2)}) collective-permute-start(bf16[2,2,32,2816]{3,2,1,0:T(8,128)(2,1)} %get-tuple-element.168), channel_id=1, source_target_pairs={{0,2},{1,3},{2,0},{3,1},{4,6},{5,7},{6,4},{7,5},{8,10},{9,11},{10,... | collective-permute-start | bytes 2162696 | tf_op jit(solution)/shard_map/ppermute | solution.py:332
  402.1 47.8 %collective-permute-start.33 = (bf16[2,2,32,2816]{3,2,1,0:T(8,128)(2,1)}, bf16[2,2,32,2816]{3,2,1,0:T(8,128)(2,1)}, u32[]{:S(2)}, u32[]{:S(2)}) collective-permute-start(bf16[2,2,32,2816]{3,2,1,0:T(8,128)(2,1)} %get-tuple-element.169), channel_id=1, source_target_pairs={{0,1},{1,0},{2,3},{3,2},{4,5},{5,4},{6,7},{7,6},{8,9},{9,8},{10,11... | collective-permute-start | bytes 2162696 | tf_op jit(solution)/shard_map/ppermute | solution.py:332
  407.2 54.3 %collective-permute-start.34 = (bf16[2,2,88,1024]{3,2,1,0:T(8,128)(2,1)}, bf16[2,2,88,1024]{3,2,1,0:T(8,128)(2,1)}, u32[]{:S(2)}, u32[]{:S(2)}) collective-permute-start(bf16[2,2,88,1024]{3,2,1,0:T(8,128)(2,1)} %fusion.59), channel_id=1, source_target_pairs={{0,16},{4,20},{8,24},{12,28},{16,0},{20,4},{24,8},{28,12},{1,17},{... | collective-permute-start | bytes 2162696 | tf_op jit(solution)/shard_map/ppermute | solution.py:332
  451.9 35.7 %collective-permute-start.29 = (bf16[2,256,512]{2,1,0:T(8,128)(2,1)}, bf16[2,256,512]{2,1,0:T(8,128)(2,1)}, u32[]{:S(2)}, u32[]{:S(2)}) collective-permute-start(bf16[2,256,512]{2,1,0:T(8,128)(2,1)} %get-tuple-element.164), channel_id=1, source_target_pairs={{0,1},{1,0},{2,3},{3,2},{4,5},{5,4},{6,7},{7,6},{8,9},{9,8},{10,11... | collective-permute-start | bytes 1572872 | tf_op jit(solution)/shard_map/ppermute | solution.py:332
  465.4 31.3 %collective-permute-start.31 = (bf16[2,256,512]{2,1,0:T(8,128)(2,1)}, bf16[2,256,512]{2,1,0:T(8,128)(2,1)}, u32[]{:S(2)}, u32[]{:S(2)}) collective-permute-start(bf16[2,256,512]{2,1,0:T(8,128)(2,1)} %get-tuple-element.166), channel_id=1, source_target_pairs={{0,3},{1,2},{2,1},{3,0},{4,7},{5,6},{6,5},{7,4},{8,11},{9,10},{10,... | collective-permute-start | bytes 1572872 | tf_op jit(solution)/shard_map/ppermute | solution.py:332
  499.7 26.6 %collective-permute-start.40 = (bf16[2,32,5632]{2,1,0:T(8,128)(2,1)}, bf16[2,32,5632]{2,1,0:T(8,128)(2,1)}, u32[]{:S(2)}, u32[]{:S(2)}) collective-permute-start(bf16[2,32,5632]{2,1,0:T(8,128)(2,1)} %fusion.68), channel_id=1, source_target_pairs={{0,8},{4,12},{8,0},{12,4},{16,24},{20,28},{24,16},{28,20},{1,9},{5... | collective-permute-start | bytes 2162696 | tf_op jit(solution)/shard_map/ppermute | solution.py:332
  548.0 33.3 %collective-permute-start.53 = (bf16[32,5632]{1,0:T(8,128)(2,1)}, bf16[32,5632]{1,0:T(8,128)(2,1)}, u32[]{:S(2)}, u32[]{:S(2)}) collective-permute-start(bf16[32,5632]{1,0:T(8,128)(2,1)} %fusion.73), channel_id=1, source_target_pairs={{0,16},{4,20},{8,24},{12,28},{16,0},{20,4},{24,8},{28,12},{1,17},{... | collective-permute-start | bytes 1081352 | tf_op jit(solution)/shard_map/ppermute | solution.py:332
  (147 other events, 1628.6 us)
Sparse Core Ops, SparseCore 0:
  11.6 196.1 all-gather.1

commit v4 on v3

--- a/solution.py
+++ b/solution.py
@@ -705,8 +705,7 @@
     cross_cots = tick(cross_cots, chain_r, chain_g, chain_u)
     cross_dq, mdk, mdv = cross_attention_back(cross_q, mk, mv, cross_cots, segments, all_memory_segments)
     mdkv = jnp.concatenate([mdk, mdv], axis=2).reshape(rows, seq_count, memory_part, -1)
-    mdkv = absolute(mdkv.swapaxes(0, 1), "seq")
-    mdkv = [mdkv[0]] + [flip(mdkv[j], "seq", j) for j in range(1, seq_count)]
+    mdkv = lax.all_to_all(mdkv, "seq", split_axis=1, concat_axis=1, tiled=True)
     cross_dq = cross_dq.reshape(-1, width)
     part_one, gain_one = norm_back(hidden_one, inv_one, gain_values[1], nt(cross_dq, w_q1))
     hidden_one_grad = hidden_two_grad + part_one
@@ -716,39 +715,43 @@
     chain_o1 = chain_of(tn(cross_flat, cross_out_grad).astype(BF16))
     chain_q1 = chain_of(tn(normed_one, cross_dq).astype(BF16))
     chain_a = joined([chain_o1, chain_q1], chain_o1.order)
+    mdkv = jnp.sum(mdkv.astype(F32), axis=1).astype(BF16).reshape(rows * memory_part, -1)
+    memory_grad = nt(mdkv, w_kv1).reshape(memory.shape)
     chain_o0 = chain_of(tn(context, self_out_grad).astype(BF16), turned=True)
-    cots = tick(cots, chain_r, chain_g, chain_u, chain_a, chain_o0)
+    chain_k1 = chain_of(tn(mem, mdkv).astype(BF16), turned=True)
+    chain_b = joined([chain_o0, chain_k1], chain_o0.order)
+    cots = tick(cots, chain_a, chain_b)
     head_cots = lax.all_to_all(cots, "seq", split_axis=2, concat_axis=1, tiled=True)
-    head_cots, mdkv = settle(head_cots, mdkv)
-    mdkv = sum(m.astype(F32) for m in mdkv).astype(BF16).reshape(rows * memory_part, -1)
-    memory_grad = nt(mdkv, w_kv1).reshape(memory.shape)
-    chain_k1 = chain_of(tn(mem, mdkv).astype(BF16), turned=True)
-    head_cots, memory_grad = tick((head_cots, memory_grad), chain_a, chain_o0, chain_k1)
+    head_cots, memory_grad = tick((head_cots, memory_grad), chain_r, chain_g, chain_u, chain_a, chain_b)
     head_grads, lag_sums = self_attention_back(head_qkv, head_cots, lse, all_segments, base)
-    relative = absolute(head_grads.reshape(rows, seq_count, part, cols).swapaxes(0, 1), "seq")
-    lag_sums, *relative = settle(lag_sums, *relative)
-    came = [relative[0]] + [flip(relative[j], "seq", j) for j in range(1, seq_count)]
+    by_place = head_grads.reshape(rows, seq_count, part, cols)
+    relative = absolute(by_place.swapaxes(0, 1), "seq")
     batch_bits = [("batch", b) for b in reversed(range(bit_count("batch")))]
     all_grads = jnp.stack(relative).reshape(-1, cols)
     chain_f = Chain(tn(all_normed, all_grads).astype(BF16), batch_bits, hops(False, False)[: len(batch_bits)])
-    lag_sums = land(lag_sums, chain_g, chain_u)
+    by_place, lag_sums = land((by_place, lag_sums), chain_g, chain_u)
     while chain_g.order[0][0] == "seq":
-        lag_sums = land(tick(lag_sums, chain_g, chain_u), chain_g, chain_u)
+        by_place, lag_sums = land(tick((by_place, lag_sums), chain_g, chain_u), chain_g, chain_u)
     chain_gu = joined([chain_g, chain_u], chain_g.order)
-    chains = (chain_f, chain_gu, chain_r, chain_a, chain_o0, chain_k1)
-    lag_sums = tick(lag_sums, *chains)
-    dqkv = jnp.concatenate(came, axis=-1).reshape(rows * part, -1)
+    chains = (chain_f, chain_gu, chain_r, chain_a, chain_b)
+    by_place, lag_sums = tick((by_place, lag_sums), *chains)
+    dqkv = lax.all_to_all(by_place, "seq", split_axis=1, concat_axis=1, tiled=True)
+    dqkv = jnp.concatenate(absolute(dqkv.swapaxes(0, 1), "seq"), axis=-1).reshape(rows * part, -1)
     dqkv = tick(dqkv, chain_f)
     part_zero, gain_zero = norm_back(x, inv_zero, gain_values[0], nt(dqkv, w_first))
     input_grad = (hidden_one_grad + part_zero).reshape(tokens.shape)
+    input_grad = land(input_grad, chain_a, chain_b)
+    while chain_a.order[0][0] == "seq":
+        input_grad = land(tick(input_grad, chain_a, chain_b), chain_a, chain_b)
+    chain_ab = joined([chain_a, chain_b], chain_a.order)
+    chains = (chain_f, chain_gu, chain_r, chain_ab)
     input_grad = tick(input_grad, *chains)
     for chain in chains:
         chain.finish()
     grad_gu, grad_reduce = chain_gu.result(), chain_r.result()
     grad_gate, grad_up = grad_gu[:, :ff], grad_gu[:, ff:]
-    grad_a = chain_a.result()
-    grad_o0, grad_k1 = chain_o0.result(), chain_k1.result()
-    grad_o1, grad_q1 = grad_a[:, :width], grad_a[:, width:]
+    grad_ab = chain_ab.result()
+    grad_o1, grad_q1, grad_o0, grad_k1 = (grad_ab[:, i * width : (i + 1) * width] for i in range(4))
     first_grads = lax.all_to_all(chain_f.result().reshape(seq_count, own, cols), "seq", 0, 0, tiled=True)
     first_grads = first_grads.transpose(1, 0, 2)
 

time: 612 us -> 593 us (0.969)
  waiting for transfers between devices: 202 us -> 188 us
  local copies, waits for them, and re-layouts: 55.5 us -> 63.7 us
  other arithmetic: 95.3 us -> 87.8 us
    ppermute x55 -> x42, waiting for transfers between devices: 120 us -> 69.4 us  [flip(): lax.ppermute(value, axis, [(i, i ^ mask) for i in range(lax.axis_size(axi...]
    all_to_all x1, waiting for transfers between devices: 6.84 us -> 28.3 us  [shards(): lax.all_to_all(cots, 'seq', split_axis=2, concat_axis=1, tiled=True)]
    all_to_all x0 -> x2, waiting for transfers between devices: none -> 13.3 us  [the longest x1 11 us: shards(): lax.all_to_all(by_place, 'seq', split_axis=1, concat_axis=1, tiled=True)]
    ppermute x55 -> x42, starting transfers between devices: 59 us -> 48.5 us  [flip(): lax.ppermute(value, axis, [(i, i ^ mask) for i in range(lax.axis_size(axi...]
    all_to_all x0 -> x2, starting transfers between devices: none -> 9.15 us  [the longest x1 4.7 us: shards(): lax.all_to_all(by_place, 'seq', split_axis=1, concat_axis=1, tiled=True)]
    convert_element_type x22 -> x15, other arithmetic: 44 us -> 37.6 us  [outgoing(): sum((p.astype(F32) for p in self.half(1 - my_bit(*self.order[0]))))]
    unnamed x235 -> x236, local copies, waits for them, and re-layouts: 9.77 us -> 12.5 us
    squeeze x7 -> x6, local copies, waits for them, and re-layouts: 11.6 us -> 13.3 us  [half(): lax.dynamic_index_in_dim(p, choice, where, False)]
  transfers between devices with their start and end apart: 61 -> 50, of which waited for: 23 -> 15; matrix products, arithmetic and copies ran while one was open for 25% -> 21% of each run, Pallas kernels for 14% -> 14%
where the time goes in v4:
time: 593 us; the launch traced here: 585 us
  waiting for transfers between devices  188 us (32%)
  Pallas kernels  109 us (18%)
  other arithmetic  87.8 us (15%)
  starting transfers between devices  75.3 us (13%)
  local copies, waits for them, and re-layouts  63.7 us (11%)
  matrix products  45 us (8%)
  between operations  16.4 us (3%)
    ppermute x42, waiting for transfers between devices, flip(): lax.ppermute(value, axis, [(i, i ^ mask) for i in range(lax.axis_size(axi...  69.4 us
    ppermute x42, starting transfers between devices, flip(): lax.ppermute(value, axis, [(i, i ^ mask) for i in range(lax.axis_size(axi...  48.5 us
    all_gather x1, waiting for transfers between devices, shards(): lax.all_gather(jnp.concatenate(pieces, axis=1), every, axis=0, tiled=True)  48.1 us
    pallas_call x1, Pallas kernels, feed_forward(): pl.pallas_call(functools.partial(ffn_kernel, core_rows=core_rows), grid=(...  38.8 us
    convert_element_type x15, other arithmetic, outgoing(): sum((p.astype(F32) for p in self.half(1 - my_bit(*self.order[0]))))  37.6 us
    all_to_all x1, waiting for transfers between devices, shards(): lax.all_to_all(cots, 'seq', split_axis=2, concat_axis=1, tiled=True)  28.3 us
    pallas_call x1, Pallas kernels, self_attention_back(): pl.pallas_call(self_bwd_kernel, grid=(rows,), in_specs=[all_spec, queries...  26.4 us
    all_to_all x1, waiting for transfers between devices, shards(): lax.all_to_all(head_context, 'seq', split_axis=1, concat_axis=2, tiled=True)  23.2 us
  transfers between devices with their start and end apart: 50, of which 15 were waited for; matrix products, arithmetic and copies ran while one was open for 21% of the time, Pallas kernels for 14%

profile of v4, /device:TPU:0, one launch (start us, length us, event | category | flops | bytes accessed | tf_op | source)
XLA Modules:
  0.0 585.3 jit_solution(619773130180790050)
XLA Ops:
  11.6 4.0 collective-permute-start.11
  25.2 4.6 gather_fusion
  33.7 16.5 %collective-permute-done.6 = bf16[4,40,512]{2,1,0:T(8,128)(2,1)S(1)} collective-permute-done((bf16[4,40,512]{2,1,0:T(8,128)(2,1)S(1)}, bf16[4,40,512]{2,1,0:T(8,128)(2,1)S(1)}, u32[]{:S(2)}, u32[]{:S(2)}) %collective-permute-start.6) | collective-permute-done | bytes 163872 | tf_op jit(solution)/shard_map/ppermute | solution.py:332
  57.1 17.6 %collective-permute-done.7 = bf16[2,4,40,512]{3,2,1,0:T(8,128)(2,1)} collective-permute-done((bf16[2,4,40,512]{3,2,1,0:T(8,128)(2,1)S(1)}, bf16[2,4,40,512]{3,2,1,0:T(8,128)(2,1)}, u32[]{:S(2)}, u32[]{:S(2)}) %collective-permute-start.7) | collective-permute-done | bytes 327712 | tf_op jit(solution)/shard_map/ppermute | solution.py:332
  75.9 17.4 %collective-permute-done.5 = bf16[256,1024]{1,0:T(8,128)(2,1)} collective-permute-done((bf16[256,1024]{1,0:T(8,128)(2,1)S(1)}, bf16[256,1024]{1,0:T(8,128)(2,1)}, u32[]{:S(2)}, u32[]{:S(2)}) %collective-permute-start.5) | collective-permute-done | bytes 524320 | tf_op jit(solution)/shard_map/ppermute | solution.py:332
  106.6 18.4 %self_attention.1 = (bf16[2,1024,256]{2,1,0:T(8,128)(2,1)S(1)}, f32[2,1024,4]{2,1,0:T(8,128)S(1)}) custom-call(bf16[2,1024,512]{2,1,0:T(8,128)(2,1)S(1)} %bitcast.465, s32[2,1,1024]{2,1,0:T(1,128)S(1)} %broadcast_in_dim_reshape.12.seg_row_ref, s32[2,1024,1]{2,1,0:T(8,128)S(1)} %broadcast_in_dim_reshape.15.seg_col_ref, ...), custom_call_target="tpu_custom_call" | custom-call | flops 805306368 | bytes 4194304 | tf_op jit(solution)/shard_map/self_attention/pallas_call | solution.py:175
  127.1 4.0 all-to-all-start.1
  132.1 23.2 %all-to-all-done.1 = bf16[2,1024,256]{2,0,1:T(2,128)(2,1)S(1)} async-done(((bf16[2,1024,256]{2,0,1:T(2,128)(2,1)}), bf16[2,1024,256]{2,0,1:T(2,128)(2,1)S(1)}, u32[]{:S(2)}, u32[]{:S(2)}) %all-to-all-start.1) | async-done | bytes 1048608 | tf_op jit(solution)/shard_map/all_to_all | solution.py:676
  157.3 48.1 %all-gather.2.cloned.1.call-done.wg_ref.wu_ref = bf16[1024,12800]{1,0:T(8,128)(2,1)} async-done(((bf16[32,12800]{1,0:T(8,128)(2,1)}), bf16[1024,12800]{1,0:T(8,128)(2,1)}) %all-gather.2.cloned.1.call-update) | async-done | bytes 26214416 | tf_op jit(solution)/shard_map/all_gather | solution.py:649
  214.1 4.3 fusion.136
  225.1 11.2 %cross_attention.1 = bf16[2,256,1024]{2,1,0:T(8,128)(2,1)S(1)} custom-call(bf16[2,256,1024]{2,1,0:T(8,128)(2,1)S(1)} %bitcast.468, bf16[2,256,512]{2,1,0:T(8,128)(2,1)S(1)} %get-tuple-element.324.k_ref, bf16[2,256,512]{2,1,0:T(8,128)(2,1)S(1)} %get-tuple-element.323.v_ref, s32[2,1,256]{2,1,0:T(1,128)S(1)} %broadcast_in_dim_reshape.14.seg_row_ref, ...), custom_call_target="tpu_custom_call" | custom-call | flops 536870912 | bytes 3145728 | tf_op jit(solution)/shard_map/cross_attention/pallas_call | solution.py:288
  236.3 4.6 fusion.45.h_ref
  244.4 38.8 %feed_forward.1 = (bf16[512,1024]{1,0:T(8,128)(2,1)}, f32[512,1024]{1,0:T(8,128)}, f32[1,1024]{1,0:T(1,128)}, bf16[512,2816]{1,0:T(8,128)(2,1)}, bf16[512,2816]{...) custom-call(s32[1]{0:T(128)} %bitcast.core_ref, ...), custom_call_target="tpu_custom_call" | custom-call | flops 26575110144 | bytes 34603008 | tf_op jit(solution)/shard_map/feed_forward/pallas_call | solution.py:550
  291.0 4.6 convolution_convert_fusion.3
  308.2 14.7 %cross_attention_back.1 = (bf16[2,256,1024]{2,1,0:T(8,128)(2,1)S(1)}, bf16[2,256,512]{2,1,0:T(8,128)(2,1)S(1)}, bf16[2,256,512]{2,1,0:T(8,128)(2,1)S(1)}) custom-call(bf16[2,256,1024]{2,1,0:T(8,128)(2,1)S(1)} %bitcast.469, bf16[2,256,512]{2,1,0:T(8,128)(2,1)S(1)} %get-tuple-element.324.k_ref, bf16[2,256,512]{2,1,0:T(8,128)(2,1)S(1)} %get-tuple-element.323.v_ref, ...), custom_call_target="tpu_custom_call" | custom-call | flops 1342177280 | bytes 5242880 | tf_op jit(solution)/shard_map/cross_attention_back/pallas_call | solution.py:305
  322.9 4.8 multiply_reduce_fusion
  328.9 4.4 all-to-all-start.2
  336.1 4.7 fusion.48
  374.0 28.3 %all-to-all-done.3 = bf16[2,256,1024]{1,0,2:T(2,128)(2,1)S(1)} async-done(((bf16[2,256,1024]{1,0,2:T(2,128)(2,1)}), bf16[2,256,1024]{1,0,2:T(2,128)(2,1)S(1)}, u32[]{:S(2)}, u32[]{:S(2)}) %all-to-all-start.3) | async-done | bytes 1048608 | tf_op jit(solution)/shard_map/all_to_all | solution.py:724
  425.4 26.4 %self_attention_back.1 = (bf16[2,1024,512]{2,1,0:T(8,128)(2,1)S(1)}, f32[4,1152]{1,0:T(4,128)S(1)}) custom-call(bf16[2,1024,512]{2,1,0:T(8,128)(2,1)} %bitcast.466, bf16[2,1024,256]{2,1,0:T(8,128)(2,1)S(1)} %bitcast.467, f32[2,1024,4]{2,1,0:T(8,128)S(1)} %copy-done.8, s32[2,1,1024]{2,1,0:T(1,128)S(1)} %broadcast_in_dim_reshape.12.seg_row_ref, ...), custom_call_target="tpu_custom_call" | custom-call | flops 2013265920 | bytes 6291456 | tf_op jit(solution)/shard_map/self_attention_back/pallas_call | solution.py:199
  469.5 4.7 all-to-all-start.4
  489.6 11.0 %all-to-all-done.4 = bf16[2,4,256,512]{3,2,0,1:T(8,128)(2,1)} async-done(((bf16[2,4,256,512]{3,2,0,1:T(8,128)(2,1)}), bf16[2,4,256,512]{3,2,0,1:T(8,128)(2,1)}, u32[]{:S(2)}, u32[]{:S(2)}) %all-to-all-start.4) | async-done | bytes 2097184 | tf_op jit(solution)/shard_map/all_to_all | solution.py:738
  541.1 4.3 all-to-all-start.5
  562.9 9.9 %collective-permute-done.39 = bf16[32,4096]{1,0:T(8,128)(2,1)S(1)} collective-permute-done((bf16[32,4096]{1,0:T(8,128)(2,1)S(1)}, bf16[32,4096]{1,0:T(8,128)(2,1)S(1)}, u32[]{:S(2)}, u32[]{:S(2)}) %collective-permute-start.39) | collective-permute-done | bytes 262176 | tf_op jit(solution)/shard_map/ppermute | solution.py:332
  (509 shorter events, 238.5 us)
Async XLA Ops:
  7.2 198.2 %all-gather.2.cloned.1.call-start = ((), (), s32[]{:S(2)}) async-start(), calls=%async_computation.7 | async-start | bytes 27033600 | tf_op jit(solution)/shard_map/all_gather | solution.py:649
  11.6 39.9 %collective-permute-start.11 = (s32[2,320]{1,0:T(2,128)S(1)}, s32[2,320]{1,0:T(2,128)S(1)}, u32[]{:S(2)}, u32[]{:S(2)}) collective-permute-start(s32[2,320]{1,0:T(2,128)S(1)} %constant_dynamic-update-slice_fusion), channel_id=1, source_target_pairs={{0,3},{1,2},{2,1},{3,0},{4,7},{5,6},{6,5},{7,4},{8,11},{9,10},{10,... | collective-permute-start | bytes 7688 | tf_op jit(solution)/shard_map/ppermute | solution.py:332
  15.5 36.9 %collective-permute-start.10 = (s32[2,320]{1,0:T(2,128)S(1)}, s32[2,320]{1,0:T(2,128)S(1)}, u32[]{:S(2)}, u32[]{:S(2)}) collective-permute-start(s32[2,320]{1,0:T(2,128)S(1)} %constant_dynamic-update-slice_fusion), channel_id=1, source_target_pairs={{0,2},{1,3},{2,0},{3,1},{4,6},{5,7},{6,4},{7,5},{8,10},{9,11},{10,... | collective-permute-start | bytes 7688 | tf_op jit(solution)/shard_map/ppermute | solution.py:332
  21.7 32.2 %collective-permute-start.4 = (bf16[256,1024]{1,0:T(8,128)(2,1)S(1)}, bf16[256,1024]{1,0:T(8,128)(2,1)S(1)}, u32[]{:S(2)}, u32[]{:S(2)}) collective-permute-start(bf16[256,1024]{1,0:T(8,128)(2,1)S(1)} %get-tuple-element.330), channel_id=1, source_target_pairs={{0,2},{1,3},{2,0},{3,1},{4,6},{5,7},{6,4},{7,5},{8,10},{9,11},{10,... | collective-permute-start | bytes 1572872 | tf_op jit(solution)/shard_map/ppermute | solution.py:332
  23.7 31.4 %collective-permute-start = (bf16[256,1024]{1,0:T(8,128)(2,1)}, bf16[256,1024]{1,0:T(8,128)(2,1)}, u32[]{:S(2)}, u32[]{:S(2)}) collective-permute-start(bf16[256,1024]{1,0:T(8,128)(2,1)} %get-tuple-element.331), channel_id=1, source_target_pairs={{0,1},{1,0},{2,3},{3,2},{4,5},{5,4},{6,7},{7,6},{8,9},{9,8},{10,11... | collective-permute-start | bytes 1572872 | tf_op jit(solution)/shard_map/ppermute | solution.py:332
  52.4 42.8 %collective-permute-start.1 = (bf16[256,1024]{1,0:T(8,128)(2,1)}, bf16[256,1024]{1,0:T(8,128)(2,1)}, u32[]{:S(2)}, u32[]{:S(2)}) collective-permute-start(bf16[256,1024]{1,0:T(8,128)(2,1)} %get-tuple-element.331), channel_id=1, source_target_pairs={{0,2},{1,3},{2,0},{3,1},{4,6},{5,7},{6,4},{7,5},{8,10},{9,11},{10,... | collective-permute-start | bytes 1572872 | tf_op jit(solution)/shard_map/ppermute | solution.py:332
  53.9 39.5 %collective-permute-start.5 = (bf16[256,1024]{1,0:T(8,128)(2,1)S(1)}, bf16[256,1024]{1,0:T(8,128)(2,1)}, u32[]{:S(2)}, u32[]{:S(2)}) collective-permute-start(bf16[256,1024]{1,0:T(8,128)(2,1)S(1)} %collective-permute-done.4), channel_id=1, source_target_pairs={{0,1},{1,0},{2,3},{3,2},{4,5},{5,4},{6,7},{7,6},{8,9},{9,8},{10,11... | collective-permute-start | bytes 1572872 | tf_op jit(solution)/shard_map/ppermute | solution.py:332
  55.1 40.1 %collective-permute-start.2 = (bf16[256,1024]{1,0:T(8,128)(2,1)}, bf16[256,1024]{1,0:T(8,128)(2,1)}, u32[]{:S(2)}, u32[]{:S(2)}) collective-permute-start(bf16[256,1024]{1,0:T(8,128)(2,1)} %collective-permute-done), channel_id=1, source_target_pairs={{0,2},{1,3},{2,0},{3,1},{4,6},{5,7},{6,4},{7,5},{8,10},{9,11},{10,... | collective-permute-start | bytes 1572872 | tf_op jit(solution)/shard_map/ppermute | solution.py:332
  240.9 46.7 %collective-permute-start.17 = (bf16[1024,512]{1,0:T(8,128)(2,1)S(1)}, bf16[1024,512]{1,0:T(8,128)(2,1)S(1)}, u32[]{:S(2)}, u32[]{:S(2)}) collective-permute-start(bf16[1024,512]{1,0:T(8,128)(2,1)S(1)} %bitcast.520), channel_id=1, source_target_pairs={{0,3},{1,2},{2,1},{3,0},{4,7},{5,6},{6,5},{7,4},{8,11},{9,10},{10,... | collective-permute-start | bytes 3145736 | tf_op jit(solution)/shard_map/ppermute | solution.py:332
  242.1 46.7 %collective-permute-start.16 = (bf16[1024,512]{1,0:T(8,128)(2,1)S(1)}, bf16[1024,512]{1,0:T(8,128)(2,1)S(1)}, u32[]{:S(2)}, u32[]{:S(2)}) collective-permute-start(bf16[1024,512]{1,0:T(8,128)(2,1)S(1)} %bitcast.521), channel_id=1, source_target_pairs={{0,2},{1,3},{2,0},{3,1},{4,6},{5,7},{6,4},{7,5},{8,10},{9,11},{10,... | collective-permute-start | bytes 3145736 | tf_op jit(solution)/shard_map/ppermute | solution.py:332
  243.2 45.6 %collective-permute-start.15 = (bf16[1024,512]{1,0:T(8,128)(2,1)S(1)}, bf16[1024,512]{1,0:T(8,128)(2,1)S(1)}, u32[]{:S(2)}, u32[]{:S(2)}) collective-permute-start(bf16[1024,512]{1,0:T(8,128)(2,1)S(1)} %bitcast.522), channel_id=1, source_target_pairs={{0,1},{1,0},{2,3},{3,2},{4,5},{5,4},{6,7},{7,6},{8,9},{9,8},{10,11... | collective-permute-start | bytes 3145736 | tf_op jit(solution)/shard_map/ppermute | solution.py:332
  353.8 51.2 %collective-permute-start.24 = (bf16[2,2,2,2,32,2048]{5,4,3,2,1,0:T(8,128)(2,1)}, bf16[2,2,2,2,32,2048]{5,4,3,2,1,0:T(8,128)(2,1)}, u32[]{:S(2)}, u32[]{:S(2)}) collective-permute-start(bf16[2,2,2,2,32,2048]{5,4,3,2,1,0:T(8,128)(2,1)} %fusion.6), channel_id=1, source_target_pairs={{0,4},{4,0},{8,12},{12,8},{16,20},{20,16},{24,28},{28,24},{1,5},{5... | collective-permute-start | bytes 6291464 | tf_op jit(solution)/shard_map/ppermute | solution.py:332
  353.8 51.2 %collective-permute-start.25 = (bf16[2,2,2,2,32,2048]{5,4,1,0,3,2:T(8,128)(2,1)}, bf16[2,2,2,2,32,2048]{5,4,1,0,3,2:T(8,128)(2,1)}, u32[]{:S(2)}, u32[]{:S(2)}) collective-permute-start(bf16[2,2,2,2,32,2048]{5,4,1,0,3,2:T(8,128)(2,1)} %copy_bitcast_fusion), channel_id=1, source_target_pairs={{0,4},{4,0},{8,12},{12,8},{16,20},{20,16},{24,28},{28,24},{1,5},{5... | collective-permute-start | bytes 6291464 | tf_op jit(solution)/shard_map/ppermute | solution.py:332
  354.3 50.6 %collective-permute-start.21 = (bf16[2,2,2,88,1024]{4,3,2,1,0:T(8,128)(2,1)}, bf16[2,2,2,88,1024]{4,3,2,1,0:T(8,128)(2,1)}, u32[]{:S(2)}, u32[]{:S(2)}) collective-permute-start(bf16[2,2,2,88,1024]{4,3,2,1,0:T(8,128)(2,1)} %fusion.3), channel_id=1, source_target_pairs={{0,8},{4,12},{8,0},{12,4},{16,24},{20,28},{24,16},{28,20},{1,9},{5... | collective-permute-start | bytes 4325384 | tf_op jit(solution)/shard_map/ppermute | solution.py:332
  356.5 48.5 %collective-permute-start.22 = (bf16[2,2,2,32,2816]{4,3,1,0,2:T(8,128)(2,1)}, bf16[2,2,2,32,2816]{4,3,1,0,2:T(8,128)(2,1)}, u32[]{:S(2)}, u32[]{:S(2)}) collective-permute-start(bf16[2,2,2,32,2816]{4,3,1,0,2:T(8,128)(2,1)} %fusion.57), channel_id=1, source_target_pairs={{0,1},{1,0},{2,3},{3,2},{4,5},{5,4},{6,7},{7,6},{8,9},{9,8},{10,11... | collective-permute-start | bytes 4325384 | tf_op jit(solution)/shard_map/ppermute | solution.py:332
  357.9 47.0 %collective-permute-start.23 = (bf16[2,2,2,32,2816]{4,3,1,0,2:T(8,128)(2,1)}, bf16[2,2,2,32,2816]{4,3,1,0,2:T(8,128)(2,1)}, u32[]{:S(2)}, u32[]{:S(2)}) collective-permute-start(bf16[2,2,2,32,2816]{4,3,1,0,2:T(8,128)(2,1)} %fusion.58), channel_id=1, source_target_pairs={{0,2},{1,3},{2,0},{3,1},{4,6},{5,7},{6,4},{7,5},{8,10},{9,11},{10,... | collective-permute-start | bytes 4325384 | tf_op jit(solution)/shard_map/ppermute | solution.py:332
  362.1 40.1 %all-to-all-start.3 = ((bf16[2,256,1024]{1,0,2:T(2,128)(2,1)}), bf16[2,256,1024]{1,0,2:T(2,128)(2,1)S(1)}, u32[]{:S(2)}, u32[]{:S(2)}) async-start(bf16[2,256,1024]{1,0,2:T(2,128)(2,1)} %copy.179), calls=%async_computation.3 | async-start | bytes 2097152 | tf_op jit(solution)/shard_map/all_to_all | solution.py:724
  419.0 40.0 %collective-permute-start.26 = (bf16[2,2,32,2816]{3,2,1,0:T(8,128)(2,1)}, bf16[2,2,32,2816]{3,2,1,0:T(8,128)(2,1)S(1)}, u32[]{:S(2)}, u32[]{:S(2)}) collective-permute-start(bf16[2,2,32,2816]{3,2,1,0:T(8,128)(2,1)} %fusion.60), channel_id=1, source_target_pairs={{0,2},{1,3},{2,0},{3,1},{4,6},{5,7},{6,4},{7,5},{8,10},{9,11},{10,... | collective-permute-start | bytes 2162696 | tf_op jit(solution)/shard_map/ppermute | solution.py:332
  419.7 39.3 %collective-permute-start.27 = (bf16[2,2,32,2816]{3,2,1,0:T(8,128)(2,1)}, bf16[2,2,32,2816]{3,2,1,0:T(8,128)(2,1)}, u32[]{:S(2)}, u32[]{:S(2)}) collective-permute-start(bf16[2,2,32,2816]{3,2,1,0:T(8,128)(2,1)} %fusion.59), channel_id=1, source_target_pairs={{0,1},{1,0},{2,3},{3,2},{4,5},{5,4},{6,7},{7,6},{8,9},{9,8},{10,11... | collective-permute-start | bytes 2162696 | tf_op jit(solution)/shard_map/ppermute | solution.py:332
  421.1 41.5 %collective-permute-start.28 = (bf16[2,2,88,1024]{3,2,1,0:T(8,128)(2,1)}, bf16[2,2,88,1024]{3,2,1,0:T(8,128)(2,1)}, u32[]{:S(2)}, u32[]{:S(2)}) collective-permute-start(bf16[2,2,88,1024]{3,2,1,0:T(8,128)(2,1)} %fusion.61), channel_id=1, source_target_pairs={{0,16},{4,20},{8,24},{12,28},{16,0},{20,4},{24,8},{28,12},{1,17},{... | collective-permute-start | bytes 2162696 | tf_op jit(solution)/shard_map/ppermute | solution.py:332
  423.4 39.2 %collective-permute-start.29 = (bf16[2,2,2,32,2048]{4,3,1,0,2:T(8,128)(2,1)}, bf16[2,2,2,32,2048]{4,3,1,0,2:T(8,128)(2,1)}, u32[]{:S(2)}, u32[]{:S(2)}) collective-permute-start(bf16[2,2,2,32,2048]{4,3,1,0,2:T(8,128)(2,1)} %fusion.16), channel_id=1, source_target_pairs={{0,1},{1,0},{2,3},{3,2},{4,5},{5,4},{6,7},{7,6},{8,9},{9,8},{10,11... | collective-permute-start | bytes 3145736 | tf_op jit(solution)/shard_map/ppermute | solution.py:332
  424.0 38.6 %collective-permute-start.30 = (bf16[2,2,2,32,2048]{4,3,1,0,2:T(8,128)(2,1)}, bf16[2,2,2,32,2048]{4,3,1,0,2:T(8,128)(2,1)}, u32[]{:S(2)}, u32[]{:S(2)}) collective-permute-start(bf16[2,2,2,32,2048]{4,3,1,0,2:T(8,128)(2,1)} %fusion.15), channel_id=1, source_target_pairs={{0,2},{1,3},{2,0},{3,1},{4,6},{5,7},{6,4},{7,5},{8,10},{9,11},{10,... | collective-permute-start | bytes 3145736 | tf_op jit(solution)/shard_map/ppermute | solution.py:332
  484.1 40.6 %collective-permute-start.35 = (bf16[2,32,5632]{2,1,0:T(8,128)(2,1)}, bf16[2,32,5632]{2,1,0:T(8,128)(2,1)}, u32[]{:S(2)}, u32[]{:S(2)}) collective-permute-start(bf16[2,32,5632]{2,1,0:T(8,128)(2,1)} %fusion.69), channel_id=1, source_target_pairs={{0,8},{4,12},{8,0},{12,4},{16,24},{20,28},{24,16},{28,20},{1,9},{5... | collective-permute-start | bytes 2162696 | tf_op jit(solution)/shard_map/ppermute | solution.py:332
  485.7 39.0 %collective-permute-start.36 = (bf16[2,88,1024]{2,1,0:T(8,128)(2,1)}, bf16[2,88,1024]{2,1,0:T(8,128)(2,1)}, u32[]{:S(2)}, u32[]{:S(2)}) collective-permute-start(bf16[2,88,1024]{2,1,0:T(8,128)(2,1)} %fusion.75), channel_id=1, source_target_pairs={{0,1},{1,0},{2,3},{3,2},{4,5},{5,4},{6,7},{7,6},{8,9},{9,8},{10,11... | collective-permute-start | bytes 1081352 | tf_op jit(solution)/shard_map/ppermute | solution.py:332
  (136 other events, 1306.5 us)
Sparse Core Ops, SparseCore 0:
  11.6 193.7 all-gather.1

commit v5 on v4

--- a/solution.py
+++ b/solution.py
@@ -729,13 +729,14 @@
     batch_bits = [("batch", b) for b in reversed(range(bit_count("batch")))]
     all_grads = jnp.stack(relative).reshape(-1, cols)
     chain_f = Chain(tn(all_normed, all_grads).astype(BF16), batch_bits, hops(False, False)[: len(batch_bits)])
-    by_place, lag_sums = land((by_place, lag_sums), chain_g, chain_u)
+    by_place, lag_sums = land((by_place, lag_sums), chain_g, chain_u, chain_r, chain_a, chain_b)
     while chain_g.order[0][0] == "seq":
         by_place, lag_sums = land(tick((by_place, lag_sums), chain_g, chain_u), chain_g, chain_u)
     chain_gu = joined([chain_g, chain_u], chain_g.order)
     chains = (chain_f, chain_gu, chain_r, chain_a, chain_b)
-    by_place, lag_sums = tick((by_place, lag_sums), *chains)
     dqkv = lax.all_to_all(by_place, "seq", split_axis=1, concat_axis=1, tiled=True)
+    lag_sums = tick(lag_sums, *chains)
+    dqkv, lag_sums = settle(dqkv, lag_sums)
     dqkv = jnp.concatenate(absolute(dqkv.swapaxes(0, 1), "seq"), axis=-1).reshape(rows * part, -1)
     dqkv = tick(dqkv, chain_f)
     part_zero, gain_zero = norm_back(x, inv_zero, gain_values[0], nt(dqkv, w_first))

time: 593 us -> 593 us (level)
  waiting for transfers between devices: 188 us -> 180 us
    all_to_all x1, waiting for transfers between devices: 28.3 us -> 22.2 us  [shards(): lax.all_to_all(cots, 'seq', split_axis=2, concat_axis=1, tiled=True)]
    unnamed x236 -> x250, local copies, waits for them, and re-layouts: 12.5 us -> 16.7 us
  transfers between devices with their start and end apart: 50 -> 50, of which waited for: 15 -> 15; matrix products, arithmetic and copies ran while one was open for 21% -> 23% of each run, Pallas kernels for 14% -> 14%
where the time goes in v5:
time: 593 us; the launch traced here: 585 us
  waiting for transfers between devices  180 us (30%)
  Pallas kernels  110 us (19%)
  other arithmetic  87.8 us (15%)
  starting transfers between devices  75.4 us (13%)
  local copies, waits for them, and re-layouts  68.6 us (12%)
  matrix products  47.2 us (8%)
  between operations  16.5 us (3%)
    ppermute x42, waiting for transfers between devices, flip(): lax.ppermute(value, axis, [(i, i ^ mask) for i in range(lax.axis_size(axi...  71.1 us
    all_gather x1, waiting for transfers between devices, shards(): lax.all_gather(jnp.concatenate(pieces, axis=1), every, axis=0, tiled=True)  48.1 us
    ppermute x42, starting transfers between devices, flip(): lax.ppermute(value, axis, [(i, i ^ mask) for i in range(lax.axis_size(axi...  48.1 us
    pallas_call x1, Pallas kernels, feed_forward(): pl.pallas_call(functools.partial(ffn_kernel, core_rows=core_rows), grid=(...  39 us
    convert_element_type x15, other arithmetic, outgoing(): sum((p.astype(F32) for p in self.half(1 - my_bit(*self.order[0]))))  35.1 us
    pallas_call x1, Pallas kernels, self_attention_back(): pl.pallas_call(self_bwd_kernel, grid=(rows,), in_specs=[all_spec, queries...  26.4 us
    all_to_all x1, waiting for transfers between devices, shards(): lax.all_to_all(head_context, 'seq', split_axis=1, concat_axis=2, tiled=True)  23.2 us
    all_to_all x1, waiting for transfers between devices, shards(): lax.all_to_all(cots, 'seq', split_axis=2, concat_axis=1, tiled=True)  22.2 us
  transfers between devices with their start and end apart: 50, of which 15 were waited for; matrix products, arithmetic and copies ran while one was open for 23% of the time, Pallas kernels for 14%

profile of v5, /device:TPU:0, one launch (start us, length us, event | category | flops | bytes accessed | tf_op | source)
XLA Modules:
  0.0 585.1 jit_solution(2324143484332021887)
XLA Ops:
  11.6 4.0 collective-permute-start.11
  25.2 4.6 gather_fusion
  33.7 16.5 %collective-permute-done.6 = bf16[4,40,512]{2,1,0:T(8,128)(2,1)S(1)} collective-permute-done((bf16[4,40,512]{2,1,0:T(8,128)(2,1)S(1)}, bf16[4,40,512]{2,1,0:T(8,128)(2,1)S(1)}, u32[]{:S(2)}, u32[]{:S(2)}) %collective-permute-start.6) | collective-permute-done | bytes 163872 | tf_op jit(solution)/shard_map/ppermute | solution.py:332
  57.1 17.7 %collective-permute-done.7 = bf16[2,4,40,512]{3,2,1,0:T(8,128)(2,1)} collective-permute-done((bf16[2,4,40,512]{3,2,1,0:T(8,128)(2,1)S(1)}, bf16[2,4,40,512]{3,2,1,0:T(8,128)(2,1)}, u32[]{:S(2)}, u32[]{:S(2)}) %collective-permute-start.7) | collective-permute-done | bytes 327712 | tf_op jit(solution)/shard_map/ppermute | solution.py:332
  75.9 17.4 %collective-permute-done.5 = bf16[256,1024]{1,0:T(8,128)(2,1)} collective-permute-done((bf16[256,1024]{1,0:T(8,128)(2,1)S(1)}, bf16[256,1024]{1,0:T(8,128)(2,1)}, u32[]{:S(2)}, u32[]{:S(2)}) %collective-permute-start.5) | collective-permute-done | bytes 524320 | tf_op jit(solution)/shard_map/ppermute | solution.py:332
  106.6 18.3 %self_attention.1 = (bf16[2,1024,256]{2,1,0:T(8,128)(2,1)S(1)}, f32[2,1024,4]{2,1,0:T(8,128)S(1)}) custom-call(bf16[2,1024,512]{2,1,0:T(8,128)(2,1)S(1)} %bitcast.465, s32[2,1,1024]{2,1,0:T(1,128)S(1)} %broadcast_in_dim_reshape.12.seg_row_ref, s32[2,1024,1]{2,1,0:T(8,128)S(1)} %broadcast_in_dim_reshape.15.seg_col_ref, ...), custom_call_target="tpu_custom_call" | custom-call | flops 805306368 | bytes 4194304 | tf_op jit(solution)/shard_map/self_attention/pallas_call | solution.py:175
  131.8 23.2 %all-to-all-done.1 = bf16[2,1024,256]{2,0,1:T(2,128)(2,1)S(1)} async-done(((bf16[2,1024,256]{2,0,1:T(2,128)(2,1)}), bf16[2,1024,256]{2,0,1:T(2,128)(2,1)S(1)}, u32[]{:S(2)}, u32[]{:S(2)}) %all-to-all-start.1) | async-done | bytes 1048608 | tf_op jit(solution)/shard_map/all_to_all | solution.py:676
  157.1 48.1 %all-gather.2.cloned.1.call-done.wg_ref.wu_ref = bf16[1024,12800]{1,0:T(8,128)(2,1)} async-done(((bf16[32,12800]{1,0:T(8,128)(2,1)}), bf16[1024,12800]{1,0:T(8,128)(2,1)}) %all-gather.2.cloned.1.call-update) | async-done | bytes 26214416 | tf_op jit(solution)/shard_map/all_gather | solution.py:649
  213.9 4.3 fusion.136
  224.9 11.2 %cross_attention.1 = bf16[2,256,1024]{2,1,0:T(8,128)(2,1)S(1)} custom-call(bf16[2,256,1024]{2,1,0:T(8,128)(2,1)S(1)} %bitcast.468, bf16[2,256,512]{2,1,0:T(8,128)(2,1)S(1)} %get-tuple-element.322.k_ref, bf16[2,256,512]{2,1,0:T(8,128)(2,1)S(1)} %get-tuple-element.321.v_ref, s32[2,1,256]{2,1,0:T(1,128)S(1)} %broadcast_in_dim_reshape.14.seg_row_ref, ...), custom_call_target="tpu_custom_call" | custom-call | flops 536870912 | bytes 3145728 | tf_op jit(solution)/shard_map/cross_attention/pallas_call | solution.py:288
  236.2 4.6 fusion.45.h_ref
  244.2 39.0 %feed_forward.1 = (bf16[512,1024]{1,0:T(8,128)(2,1)}, f32[512,1024]{1,0:T(8,128)}, f32[1,1024]{1,0:T(1,128)}, bf16[512,2816]{1,0:T(8,128)(2,1)}, bf16[512,2816]{...) custom-call(s32[1]{0:T(128)} %bitcast.core_ref, ...), custom_call_target="tpu_custom_call" | custom-call | flops 26575110144 | bytes 34603008 | tf_op jit(solution)/shard_map/feed_forward/pallas_call | solution.py:550
  290.8 4.7 convolution_convert_fusion.3
  308.2 14.7 %cross_attention_back.1 = (bf16[2,256,1024]{2,1,0:T(8,128)(2,1)S(1)}, bf16[2,256,512]{2,1,0:T(8,128)(2,1)S(1)}, bf16[2,256,512]{2,1,0:T(8,128)(2,1)S(1)}) custom-call(bf16[2,256,1024]{2,1,0:T(8,128)(2,1)S(1)} %bitcast.469, bf16[2,256,512]{2,1,0:T(8,128)(2,1)S(1)} %get-tuple-element.322.k_ref, bf16[2,256,512]{2,1,0:T(8,128)(2,1)S(1)} %get-tuple-element.321.v_ref, ...), custom_call_target="tpu_custom_call" | custom-call | flops 1342177280 | bytes 5242880 | tf_op jit(solution)/shard_map/cross_attention_back/pallas_call | solution.py:305
  322.9 4.8 multiply_reduce_fusion
  328.9 4.4 all-to-all-start.2
  336.1 4.7 fusion.48
  369.2 4.2 all-to-all-start.3
  382.2 22.2 %all-to-all-done.3 = bf16[2,256,1024]{1,0,2:T(2,128)(2,1)} async-done(((bf16[2,256,1024]{1,0,2:T(2,128)(2,1)}), bf16[2,256,1024]{1,0,2:T(2,128)(2,1)}, u32[]{:S(2)}, u32[]{:S(2)}) %all-to-all-start.3) | async-done | bytes 1048608 | tf_op jit(solution)/shard_map/all_to_all | solution.py:724
  424.8 26.4 %self_attention_back.1 = (bf16[2,1024,512]{2,1,0:T(8,128)(2,1)S(1)}, f32[4,1152]{1,0:T(4,128)S(1)}) custom-call(bf16[2,1024,512]{2,1,0:T(8,128)(2,1)} %bitcast.466, bf16[2,1024,256]{2,1,0:T(8,128)(2,1)S(1)} %bitcast.467, f32[2,1024,4]{2,1,0:T(8,128)S(1)} %copy-done.8, s32[2,1,1024]{2,1,0:T(1,128)S(1)} %broadcast_in_dim_reshape.12.seg_row_ref, ...), custom_call_target="tpu_custom_call" | custom-call | flops 2013265920 | bytes 6291456 | tf_op jit(solution)/shard_map/self_attention_back/pallas_call | solution.py:199
  464.6 4.7 all-to-all-start.4
  486.0 9.7 %all-to-all-done.4 = bf16[2,4,256,512]{3,2,0,1:T(8,128)(2,1)} async-done(((bf16[2,4,256,512]{3,2,0,1:T(8,128)(2,1)}), bf16[2,4,256,512]{3,2,0,1:T(8,128)(2,1)}, u32[]{:S(2)}, u32[]{:S(2)}) %all-to-all-start.4) | async-done | bytes 2097184 | tf_op jit(solution)/shard_map/all_to_all | solution.py:737
  539.8 4.2 all-to-all-start.5
  561.6 11.1 %collective-permute-done.39 = bf16[32,4096]{1,0:T(8,128)(2,1)S(1)} collective-permute-done((bf16[32,4096]{1,0:T(8,128)(2,1)S(1)}, bf16[32,4096]{1,0:T(8,128)(2,1)S(1)}, u32[]{:S(2)}, u32[]{:S(2)}) %collective-permute-start.39) | collective-permute-done | bytes 262176 | tf_op jit(solution)/shard_map/ppermute | solution.py:332
  (523 shorter events, 243.9 us)
Async XLA Ops:
  7.2 198.0 %all-gather.2.cloned.1.call-start = ((), (), s32[]{:S(2)}) async-start(), calls=%async_computation.7 | async-start | bytes 27033600 | tf_op jit(solution)/shard_map/all_gather | solution.py:649
  11.6 39.9 %collective-permute-start.11 = (s32[2,320]{1,0:T(2,128)S(1)}, s32[2,320]{1,0:T(2,128)S(1)}, u32[]{:S(2)}, u32[]{:S(2)}) collective-permute-start(s32[2,320]{1,0:T(2,128)S(1)} %constant_dynamic-update-slice_fusion), channel_id=1, source_target_pairs={{0,3},{1,2},{2,1},{3,0},{4,7},{5,6},{6,5},{7,4},{8,11},{9,10},{10,... | collective-permute-start | bytes 7688 | tf_op jit(solution)/shard_map/ppermute | solution.py:332
  15.5 36.9 %collective-permute-start.10 = (s32[2,320]{1,0:T(2,128)S(1)}, s32[2,320]{1,0:T(2,128)S(1)}, u32[]{:S(2)}, u32[]{:S(2)}) collective-permute-start(s32[2,320]{1,0:T(2,128)S(1)} %constant_dynamic-update-slice_fusion), channel_id=1, source_target_pairs={{0,2},{1,3},{2,0},{3,1},{4,6},{5,7},{6,4},{7,5},{8,10},{9,11},{10,... | collective-permute-start | bytes 7688 | tf_op jit(solution)/shard_map/ppermute | solution.py:332
  21.7 32.2 %collective-permute-start.4 = (bf16[256,1024]{1,0:T(8,128)(2,1)S(1)}, bf16[256,1024]{1,0:T(8,128)(2,1)S(1)}, u32[]{:S(2)}, u32[]{:S(2)}) collective-permute-start(bf16[256,1024]{1,0:T(8,128)(2,1)S(1)} %get-tuple-element.328), channel_id=1, source_target_pairs={{0,2},{1,3},{2,0},{3,1},{4,6},{5,7},{6,4},{7,5},{8,10},{9,11},{10,... | collective-permute-start | bytes 1572872 | tf_op jit(solution)/shard_map/ppermute | solution.py:332
  23.7 31.4 %collective-permute-start = (bf16[256,1024]{1,0:T(8,128)(2,1)}, bf16[256,1024]{1,0:T(8,128)(2,1)}, u32[]{:S(2)}, u32[]{:S(2)}) collective-permute-start(bf16[256,1024]{1,0:T(8,128)(2,1)} %get-tuple-element.329), channel_id=1, source_target_pairs={{0,1},{1,0},{2,3},{3,2},{4,5},{5,4},{6,7},{7,6},{8,9},{9,8},{10,11... | collective-permute-start | bytes 1572872 | tf_op jit(solution)/shard_map/ppermute | solution.py:332
  52.4 42.8 %collective-permute-start.1 = (bf16[256,1024]{1,0:T(8,128)(2,1)}, bf16[256,1024]{1,0:T(8,128)(2,1)}, u32[]{:S(2)}, u32[]{:S(2)}) collective-permute-start(bf16[256,1024]{1,0:T(8,128)(2,1)} %get-tuple-element.329), channel_id=1, source_target_pairs={{0,2},{1,3},{2,0},{3,1},{4,6},{5,7},{6,4},{7,5},{8,10},{9,11},{10,... | collective-permute-start | bytes 1572872 | tf_op jit(solution)/shard_map/ppermute | solution.py:332
  53.9 39.5 %collective-permute-start.5 = (bf16[256,1024]{1,0:T(8,128)(2,1)S(1)}, bf16[256,1024]{1,0:T(8,128)(2,1)}, u32[]{:S(2)}, u32[]{:S(2)}) collective-permute-start(bf16[256,1024]{1,0:T(8,128)(2,1)S(1)} %collective-permute-done.4), channel_id=1, source_target_pairs={{0,1},{1,0},{2,3},{3,2},{4,5},{5,4},{6,7},{7,6},{8,9},{9,8},{10,11... | collective-permute-start | bytes 1572872 | tf_op jit(solution)/shard_map/ppermute | solution.py:332
  55.1 40.1 %collective-permute-start.2 = (bf16[256,1024]{1,0:T(8,128)(2,1)}, bf16[256,1024]{1,0:T(8,128)(2,1)}, u32[]{:S(2)}, u32[]{:S(2)}) collective-permute-start(bf16[256,1024]{1,0:T(8,128)(2,1)} %collective-permute-done), channel_id=1, source_target_pairs={{0,2},{1,3},{2,0},{3,1},{4,6},{5,7},{6,4},{7,5},{8,10},{9,11},{10,... | collective-permute-start | bytes 1572872 | tf_op jit(solution)/shard_map/ppermute | solution.py:332
  240.7 46.8 %collective-permute-start.17 = (bf16[1024,512]{1,0:T(8,128)(2,1)S(1)}, bf16[1024,512]{1,0:T(8,128)(2,1)S(1)}, u32[]{:S(2)}, u32[]{:S(2)}) collective-permute-start(bf16[1024,512]{1,0:T(8,128)(2,1)S(1)} %bitcast.520), channel_id=1, source_target_pairs={{0,3},{1,2},{2,1},{3,0},{4,7},{5,6},{6,5},{7,4},{8,11},{9,10},{10,... | collective-permute-start | bytes 3145736 | tf_op jit(solution)/shard_map/ppermute | solution.py:332
  241.9 46.7 %collective-permute-start.16 = (bf16[1024,512]{1,0:T(8,128)(2,1)S(1)}, bf16[1024,512]{1,0:T(8,128)(2,1)S(1)}, u32[]{:S(2)}, u32[]{:S(2)}) collective-permute-start(bf16[1024,512]{1,0:T(8,128)(2,1)S(1)} %bitcast.521), channel_id=1, source_target_pairs={{0,2},{1,3},{2,0},{3,1},{4,6},{5,7},{6,4},{7,5},{8,10},{9,11},{10,... | collective-permute-start | bytes 3145736 | tf_op jit(solution)/shard_map/ppermute | solution.py:332
  242.9 45.7 %collective-permute-start.15 = (bf16[1024,512]{1,0:T(8,128)(2,1)S(1)}, bf16[1024,512]{1,0:T(8,128)(2,1)S(1)}, u32[]{:S(2)}, u32[]{:S(2)}) collective-permute-start(bf16[1024,512]{1,0:T(8,128)(2,1)S(1)} %bitcast.522), channel_id=1, source_target_pairs={{0,1},{1,0},{2,3},{3,2},{4,5},{5,4},{6,7},{7,6},{8,9},{9,8},{10,11... | collective-permute-start | bytes 3145736 | tf_op jit(solution)/shard_map/ppermute | solution.py:332
  354.0 52.4 %collective-permute-start.24 = (bf16[2,2,2,2,32,2048]{5,4,3,2,1,0:T(8,128)(2,1)}, bf16[2,2,2,2,32,2048]{5,4,3,2,1,0:T(8,128)(2,1)}, u32[]{:S(2)}, u32[]{:S(2)}) collective-permute-start(bf16[2,2,2,2,32,2048]{5,4,3,2,1,0:T(8,128)(2,1)} %fusion.6), channel_id=1, source_target_pairs={{0,4},{4,0},{8,12},{12,8},{16,20},{20,16},{24,28},{28,24},{1,5},{5... | collective-permute-start | bytes 6291464 | tf_op jit(solution)/shard_map/ppermute | solution.py:332
  354.0 52.4 %collective-permute-start.25 = (bf16[2,2,2,2,32,2048]{5,4,1,0,3,2:T(8,128)(2,1)}, bf16[2,2,2,2,32,2048]{5,4,1,0,3,2:T(8,128)(2,1)}, u32[]{:S(2)}, u32[]{:S(2)}) collective-permute-start(bf16[2,2,2,2,32,2048]{5,4,1,0,3,2:T(8,128)(2,1)} %copy_bitcast_fusion), channel_id=1, source_target_pairs={{0,4},{4,0},{8,12},{12,8},{16,20},{20,16},{24,28},{28,24},{1,5},{5... | collective-permute-start | bytes 6291464 | tf_op jit(solution)/shard_map/ppermute | solution.py:332
  356.0 50.3 %collective-permute-start.21 = (bf16[2,2,2,88,1024]{4,3,2,1,0:T(8,128)(2,1)}, bf16[2,2,2,88,1024]{4,3,2,1,0:T(8,128)(2,1)}, u32[]{:S(2)}, u32[]{:S(2)}) collective-permute-start(bf16[2,2,2,88,1024]{4,3,2,1,0:T(8,128)(2,1)} %fusion.3), channel_id=1, source_target_pairs={{0,8},{4,12},{8,0},{12,4},{16,24},{20,28},{24,16},{28,20},{1,9},{5... | collective-permute-start | bytes 4325384 | tf_op jit(solution)/shard_map/ppermute | solution.py:332
  358.5 47.9 %collective-permute-start.22 = (bf16[2,2,2,32,2816]{4,3,1,0,2:T(8,128)(2,1)}, bf16[2,2,2,32,2816]{4,3,1,0,2:T(8,128)(2,1)}, u32[]{:S(2)}, u32[]{:S(2)}) collective-permute-start(bf16[2,2,2,32,2816]{4,3,1,0,2:T(8,128)(2,1)} %fusion.57), channel_id=1, source_target_pairs={{0,1},{1,0},{2,3},{3,2},{4,5},{5,4},{6,7},{7,6},{8,9},{9,8},{10,11... | collective-permute-start | bytes 4325384 | tf_op jit(solution)/shard_map/ppermute | solution.py:332
  359.9 46.4 %collective-permute-start.23 = (bf16[2,2,2,32,2816]{4,3,1,0,2:T(8,128)(2,1)}, bf16[2,2,2,32,2816]{4,3,1,0,2:T(8,128)(2,1)}, u32[]{:S(2)}, u32[]{:S(2)}) collective-permute-start(bf16[2,2,2,32,2816]{4,3,1,0,2:T(8,128)(2,1)} %fusion.58), channel_id=1, source_target_pairs={{0,2},{1,3},{2,0},{3,1},{4,6},{5,7},{6,4},{7,5},{8,10},{9,11},{10,... | collective-permute-start | bytes 4325384 | tf_op jit(solution)/shard_map/ppermute | solution.py:332
  369.2 35.2 %all-to-all-start.3 = ((bf16[2,256,1024]{1,0,2:T(2,128)(2,1)}), bf16[2,256,1024]{1,0,2:T(2,128)(2,1)}, u32[]{:S(2)}, u32[]{:S(2)}) async-start(bf16[2,256,1024]{1,0,2:T(2,128)(2,1)} %copy.179), calls=%async_computation.3 | async-start | bytes 2097152 | tf_op jit(solution)/shard_map/all_to_all | solution.py:724
  418.4 42.7 %collective-permute-start.26 = (bf16[2,2,32,2816]{3,2,1,0:T(8,128)(2,1)}, bf16[2,2,32,2816]{3,2,1,0:T(8,128)(2,1)S(1)}, u32[]{:S(2)}, u32[]{:S(2)}) collective-permute-start(bf16[2,2,32,2816]{3,2,1,0:T(8,128)(2,1)} %fusion.60), channel_id=1, source_target_pairs={{0,2},{1,3},{2,0},{3,1},{4,6},{5,7},{6,4},{7,5},{8,10},{9,11},{10,... | collective-permute-start | bytes 2162696 | tf_op jit(solution)/shard_map/ppermute | solution.py:332
  419.8 41.3 %collective-permute-start.27 = (bf16[2,2,32,2816]{3,2,1,0:T(8,128)(2,1)}, bf16[2,2,32,2816]{3,2,1,0:T(8,128)(2,1)S(1)}, u32[]{:S(2)}, u32[]{:S(2)}) collective-permute-start(bf16[2,2,32,2816]{3,2,1,0:T(8,128)(2,1)} %fusion.59), channel_id=1, source_target_pairs={{0,1},{1,0},{2,3},{3,2},{4,5},{5,4},{6,7},{7,6},{8,9},{9,8},{10,11... | collective-permute-start | bytes 2162696 | tf_op jit(solution)/shard_map/ppermute | solution.py:332
  420.5 40.6 %collective-permute-start.28 = (bf16[2,2,88,1024]{3,2,1,0:T(8,128)(2,1)}, bf16[2,2,88,1024]{3,2,1,0:T(8,128)(2,1)S(1)}, u32[]{:S(2)}, u32[]{:S(2)}) collective-permute-start(bf16[2,2,88,1024]{3,2,1,0:T(8,128)(2,1)} %fusion.61), channel_id=1, source_target_pairs={{0,16},{4,20},{8,24},{12,28},{16,0},{20,4},{24,8},{28,12},{1,17},{... | collective-permute-start | bytes 2162696 | tf_op jit(solution)/shard_map/ppermute | solution.py:332
  422.8 38.4 %collective-permute-start.29 = (bf16[2,2,2,32,2048]{4,3,1,0,2:T(8,128)(2,1)S(1)}, bf16[2,2,2,32,2048]{4,3,1,0,2:T(8,128)(2,1)S(1)}, u32[]{:S(2)}, u32[]{:S(2)}) collective-permute-start(bf16[2,2,2,32,2048]{4,3,1,0,2:T(8,128)(2,1)S(1)} %fusion.16), channel_id=1, source_target_pairs={{0,1},{1,0},{2,3},{3,2},{4,5},{5,4},{6,7},{7,6},{8,9},{9,8},{10,11... | collective-permute-start | bytes 3145736 | tf_op jit(solution)/shard_map/ppermute | solution.py:332
  424.1 37.0 %collective-permute-start.30 = (bf16[2,2,2,32,2048]{4,3,1,0,2:T(8,128)(2,1)S(1)}, bf16[2,2,2,32,2048]{4,3,1,0,2:T(8,128)(2,1)S(1)}, u32[]{:S(2)}, u32[]{:S(2)}) collective-permute-start(bf16[2,2,2,32,2048]{4,3,1,0,2:T(8,128)(2,1)S(1)} %fusion.15), channel_id=1, source_target_pairs={{0,2},{1,3},{2,0},{3,1},{4,6},{5,7},{6,4},{7,5},{8,10},{9,11},{10,... | collective-permute-start | bytes 3145736 | tf_op jit(solution)/shard_map/ppermute | solution.py:332
  482.2 41.3 %collective-permute-start.35 = (bf16[2,32,5632]{2,1,0:T(8,128)(2,1)}, bf16[2,32,5632]{2,1,0:T(8,128)(2,1)}, u32[]{:S(2)}, u32[]{:S(2)}) collective-permute-start(bf16[2,32,5632]{2,1,0:T(8,128)(2,1)} %fusion.69), channel_id=1, source_target_pairs={{0,8},{4,12},{8,0},{12,4},{16,24},{20,28},{24,16},{28,20},{1,9},{5... | collective-permute-start | bytes 2162696 | tf_op jit(solution)/shard_map/ppermute | solution.py:332
  483.8 39.7 %collective-permute-start.36 = (bf16[2,88,1024]{2,1,0:T(8,128)(2,1)}, bf16[2,88,1024]{2,1,0:T(8,128)(2,1)}, u32[]{:S(2)}, u32[]{:S(2)}) collective-permute-start(bf16[2,88,1024]{2,1,0:T(8,128)(2,1)} %fusion.75), channel_id=1, source_target_pairs={{0,1},{1,0},{2,3},{3,2},{4,5},{5,4},{6,7},{7,6},{8,9},{9,8},{10,11... | collective-permute-start | bytes 1081352 | tf_op jit(solution)/shard_map/ppermute | solution.py:332
  (143 other events, 1214.5 us)
Sparse Core Ops, SparseCore 0:
  11.6 193.5 all-gather.1
